TPU v7x, 32 devices: a whole 2x2x4 slice. The times are simulated.
32 devices in a mesh: rep: 4 (over y, x), shard: 8 (over z, core).
Axes of the slice: x: 2, y: 2, z: 4, core: 2. Of those that a mesh axis runs over, the one named last changes fastest.
Arguments:
- block_in: bfloat16 [16384, 768], P(('rep', 'shard')), may hold values from -6 to 6
- earlier: bfloat16 [4, 16384, 768], P(None, ('rep', 'shard')), may hold values from -6 to 6
- cotangent: float32 [16384, 768], P(('rep', 'shard')), may hold values from -6 to 6
- qkv_weight: float32 [768, 2304], P('shard'), may hold values from -0.21875 to 0.21875
- out_weight: float32 [768, 768], P('shard'), may hold values from -6 to 6
- in_weight: float32 [768, 3072], P('shard'), may hold values from -0.21875 to 0.21875
- down_weight: float32 [3072, 768], P('shard'), may hold values from -0.109375 to 0.109375
- qk_bias: float32 [1536], P('shard'), may hold values from -3 to 3
- value_bias: float32 [768], P('shard'), may hold values from -3 to 3
- out_bias: float32 [768], P('shard'), may hold values from -3 to 3
- in_bias: float32 [3072], P('shard'), may hold values from -3 to 3
- down_bias: float32 [768], P('shard'), may hold values from -3 to 3
- gain_one: float32 [768], P('shard'), may hold values from 0.5 to 1.5
- shift_one: float32 [768], P('shard'), may hold values from -3 to 3
- gain_two: float32 [768], P('shard'), may hold values from 0.5 to 1.5
- shift_two: float32 [768], P('shard'), may hold values from -3 to 3
- depth_weights: float32 [5], replicated, may hold values from 0.3 to 1.2
Outputs:
- layer_out: float32 [16384, 768], P(('rep', 'shard'))
- grad_block_in: float32 [16384, 768], P(('rep', 'shard'))
- grad_earlier: float32 [4, 16384, 768], P(None, ('rep', 'shard'))
- grad_qkv_weight: float32 [768, 2304], P('shard')
- grad_out_weight: float32 [768, 768], P('shard')
- grad_in_weight: float32 [768, 3072], P('shard')
- grad_down_weight: float32 [3072, 768], P('shard')
- grad_qk_bias: float32 [1536], P('shard')
- grad_value_bias: float32 [768], P('shard')
- grad_out_bias: float32 [768], P('shard')
- grad_in_bias: float32 [3072], P('shard')
- grad_down_bias: float32 [768], P('shard')
- grad_gain_one: float32 [768], P('shard')
- grad_shift_one: float32 [768], P('shard')
- grad_gain_two: float32 [768], P('shard')
- grad_shift_two: float32 [768], P('shard')
- grad_depth: float32 [5], replicated
All inputs are finite; a program needn't handle non-finite values.
Results may differ from a plain program's by a relative error of at most 0.035.
Values may be sent and summed in bfloat16 or wider, within the bound.
No kernel may reach another device: no remote copies, remote signals or barrier semaphores. Data moves between devices by JAX's collectives and lax.ppermute only.
A program may use at most 192 MiB of HBM per device.

v0:
```python
from functools import partial
import math

import jax
import jax.numpy as jnp
from jax import lax
from jax.experimental import pallas as pl
from jax.experimental.pallas import tpu as pltpu
from jax.sharding import PartitionSpec as P

HEAD_DIM = 64
BLOCK = 256


NEG = -1e30
EPSILON = 1e-05


def layer_norm(inputs, gain, shift):
    center = inputs - jnp.mean(inputs, axis=-1, keepdims=True)
    spread = jnp.mean(center * center, axis=-1, keepdims=True)
    return center * lax.rsqrt(spread + EPSILON) * gain + shift


def rotate(inputs, positions):
    row_count = inputs.shape[0]
    split = inputs.reshape(row_count, -1, HEAD_DIM)
    half_dim = HEAD_DIM // 2
    freqs = 10000.0 ** (-jnp.arange(half_dim, dtype=jnp.float32) / half_dim)
    angles = positions.astype(jnp.float32)[:, None] * freqs[None, :]
    cosine = jnp.cos(angles)[:, None, :]
    sine = jnp.sin(angles)[:, None, :]
    former = split[..., :half_dim]
    latter = split[..., half_dim:]
    turned = jnp.concatenate(
        [former * cosine - latter * sine, former * sine + latter * cosine], axis=-1
    )
    return turned.reshape(row_count, -1)


def generic_device(
    block_in,
    earlier,
    cotangent,
    qkv_weight,
    out_weight,
    in_weight,
    down_weight,
    qk_bias,
    value_bias,
    out_bias,
    in_bias,
    down_bias,
    gain_one,
    shift_one,
    gain_two,
    shift_two,
    depth_weights,
):
    bf16 = jnp.bfloat16
    f32 = jnp.float32
    w_qkv, w_out, w_in, w_down, b_qk, b_value, b_out, b_in, b_down, g_one, s_one, g_two, s_two = (
        lax.all_gather(qkv_weight.astype(bf16), "shard", axis=0, tiled=True),
        lax.all_gather(out_weight.astype(bf16), "shard", axis=0, tiled=True),
        lax.all_gather(in_weight.astype(bf16), "shard", axis=0, tiled=True),
        lax.all_gather(down_weight.astype(bf16), "shard", axis=0, tiled=True),
        lax.all_gather(qk_bias.astype(bf16), "shard", axis=0, tiled=True),
        lax.all_gather(value_bias.astype(bf16), "shard", axis=0, tiled=True),
        lax.all_gather(out_bias.astype(bf16), "shard", axis=0, tiled=True),
        lax.all_gather(in_bias.astype(bf16), "shard", axis=0, tiled=True),
        lax.all_gather(down_bias.astype(bf16), "shard", axis=0, tiled=True),
        lax.all_gather(gain_one.astype(bf16), "shard", axis=0, tiled=True),
        lax.all_gather(shift_one.astype(bf16), "shard", axis=0, tiled=True),
        lax.all_gather(gain_two.astype(bf16), "shard", axis=0, tiled=True),
        lax.all_gather(shift_two.astype(bf16), "shard", axis=0, tiled=True),
    )
    row_count, model_width = block_in.shape
    head_count = model_width // HEAD_DIM
    groups = lax.axis_size("shard")
    length = row_count * groups
    window = min(512, length)
    member = lax.axis_index("shard")
    first_row = member * row_count
    last_end = first_row + row_count
    positions = first_row + jnp.arange(row_count, dtype=jnp.int32)
    query_block = positions // BLOCK
    score_scale = HEAD_DIM ** (-0.5)
    needed = (last_end + window - 1) // window
    inputs = block_in.astype(f32)
    normed, norm_back = jax.vjp(layer_norm, inputs, g_one.astype(f32), s_one.astype(f32))
    normed_low = normed.astype(bf16)
    joint_bias = jnp.concatenate([b_qk.astype(f32), b_value.astype(f32)])
    projected = jnp.dot(normed_low, w_qkv, preferred_element_type=f32) + joint_bias
    queries = rotate(projected[:, :model_width], positions).astype(bf16)
    key_rows = rotate(projected[:, model_width : 2 * model_width], positions).astype(bf16)
    values = projected[:, 2 * model_width :].astype(bf16)
    query_heads = queries.reshape(row_count, head_count, HEAD_DIM)

    def masked_scores(key_piece, key_start):
        piece_rows = key_piece.shape[0]
        key_heads = key_piece.reshape(piece_rows, head_count, HEAD_DIM)
        scores = (
            jnp.einsum("qhd,khd->hqk", query_heads, key_heads, preferred_element_type=f32)
            * score_scale
        )
        key_block = (key_start + jnp.arange(piece_rows, dtype=jnp.int32)) // BLOCK
        allowed = key_block[None, :] <= query_block[:, None]
        return (scores, allowed)

    def absorb(running, key_piece, value_piece, key_start):
        highest, denominator, summed = running
        scores, allowed = masked_scores(key_piece, key_start)
        scores = jnp.where(allowed[None], scores, NEG)
        new_high = jnp.maximum(highest, jnp.max(scores, axis=-1))
        rescale = jnp.exp(highest - new_high)
        weights = jnp.where(allowed[None], jnp.exp(scores - new_high[..., None]), 0.0)
        value_heads = value_piece.reshape(-1, head_count, HEAD_DIM)
        summed = summed * rescale[..., None] + jnp.einsum(
            "hqk,khd->hqd", weights.astype(bf16), value_heads, preferred_element_type=f32
        )
        return (new_high, denominator * rescale + jnp.sum(weights, axis=-1), summed)

    start_state = (
        jnp.full((head_count, row_count), NEG, f32),
        jnp.zeros((head_count, row_count), f32),
        jnp.zeros((head_count, row_count, HEAD_DIM), f32),
    )
    key_piece = lax.all_gather(key_rows, "shard", axis=0, tiled=True)
    value_piece = lax.all_gather(values, "shard", axis=0, tiled=True)
    piece_rows = key_piece.shape[0]
    sub_rows = math.gcd(piece_rows, window)
    usable = jnp.clip((last_end + sub_rows - 1) // sub_rows, 0, piece_rows // sub_rows)

    def advance(block_step, state_inner):
        offset = block_step * sub_rows
        return absorb(
            state_inner,
            lax.dynamic_slice_in_dim(key_piece, offset, sub_rows, 0),
            lax.dynamic_slice_in_dim(value_piece, offset, sub_rows, 0),
            offset,
        )

    highest, denominator, summed = lax.fori_loop(0, usable, advance, start_state)
    attended = summed / denominator[..., None]
    log_norm = highest + jnp.log(denominator)
    mixed = jnp.transpose(attended, (1, 0, 2)).reshape(row_count, model_width).astype(bf16)
    branch = jnp.dot(mixed, w_out, preferred_element_type=f32) + b_out.astype(f32)
    middle = inputs + branch
    normed_two, norm_two_back = jax.vjp(layer_norm, middle, g_two.astype(f32), s_two.astype(f32))
    normed_two_low = normed_two.astype(bf16)
    hidden = jnp.dot(normed_two_low, w_in, preferred_element_type=f32) + b_in.astype(f32)
    active_full, gelu_back = jax.vjp(partial(jax.nn.gelu, approximate=True), hidden)
    active = active_full.astype(bf16)
    result = middle + jnp.dot(active, w_down, preferred_element_type=f32) + b_down.astype(f32)
    stacked = earlier.astype(f32)
    layer_out = depth_weights[4] * result
    for level in range(4):
        layer_out = layer_out + depth_weights[level] * stacked[level]
    grad_earlier = depth_weights[:4][:, None, None] * cotangent[None]
    local_depth = jnp.concatenate(
        [jnp.sum(stacked * cotangent[None], axis=(1, 2)), jnp.sum(result * cotangent)[None]]
    )
    grad_depth = lax.psum(local_depth, ("rep", "shard"))
    grad_result = depth_weights[4] * cotangent
    down_grad = grad_result.astype(bf16)
    grad_down_w = jnp.einsum("tf,td->fd", active, down_grad, preferred_element_type=f32)
    grad_down_b = jnp.sum(down_grad.astype(f32), axis=0)
    grad_active = jnp.einsum("td,fd->tf", down_grad, w_down, preferred_element_type=f32)
    grad_hidden = gelu_back(grad_active)[0].astype(bf16)
    grad_in_w = jnp.einsum("td,tf->df", normed_two_low, grad_hidden, preferred_element_type=f32)
    grad_in_b = jnp.sum(grad_hidden.astype(f32), axis=0)
    grad_normed_two = jnp.einsum("tf,df->td", grad_hidden, w_in, preferred_element_type=f32)
    grad_mid_norm, grad_gain_two, grad_shift_two = norm_two_back(grad_normed_two)
    grad_middle = grad_result + grad_mid_norm
    branch_grad = grad_middle.astype(bf16)
    grad_out_w = jnp.einsum("td,te->de", mixed, branch_grad, preferred_element_type=f32)
    grad_out_b = jnp.sum(branch_grad.astype(f32), axis=0)
    grad_mixed = jnp.einsum("te,de->td", branch_grad, w_out, preferred_element_type=f32).astype(
        bf16
    )
    key_all, value_all = (
        lax.all_gather(key_rows, "shard", axis=0, tiled=True),
        lax.all_gather(values, "shard", axis=0, tiled=True),
    )
    grad_heads = grad_mixed.reshape(row_count, head_count, HEAD_DIM)
    delta = jnp.einsum("qhd,hqd->hq", grad_heads.astype(f32), attended)

    def score_grads(key_piece, value_piece, offset, piece_rows):
        scores, allowed = masked_scores(key_piece, offset)
        probs = jnp.where(allowed[None], jnp.exp(scores - log_norm[..., None]), 0.0)
        value_heads = value_piece.reshape(piece_rows, head_count, HEAD_DIM)
        grad_probs = jnp.einsum("qhd,khd->hqk", grad_heads, value_heads, preferred_element_type=f32)
        grad_scores = (probs * (grad_probs - delta[..., None])).astype(bf16)
        return (probs, grad_scores)

    def retrace(block_step, running):
        grad_query, grad_keys, grad_values = running
        offset = block_step * window
        key_piece = lax.dynamic_slice_in_dim(key_all, offset, window, 0)
        value_piece = lax.dynamic_slice_in_dim(value_all, offset, window, 0)
        probs, grad_scores = score_grads(key_piece, value_piece, offset, window)
        key_heads = key_piece.reshape(window, head_count, HEAD_DIM)
        grad_query = grad_query + jnp.einsum(
            "hqk,khd->qhd", grad_scores, key_heads, preferred_element_type=f32
        )
        piece_keys = (
            jnp.einsum("hqk,qhd->khd", grad_scores, query_heads, preferred_element_type=f32)
            * score_scale
        )
        piece_values = jnp.einsum(
            "hqk,qhd->khd", probs.astype(bf16), grad_heads, preferred_element_type=f32
        )
        grad_keys = lax.dynamic_update_slice_in_dim(
            grad_keys, piece_keys.reshape(window, model_width), offset, 0
        )
        grad_values = lax.dynamic_update_slice_in_dim(
            grad_values, piece_values.reshape(window, model_width), offset, 0
        )
        return (grad_query, grad_keys, grad_values)

    start_back = (
        jnp.zeros((row_count, head_count, HEAD_DIM), f32),
        jnp.zeros((length, model_width), f32),
        jnp.zeros((length, model_width), f32),
    )
    grad_query, grad_keys, grad_values = lax.fori_loop(0, needed, retrace, start_back)
    own_keys, own_values = (
        lax.psum_scatter(
            grad_keys.astype(jnp.bfloat16), "shard", scatter_dimension=0, tiled=True
        ).astype(jnp.float32),
        lax.psum_scatter(
            grad_values.astype(jnp.bfloat16), "shard", scatter_dimension=0, tiled=True
        ).astype(jnp.float32),
    )
    grad_q_turned = rotate(grad_query.reshape(row_count, model_width) * score_scale, -positions)
    grad_k_turned = rotate(own_keys, -positions)
    grad_joint = jnp.concatenate([grad_q_turned, grad_k_turned, own_values], axis=1).astype(bf16)
    grad_qkv_w = jnp.einsum("td,tf->df", normed_low, grad_joint, preferred_element_type=f32)
    joint_sums = jnp.sum(grad_joint.astype(f32), axis=0)
    grad_qk_b = joint_sums[: 2 * model_width]
    grad_value_b = joint_sums[2 * model_width :]
    grad_normed = jnp.einsum("tf,df->td", grad_joint, w_qkv, preferred_element_type=f32)
    grad_in_norm, grad_gain_one, grad_shift_one = norm_back(grad_normed)
    grad_block = grad_middle + grad_in_norm
    (
        own_qkv_w,
        own_out_w,
        own_in_w,
        own_down_w,
        own_qk_b,
        own_value_b,
        own_out_b,
        own_in_b,
        own_down_b,
        own_gain_one,
        own_shift_one,
        own_gain_two,
        own_shift_two,
    ) = (
        lax.psum_scatter(
            grad_qkv_w.astype(jnp.bfloat16), "shard", scatter_dimension=0, tiled=True
        ).astype(jnp.float32),
        lax.psum_scatter(
            grad_out_w.astype(jnp.bfloat16), "shard", scatter_dimension=0, tiled=True
        ).astype(jnp.float32),
        lax.psum_scatter(
            grad_in_w.astype(jnp.bfloat16), "shard", scatter_dimension=0, tiled=True
        ).astype(jnp.float32),
        lax.psum_scatter(
            grad_down_w.astype(jnp.bfloat16), "shard", scatter_dimension=0, tiled=True
        ).astype(jnp.float32),
        lax.psum_scatter(
            grad_qk_b.astype(jnp.bfloat16), "shard", scatter_dimension=0, tiled=True
        ).astype(jnp.float32),
        lax.psum_scatter(
            grad_value_b.astype(jnp.bfloat16), "shard", scatter_dimension=0, tiled=True
        ).astype(jnp.float32),
        lax.psum_scatter(
            grad_out_b.astype(jnp.bfloat16), "shard", scatter_dimension=0, tiled=True
        ).astype(jnp.float32),
        lax.psum_scatter(
            grad_in_b.astype(jnp.bfloat16), "shard", scatter_dimension=0, tiled=True
        ).astype(jnp.float32),
        lax.psum_scatter(
            grad_down_b.astype(jnp.bfloat16), "shard", scatter_dimension=0, tiled=True
        ).astype(jnp.float32),
        lax.psum_scatter(
            grad_gain_one.astype(jnp.bfloat16), "shard", scatter_dimension=0, tiled=True
        ).astype(jnp.float32),
        lax.psum_scatter(
            grad_shift_one.astype(jnp.bfloat16), "shard", scatter_dimension=0, tiled=True
        ).astype(jnp.float32),
        lax.psum_scatter(
            grad_gain_two.astype(jnp.bfloat16), "shard", scatter_dimension=0, tiled=True
        ).astype(jnp.float32),
        lax.psum_scatter(
            grad_shift_two.astype(jnp.bfloat16), "shard", scatter_dimension=0, tiled=True
        ).astype(jnp.float32),
    )
    (
        sum_qkv_w,
        sum_out_w,
        sum_in_w,
        sum_down_w,
        sum_qk_b,
        sum_value_b,
        sum_out_b,
        sum_in_b,
        sum_down_b,
        sum_gain_one,
        sum_shift_one,
        sum_gain_two,
        sum_shift_two,
    ) = (
        lax.psum(own_qkv_w.astype(jnp.bfloat16), "rep").astype(jnp.float32),
        lax.psum(own_out_w.astype(jnp.bfloat16), "rep").astype(jnp.float32),
        lax.psum(own_in_w.astype(jnp.bfloat16), "rep").astype(jnp.float32),
        lax.psum(own_down_w.astype(jnp.bfloat16), "rep").astype(jnp.float32),
        lax.psum(own_qk_b.astype(jnp.bfloat16), "rep").astype(jnp.float32),
        lax.psum(own_value_b.astype(jnp.bfloat16), "rep").astype(jnp.float32),
        lax.psum(own_out_b.astype(jnp.bfloat16), "rep").astype(jnp.float32),
        lax.psum(own_in_b.astype(jnp.bfloat16), "rep").astype(jnp.float32),
        lax.psum(own_down_b.astype(jnp.bfloat16), "rep").astype(jnp.float32),
        lax.psum(own_gain_one.astype(jnp.bfloat16), "rep").astype(jnp.float32),
        lax.psum(own_shift_one.astype(jnp.bfloat16), "rep").astype(jnp.float32),
        lax.psum(own_gain_two.astype(jnp.bfloat16), "rep").astype(jnp.float32),
        lax.psum(own_shift_two.astype(jnp.bfloat16), "rep").astype(jnp.float32),
    )
    return (
        layer_out,
        grad_block,
        grad_earlier,
        sum_qkv_w,
        sum_out_w,
        sum_in_w,
        sum_down_w,
        sum_qk_b,
        sum_value_b,
        sum_out_b,
        sum_in_b,
        sum_down_b,
        sum_gain_one,
        sum_shift_one,
        sum_gain_two,
        sum_shift_two,
        grad_depth,
    )


F32 = jnp.float32
BF16 = jnp.bfloat16
CHUNK = 2 * BLOCK
VMEM_LIMIT = 56 * 1024 * 1024


def cost(flops, moved, exps=0):
    return pl.CostEstimate(flops=flops, bytes_accessed=moved, transcendentals=exps)


def contract(left, right, left_dim, right_dim):
    return lax.dot_general(
        left, right, (((left_dim,), (right_dim,)), ((), ())), preferred_element_type=F32
    )


def qkv_kernel(
    x_ref, weight_ref, bias_ref, gain_ref, shift_ref, cos_ref, sin_ref,
    plain_ref, qt_ref, kt_ref, vt_ref, kv_ref,
):
    x = x_ref[...].astype(F32)
    center = x - jnp.mean(x, axis=-1, keepdims=True)
    spread = jnp.mean(center * center, axis=-1, keepdims=True)
    plain = center * lax.rsqrt(spread + EPSILON)
    plain_ref[...] = plain.astype(BF16)
    low = (plain * gain_ref[...] + shift_ref[...]).astype(BF16)
    width = qt_ref.shape[0]
    half = HEAD_DIM // 2
    joint = contract(weight_ref[...], low, 1, 1) + bias_ref[...]
    cosine = cos_ref[...]
    sine = sin_ref[...]
    for head in range(width // HEAD_DIM):
        base = head * HEAD_DIM
        for part in range(2):
            start = part * width + base
            former = joint[start : start + half]
            latter = joint[start + half : start + HEAD_DIM]
            turned = jnp.concatenate(
                [former * cosine - latter * sine, former * sine + latter * cosine], axis=0
            )
            if part == 0:
                qt_ref[base : base + HEAD_DIM, :] = (turned * HEAD_DIM ** (-0.5)).astype(BF16)
            else:
                kt_ref[base : base + HEAD_DIM, :] = turned.astype(BF16)
                key = turned
        start = 2 * width + base
        value = joint[start : start + HEAD_DIM]
        vt_ref[base : base + HEAD_DIM, :] = value.astype(BF16)
        kv_ref[head] = jnp.transpose(jnp.concatenate([key, value], axis=0)).astype(BF16)


def project(tokens, weight_t, bias, gain, shift, cosine, sine):
    length, model_width = tokens.shape
    columns = weight_t.shape[0]
    width = columns // 3
    heads = width // HEAD_DIM
    half = HEAD_DIM // 2
    tile = CHUNK
    fixed = lambda i: (0, 0)
    across = lambda i: (0, i)
    return pl.pallas_call(
        qkv_kernel,
        name="project",
        cost_estimate=cost(2 * length * model_width * columns, 12 * length * model_width),
        grid=(length // tile,),
        in_specs=[
            pl.BlockSpec((tile, model_width), lambda i: (i, 0)),
            pl.BlockSpec((columns, model_width), fixed),
            pl.BlockSpec((columns, 1), fixed),
            pl.BlockSpec((1, model_width), fixed),
            pl.BlockSpec((1, model_width), fixed),
            pl.BlockSpec((half, tile), across),
            pl.BlockSpec((half, tile), across),
        ],
        out_specs=[
            pl.BlockSpec((tile, model_width), lambda i: (i, 0)),
            pl.BlockSpec((width, tile), across),
            pl.BlockSpec((width, tile), across),
            pl.BlockSpec((width, tile), across),
            pl.BlockSpec((heads, tile, 2 * HEAD_DIM), lambda i: (0, i, 0)),
        ],
        out_shape=[
            jax.ShapeDtypeStruct((length, model_width), BF16),
            jax.ShapeDtypeStruct((width, length), BF16),
            jax.ShapeDtypeStruct((width, length), BF16),
            jax.ShapeDtypeStruct((width, length), BF16),
            jax.ShapeDtypeStruct((heads, length, 2 * HEAD_DIM), BF16),
        ],
        compiler_params=pltpu.CompilerParams(vmem_limit_bytes=VMEM_LIMIT),
    )(tokens, weight_t, bias, gain, shift, cosine, sine)


def average_kernel(weights_ref, earlier_ref, cotangent_ref, grad_ref, mix_ref, sums_ref):
    @pl.when(pl.program_id(0) == 0)
    def _():
        sums_ref[...] = jnp.zeros_like(sums_ref)

    cotangent = cotangent_ref[...]
    rows, columns = cotangent.shape
    mix = jnp.zeros_like(cotangent)
    for level in range(earlier_ref.shape[0]):
        value = earlier_ref[level].astype(F32)
        weight = weights_ref[level]
        mix = mix + weight * value
        grad_ref[level] = weight * cotangent
        sums_ref[level] += jnp.sum((value * cotangent).reshape(rows // 8, 8, columns), axis=0)
    mix_ref[...] = mix


def average(depth_weights, earlier, cotangent):
    levels, row_count, model_width = earlier.shape
    tile = row_count // 4
    return pl.pallas_call(
        average_kernel,
        name="average",
        cost_estimate=cost(6 * earlier.size, 6 * earlier.size + 8 * cotangent.size),
        grid_spec=pltpu.PrefetchScalarGridSpec(
            num_scalar_prefetch=1,
            grid=(4,),
            in_specs=[
                pl.BlockSpec((levels, tile, model_width), lambda i, w: (0, i, 0)),
                pl.BlockSpec((tile, model_width), lambda i, w: (i, 0)),
            ],
            out_specs=[
                pl.BlockSpec((levels, tile, model_width), lambda i, w: (0, i, 0)),
                pl.BlockSpec((tile, model_width), lambda i, w: (i, 0)),
                pl.BlockSpec((levels, 8, model_width), lambda i, w: (0, 0, 0)),
            ],
        ),
        out_shape=[
            jax.ShapeDtypeStruct(earlier.shape, F32),
            jax.ShapeDtypeStruct(cotangent.shape, F32),
            jax.ShapeDtypeStruct((levels, 8, model_width), F32),
        ],
        compiler_params=pltpu.CompilerParams(vmem_limit_bytes=VMEM_LIMIT),
    )(depth_weights, earlier, cotangent)


def last_mask(odd, rows):
    row = lax.broadcasted_iota(jnp.int32, (rows, BLOCK), 0)
    return row < rows - BLOCK * (1 - odd)


def over_chunks(pair, absorb, state):
    state = lax.fori_loop(0, pair // 2, lambda i, s: absorb(2 * i, 2 * CHUNK, s, False), state)
    return lax.cond(
        pair % 2 == 0,
        lambda s: absorb(pair, CHUNK, s, True),
        lambda s: absorb(pair - 1, 2 * CHUNK, s, True),
        state,
    )


def attend_kernel(core_ref, qt_ref, kv_ref, vt_ref, low_ref, full_ref, stat_ref, scores_ref):
    pair = pl.program_id(0)
    odd = core_ref[0] ^ (pair & 1)
    heads = qt_ref.shape[0] // HEAD_DIM
    blank = jnp.zeros((HEAD_DIM, BLOCK), BF16)
    queries = [
        jnp.concatenate([qt_ref[h * HEAD_DIM : (h + 1) * HEAD_DIM, :], blank], axis=0)
        for h in range(heads)
    ]
    fold = lambda value: value.reshape(value.shape[0] // 8, 8, BLOCK)

    def score(step, size, state, masked):
        keys = pl.ds(pl.multiple_of(step * CHUNK, CHUNK), size)
        fresh = []
        for h in range(heads):
            scores = contract(kv_ref[h, keys, :], queries[h], 1, 0)
            if masked:
                scores = jnp.where(last_mask(odd, size), scores, NEG)
            scores_ref[h, keys, :] = scores
            fresh.append(jnp.maximum(state[h], jnp.max(fold(scores), axis=0)))
        return fresh

    def mix(step, size, state, masked):
        keys = pl.ds(pl.multiple_of(step * CHUNK, CHUNK), size)
        fresh = []
        for h in range(heads):
            total, summed = state[h]
            weights = jnp.exp(scores_ref[h, keys, :] - highest[h])
            values = vt_ref[h * HEAD_DIM : (h + 1) * HEAD_DIM, keys]
            fresh.append(
                (
                    total + jnp.sum(fold(weights), axis=0),
                    summed + contract(values, weights.astype(BF16), 1, 0),
                )
            )
        return fresh

    state = [jnp.full((8, BLOCK), NEG, F32) for _ in range(heads)]
    state = over_chunks(pair, score, state)
    highest = [jnp.max(value, axis=0, keepdims=True) for value in state]
    state = [
        (jnp.zeros((8, BLOCK), F32), jnp.zeros((HEAD_DIM, BLOCK), F32)) for _ in range(heads)
    ]
    state = over_chunks(pair, mix, state)
    for h in range(heads):
        total, summed = state[h]
        total = jnp.sum(total, axis=0, keepdims=True)
        attended = summed / total
        full_ref[0, h * HEAD_DIM : (h + 1) * HEAD_DIM, :] = attended
        low_ref[0, h * HEAD_DIM : (h + 1) * HEAD_DIM, :] = attended.astype(BF16)
        stat_ref[0, h : h + 1, :] = highest[h] + jnp.log(total)


def attend(core, qt, kv, vt):
    width, length = qt.shape
    pairs = length // CHUNK
    own = lambda j, core: (0, 2 * j + (core[0] ^ (j & 1)))
    slot = lambda j, core: (j, 0, 0)
    return pl.pallas_call(
        attend_kernel,
        name="attend",
        cost_estimate=cost(
            2 * 2 * BLOCK * BLOCK * BLOCK * 2 * sum(range(1, pairs + 1)) * (width // HEAD_DIM),
            4 * kv.size + 8 * pairs * width * BLOCK,
            CHUNK * BLOCK * sum(range(1, pairs + 1)) * (width // HEAD_DIM),
        ),
        grid_spec=pltpu.PrefetchScalarGridSpec(
            num_scalar_prefetch=1,
            grid=(pairs,),
            in_specs=[
                pl.BlockSpec((width, BLOCK), own),
                pl.BlockSpec(kv.shape, lambda j, core: (0, 0, 0)),
                pl.BlockSpec(vt.shape, lambda j, core: (0, 0)),
            ],
            out_specs=[
                pl.BlockSpec((1, width, BLOCK), slot),
                pl.BlockSpec((1, width, BLOCK), slot),
                pl.BlockSpec((1, 8, BLOCK), slot),
            ],
            scratch_shapes=[pltpu.VMEM((width // HEAD_DIM, length, BLOCK), F32)],
        ),
        out_shape=[
            jax.ShapeDtypeStruct((pairs, width, BLOCK), BF16),
            jax.ShapeDtypeStruct((pairs, width, BLOCK), F32),
            jax.ShapeDtypeStruct((pairs, 8, BLOCK), F32),
        ],
        compiler_params=pltpu.CompilerParams(vmem_limit_bytes=VMEM_LIMIT),
    )(core, qt, kv, vt)


def retrace_kernel(
    core_ref, qt_ref, grad_ref, full_ref, stat_ref, cos_ref, sin_ref, kv_ref, kt_ref,
    joint_ref, dkv_ref,
):
    step_id = pl.program_id(0)
    pair = pl.num_programs(0) - 1 - step_id
    odd = core_ref[0] ^ (pair & 1)
    width = qt_ref.shape[0]
    heads = width // HEAD_DIM
    half = HEAD_DIM // 2

    @pl.when(step_id == 0)
    def _():
        dkv_ref[...] = jnp.zeros_like(dkv_ref)

    blank = jnp.zeros((HEAD_DIM, BLOCK), BF16)
    lefts, rights, deltas, norms = [], [], [], []
    for h in range(heads):
        rows = slice(h * HEAD_DIM, (h + 1) * HEAD_DIM)
        query = qt_ref[rows, :]
        grad = grad_ref[0, rows, :]
        lefts.append(
            jnp.concatenate(
                [
                    jnp.concatenate([query, blank], axis=1),
                    jnp.concatenate([blank, grad], axis=1),
                ],
                axis=0,
            )
        )
        rights.append(
            jnp.concatenate(
                [
                    jnp.concatenate([blank, query], axis=1),
                    jnp.concatenate([grad, blank], axis=1),
                ],
                axis=0,
            )
        )
        deltas.append(jnp.sum(grad.astype(F32) * full_ref[0, rows, :], axis=0, keepdims=True))
        norms.append(stat_ref[0, h : h + 1, :])

    def absorb(step, state, masked):
        keys = pl.ds(pl.multiple_of(step * CHUNK, CHUNK), CHUNK)
        fresh = []
        for h in range(heads):
            both = contract(kv_ref[h, keys, :], lefts[h], 1, 0)
            probs = jnp.exp(both[:, :BLOCK] - norms[h])
            if masked:
                probs = jnp.where(last_mask(odd, CHUNK), probs, 0.0)
            grad_scores = (probs * (both[:, BLOCK:] - deltas[h])).astype(BF16)
            joined = jnp.concatenate([probs.astype(BF16), grad_scores], axis=1)
            dkv_ref[h, keys, :] += contract(joined, rights[h], 1, 1)
            turned = kt_ref[h * HEAD_DIM : (h + 1) * HEAD_DIM, keys]
            fresh.append(state[h] + contract(turned, grad_scores, 1, 0))
        return fresh

    state = [jnp.zeros((HEAD_DIM, BLOCK), F32) for _ in range(heads)]
    state = lax.fori_loop(0, pair, lambda i, s: absorb(i, s, False), state)
    state = absorb(pair, state, True)
    offset = pl.multiple_of(pair * CHUNK, CHUNK)
    cosine = cos_ref[...]
    sine = sin_ref[...]
    column = lax.broadcasted_iota(jnp.int32, (HEAD_DIM, CHUNK), 1) // BLOCK

    for h in range(heads):
        base = h * HEAD_DIM
        doubled = jnp.concatenate([state[h], state[h]], axis=1) * HEAD_DIM ** (-0.5)
        doubled = jnp.where(column == odd, doubled, 0.0)
        turned_back = jnp.transpose(dkv_ref[h, pl.ds(offset, CHUNK), :])
        for part, value in ((0, doubled), (1, turned_back[:HEAD_DIM])):
            former = value[:half]
            latter = value[half:]
            turned = jnp.concatenate(
                [former * cosine + latter * sine, latter * cosine - former * sine], axis=0
            )
            start = part * width + base
            joint_ref[start : start + HEAD_DIM, :] = turned.astype(BF16)
        start = 2 * width + base
        joint_ref[start : start + HEAD_DIM, :] = turned_back[HEAD_DIM:].astype(BF16)


def retrace(core, qt, grads, full, stats, cosine, sine, kv, kt):
    width, length = qt.shape
    heads = width // HEAD_DIM
    half = HEAD_DIM // 2
    pairs = length // CHUNK
    back = lambda j: pairs - 1 - j
    own = lambda j, core: (0, 2 * back(j) + (core[0] ^ (back(j) & 1)))
    slot = lambda j, core: (back(j), 0, 0)
    across = lambda j, core: (0, back(j))
    return pl.pallas_call(
        retrace_kernel,
        name="retrace",
        cost_estimate=cost(
            5 * 2 * BLOCK * BLOCK * BLOCK * 2 * sum(range(1, pairs + 1)) * heads,
            3 * kv.size + 16 * pairs * width * BLOCK,
            CHUNK * BLOCK * sum(range(1, pairs + 1)) * heads,
        ),
        grid_spec=pltpu.PrefetchScalarGridSpec(
            num_scalar_prefetch=1,
            grid=(pairs,),
            in_specs=[
                pl.BlockSpec((width, BLOCK), own),
                pl.BlockSpec((1, width, BLOCK), slot),
                pl.BlockSpec((1, width, BLOCK), slot),
                pl.BlockSpec((1, 8, BLOCK), slot),
                pl.BlockSpec((half, CHUNK), across),
                pl.BlockSpec((half, CHUNK), across),
                pl.BlockSpec(kv.shape, lambda j, core: (0, 0, 0)),
                pl.BlockSpec(kt.shape, lambda j, core: (0, 0)),
            ],
            out_specs=pl.BlockSpec((3 * width, CHUNK), across),
            scratch_shapes=[pltpu.VMEM((heads, length, 2 * HEAD_DIM), F32)],
        ),
        out_shape=jax.ShapeDtypeStruct((3 * width, length), BF16),
        compiler_params=pltpu.CompilerParams(vmem_limit_bytes=VMEM_LIMIT),
    )(core, qt, grads, full, stats, cosine, sine, kv, kt)


def after(values, *earlier_values):
    values = tuple(values)
    return lax.optimization_barrier(values + tuple(earlier_values))[: len(values)]


def assemble_kernel(place_ref, *refs):
    down_ref, out_ref, late_ref = refs[-3:]
    rep = place_ref[1]
    reps = (len(refs) - 3) // 2
    part = out_ref.shape[0]
    for side in range(2):
        @pl.when(pl.program_id(0) == side)
        def _():
            for k in range(reps):
                piece = refs[side * reps + k]
                rows = piece.shape[1]
                target = rep ^ k

                @pl.when(target < reps - 1)
                def _():
                    down_ref[pl.ds(pl.multiple_of(target * rows, rows), rows), :] = piece[0]

                @pl.when(target == reps - 1)
                def _():
                    out_ref[...] = piece[0, :part]
                    late_ref[0] = piece[0, part : part + 8]


def assemble(place, mine, twin, part):
    owners, rows, columns = mine[0].shape
    reps = len(mine)
    groups = 2 * owners

    def held(side):
        def index(which, z, place):
            moving = (place[0] // 2 + owners - z) % owners
            fixed = (place[0] // 2 + owners - (owners - 1) * (1 - side)) % owners
            return (jnp.where(which == side, moving, fixed), 0, 0)

        return pl.BlockSpec((1, rows, columns), index)

    device = lambda which, z, place: 2 * z + (which ^ (place[0] % 2))
    target = lambda which, z, place: (device(which, z, place), 0)
    return pl.pallas_call(
        assemble_kernel,
        name="assemble",
        cost_estimate=cost(0, 4 * 2 * reps * owners * rows * columns),
        grid_spec=pltpu.PrefetchScalarGridSpec(
            num_scalar_prefetch=1,
            grid=(2, owners),
            in_specs=[held(0)] * reps + [held(1)] * reps,
            out_specs=[
                pl.BlockSpec(((reps - 1) * rows, columns), target),
                pl.BlockSpec((part, columns), target),
                pl.BlockSpec(
                    (1, 8, columns), lambda which, z, place: (device(which, z, place), 0, 0)
                ),
            ],
        ),
        out_shape=[
            jax.ShapeDtypeStruct((groups * (reps - 1) * rows, columns), BF16),
            jax.ShapeDtypeStruct((groups * part, columns), BF16),
            jax.ShapeDtypeStruct((groups, 8, columns), BF16),
        ],
        compiler_params=pltpu.CompilerParams(vmem_limit_bytes=VMEM_LIMIT),
    )(place, *mine, *twin)


def swap_core(value):
    groups = lax.axis_size("shard")
    return lax.ppermute(value, "shard", [(i, i ^ 1) for i in range(groups)])


def shift_owner(value, distance):
    groups = lax.axis_size("shard")
    step = 2 * distance
    return lax.ppermute(value, "shard", [(i, (i + step) % groups) for i in range(groups)])


def cross_rep(value, mask):
    return lax.ppermute(value, "rep", [(i, i ^ mask) for i in range(lax.axis_size("rep"))])


def pick(stacked, index, axis=0):
    return lax.dynamic_index_in_dim(stacked, index, axis, keepdims=False)


def add_low(*values):
    total = values[0].astype(F32)
    for value in values[1:]:
        total = total + value.astype(F32)
    return total.astype(BF16)


def fold_core(partial_sums, core):
    halves = partial_sums.reshape((-1, 2) + partial_sums.shape[1:])
    received = swap_core(pick(halves, 1 - core, 1))
    return add_low(pick(halves, core, 1), received)


def rep_parts(value):
    reps = lax.axis_size("rep")
    owners, rows, columns = value.shape
    return value.reshape(owners, reps, rows // reps, columns)


def send_rep(value):
    rep = lax.axis_index("rep")
    parts = rep_parts(value)
    return [cross_rep(pick(parts, rep ^ k, 1), k) for k in range(1, lax.axis_size("rep"))]


def pick_parts(value):
    rep = lax.axis_index("rep")
    parts = rep_parts(value)
    return [pick(parts, rep ^ k, 1) for k in range(lax.axis_size("rep"))]


def join_rep(value, received):
    return add_low(pick(rep_parts(value), lax.axis_index("rep"), 1), *received)


def unpack_kernel(rep_ref, *refs):
    in_ref, out_ref, qkv_ref, small_ref, down_ref = refs[-5:]
    pieces = refs[:-5]
    reps = len(pieces) // 3
    hidden_width = in_ref.shape[1]
    model_width = out_ref.shape[1]
    columns = qkv_ref.shape[1] // 3
    owners = down_ref.shape[0] // in_ref.shape[0]
    width = columns // owners
    for k in range(reps):
        pair, joint, down = pieces[k::reps]
        rows = pair.shape[0]
        first = pl.multiple_of((rep_ref[0] ^ k) * rows, 8)
        own = pl.ds(first, rows)
        in_ref[own, :] = pair[:, :hidden_width].astype(F32)
        out_ref[own, :] = pair[:, hidden_width:].astype(F32)
        whole = joint[:, : 3 * columns].astype(F32)
        for part in range(3):
            qkv_ref[own, part * columns : (part + 1) * columns] = jnp.concatenate(
                [
                    whole[:, (3 * z + part) * width : (3 * z + part + 1) * width]
                    for z in range(owners)
                ],
                axis=1,
            )
        small_ref[own, :] = joint[:, 3 * columns :].astype(F32)
        for z in range(owners):
            block = pl.ds(pl.multiple_of(owners * first + z * rows, 8), rows)
            down_ref[block, :] = down[:, z * model_width : (z + 1) * model_width].astype(F32)


def unpack(rep, pair, joint, down, widths):
    hidden_width, model_width, columns = widths
    pieces = [*pair, *joint, *down]
    rows = len(pair) * pair[0].shape[0]
    owners = model_width * 3 // columns
    shapes = [
        (rows, hidden_width),
        (rows, model_width),
        (rows, 3 * model_width),
        (rows, 128),
        (owners * rows, model_width),
    ]
    whole = pl.BlockSpec(memory_space=pltpu.VMEM)
    return pl.pallas_call(
        unpack_kernel,
        name="unpack",
        cost_estimate=cost(0, 6 * sum(a * b for a, b in shapes)),
        in_specs=[pl.BlockSpec(memory_space=pltpu.SMEM)] + [whole] * len(pieces),
        out_specs=[whole] * 5,
        out_shape=[jax.ShapeDtypeStruct(shape, F32) for shape in shapes],
        compiler_params=pltpu.CompilerParams(vmem_limit_bytes=VMEM_LIMIT),
    )(rep, *pieces)


def every_rep(value):
    return [value] + [cross_rep(value, k) for k in range(1, lax.axis_size("rep"))]


def exchange_owner(value, owner):
    owners = value.shape[0]
    received = [pick(value, owner)]
    for k in range(1, owners):
        received.append(shift_owner(pick(value, (owner + k) % owners), k))
    return received


def middle_kernel(
    core_ref, weights_ref, mixed_ref, x_ref, cotangent_ref, w_out_ref, b_out_ref, gain_ref,
    shift_ref, w_in_ref, b_in_ref, grad_ref,
    middle_ref, low_ref, active_ref, hidden_ref, total_ref, branch_ref, send_ref,
    sums_ref, hidden_sums_ref, plain_ref, scale_ref, back_ref,
):
    step = pl.program_id(0)
    core = core_ref[0]
    owners = mixed_ref.shape[0] // 2
    width = mixed_ref.shape[1]

    @pl.when(step == 0)
    def _():
        for half in range(2):
            rows = slice(half * BLOCK, (half + 1) * BLOCK)
            mixed = jnp.concatenate(
                [mixed_ref[2 * z + (core ^ half)] for z in range(owners)], axis=0
            )
            branch = contract(mixed, w_out_ref[...], 0, 0) + b_out_ref[...]
            middle = x_ref[rows, :].astype(F32) + branch
            middle_ref[rows, :] = middle
            center = middle - jnp.mean(middle, axis=-1, keepdims=True)
            scale = lax.rsqrt(jnp.mean(center * center, axis=-1, keepdims=True) + EPSILON)
            plain = center * scale
            scale_ref[rows, :] = jnp.broadcast_to(scale, (BLOCK, scale_ref.shape[1]))
            plain_ref[rows, :] = plain
            low_ref[rows, :] = (plain * gain_ref[...] + shift_ref[...]).astype(BF16)
        back_ref[...] = jnp.zeros_like(back_ref)

    hidden = contract(low_ref[...], w_in_ref[...], 1, 0) + b_in_ref[...]
    square = hidden * hidden
    bend = math.sqrt(2 / math.pi)
    turned = jnp.tanh(hidden * (bend + (bend * 0.044715) * square))
    share = 0.5 + 0.5 * turned
    active_ref[...] = (hidden * share).astype(BF16)
    slope = (0.5 * hidden) * (1.0 - turned * turned) * (bend + (3 * bend * 0.044715) * square)
    grad = (grad_ref[...] * (share + slope)).astype(BF16)
    hidden_ref[...] = grad
    hidden_sums_ref[...] = jnp.sum(grad.astype(F32), axis=0, keepdims=True)
    back_ref[...] += contract(grad, w_in_ref[...], 1, 1)

    @pl.when(step == pl.num_programs(0) - 1)
    def _():
        weight = weights_ref[4]
        sums = [jnp.zeros((1, back_ref.shape[1]), F32)] * 3
        for half in range(2):
            rows = slice(half * BLOCK, (half + 1) * BLOCK)
            back = back_ref[rows, :]
            plain = plain_ref[rows, :]
            scaled = back * gain_ref[...]
            total = weight * cotangent_ref[rows, :] + scale_ref[rows, :1] * (
                scaled
                - jnp.mean(scaled, axis=-1, keepdims=True)
                - plain * jnp.mean(scaled * plain, axis=-1, keepdims=True)
            )
            total_ref[rows, :] = total
            low = total.astype(BF16)
            branch_ref[rows, :] = low
            mixed = contract(w_out_ref[...], low, 1, 1).astype(BF16)
            for z in range(owners):
                send_ref[2 * z + (core ^ half)] = mixed[z * width : (z + 1) * width, :]
            for i, value in enumerate((low.astype(F32), back * plain, back)):
                sums[i] = sums[i] + jnp.sum(value, axis=0, keepdims=True)
        for i in range(3):
            sums_ref[i : i + 1, :] = sums[i]


def middle_part(
    core, depth_weights, mixed, x, cotangent, w_out, b_out, gain, shift, w_in, b_in, grad_active
):
    rows, model_width = x.shape
    hidden_width = w_in.shape[1]
    chunk = CHUNK
    whole = lambda value: pl.BlockSpec(value.shape, lambda j, *_: (0,) * value.ndim)
    across = pl.BlockSpec((rows, chunk), lambda j, *_: (0, j))
    line = pl.BlockSpec((1, chunk), lambda j, *_: (0, j))
    shapes = [
        jax.ShapeDtypeStruct((rows, model_width), F32),
        jax.ShapeDtypeStruct((rows, model_width), BF16),
        jax.ShapeDtypeStruct((rows, hidden_width), BF16),
        jax.ShapeDtypeStruct((rows, hidden_width), BF16),
        jax.ShapeDtypeStruct((rows, model_width), F32),
        jax.ShapeDtypeStruct((rows, model_width), BF16),
        jax.ShapeDtypeStruct(mixed.shape, BF16),
        jax.ShapeDtypeStruct((8, model_width), F32),
        jax.ShapeDtypeStruct((1, hidden_width), F32),
    ]
    out_specs = [whole(shape) for shape in shapes]
    out_specs[2] = out_specs[3] = across
    out_specs[8] = line
    return pl.pallas_call(
        middle_kernel,
        name="middle",
        cost_estimate=cost(
            4 * rows * model_width * (hidden_width + model_width),
            2 * w_in.size + 8 * grad_active.size,
            grad_active.size,
        ),
        grid_spec=pltpu.PrefetchScalarGridSpec(
            num_scalar_prefetch=2,
            grid=(hidden_width // chunk,),
            in_specs=[
                whole(mixed),
                whole(x),
                whole(cotangent),
                whole(w_out),
                whole(b_out),
                whole(gain),
                whole(shift),
                pl.BlockSpec((model_width, chunk), lambda j, *_: (0, j)),
                line,
                across,
            ],
            out_specs=out_specs,
            scratch_shapes=[
                pltpu.VMEM((rows, model_width), F32),
                pltpu.VMEM((rows, 128), F32),
                pltpu.VMEM((rows, model_width), F32),
            ],
        ),
        out_shape=shapes,
        compiler_params=pltpu.CompilerParams(vmem_limit_bytes=VMEM_LIMIT),
    )(
        core, depth_weights, mixed, x, cotangent, w_out, b_out, gain, shift, w_in, b_in,
        grad_active,
    )


def pair_kernel(core_ref, low_ref, hidden_ref, mixed_ref, branch_ref, own_ref, other_ref, full_ref):
    step = pl.program_id(0)
    core = core_ref[0]
    owners, part, _ = own_ref.shape

    @pl.when(step < pl.num_programs(0) - 1)
    def _():
        full_ref[...] = contract(low_ref[...], hidden_ref[...], 0, 0)

    @pl.when(step == pl.num_programs(0) - 1)
    def _():
        for half in range(2):
            mixed = jnp.concatenate(
                [mixed_ref[2 * z + (core ^ half)] for z in range(owners)], axis=0
            )
            product = contract(mixed, branch_ref[half * BLOCK : (half + 1) * BLOCK, :], 1, 0)
            if half == 0:
                full_ref[...] = product
            else:
                full_ref[...] += product

    for z in range(owners):
        for side, ref in ((0, own_ref), (1, other_ref)):
            start = pl.multiple_of((2 * z + (core ^ side)) * part, part)
            ref[z] = full_ref[pl.ds(start, part), :].astype(BF16)


def pair_sums(core, low, hidden, mixed, branch):
    rows, model_width = low.shape
    owners = mixed.shape[0] // 2
    part = model_width // (2 * owners)
    steps = hidden.shape[1] // model_width
    whole = lambda value: pl.BlockSpec(value.shape, lambda j, core: (0,) * value.ndim)
    target = pl.BlockSpec((owners, part, model_width), lambda j, core: (0, 0, j))
    shape = jax.ShapeDtypeStruct((owners, part, (steps + 1) * model_width), BF16)
    return pl.pallas_call(
        pair_kernel,
        name="pair_sums",
        grid_spec=pltpu.PrefetchScalarGridSpec(
            num_scalar_prefetch=1,
            grid=(steps + 1,),
            in_specs=[
                whole(low),
                pl.BlockSpec(
                    (rows, model_width), lambda j, core: (0, jnp.minimum(j, steps - 1))
                ),
                whole(mixed),
                whole(branch),
            ],
            out_specs=[target, target],
            scratch_shapes=[pltpu.VMEM((model_width, model_width), F32)],
        ),
        out_shape=[shape, shape],
        compiler_params=pltpu.CompilerParams(vmem_limit_bytes=VMEM_LIMIT),
    )(core, low, hidden, mixed, branch)


def head_split_device(
    block_in,
    earlier,
    cotangent,
    qkv_weight,
    out_weight,
    in_weight,
    down_weight,
    qk_bias,
    value_bias,
    out_bias,
    in_bias,
    down_bias,
    gain_one,
    shift_one,
    gain_two,
    shift_two,
    depth_weights,
):
    row_count, model_width = block_in.shape
    hidden_width = in_weight.shape[1]
    groups = lax.axis_size("shard")
    owners = groups // 2
    width = model_width // owners
    part = model_width // groups
    length = row_count * groups
    half = HEAD_DIM // 2
    member = lax.axis_index("shard")
    owner = member // 2
    core = member % 2

    pieces = qkv_weight.astype(BF16).reshape(part, 3, owners, width)
    pieces = jnp.transpose(pieces, (2, 0, 1, 3)).reshape(owners, part, 3 * width)
    early = jnp.concatenate([qk_bias, value_bias, gain_one, shift_one]).astype(BF16)
    early = jnp.pad(early, (0, 8 * 3 * width - early.shape[0])).reshape(8, 3 * width)
    early = jnp.broadcast_to(early, (owners, 8, 3 * width))
    packets = exchange_owner(jnp.concatenate([pieces, early], axis=1), owner)
    packet = jnp.stack(packets)
    other_packet = swap_core(packet)

    tokens = lax.all_gather(block_in, "shard", axis=0, tiled=True)
    grad_earlier, mix, depth_sums = average(depth_weights, earlier, cotangent)

    by_core = jnp.stack([packet, other_packet])
    packet = jnp.stack(
        [
            lax.dynamic_slice(
                by_core,
                (core ^ (d % 2), (owner - d // 2) % owners, 0, 0),
                (1, 1, part + 8, 3 * width),
            )[0, 0]
            for d in range(groups)
        ]
    )
    w_own = packet[:, :part].reshape(model_width, 3 * width)
    early = packet[:, part].astype(F32)
    b_qk = early[:, : 2 * part].reshape(2 * model_width)
    b_value = early[:, 2 * part : 3 * part].reshape(model_width)
    g_one = early[:, 3 * part : 4 * part].reshape(1, model_width)
    s_one = early[:, 4 * part : 5 * part].reshape(1, model_width)
    b_joint = jnp.concatenate([b_qk, b_value]).reshape(3, owners, width)
    b_own = lax.dynamic_index_in_dim(b_joint, owner, 1, keepdims=False).reshape(3 * width, 1)
    w_turned = jnp.transpose(w_own)

    freqs = 10000.0 ** (-jnp.arange(half, dtype=F32) / half)
    angles = freqs[:, None] * jnp.arange(length, dtype=jnp.int32).astype(F32)[None, :]
    cosine = jnp.cos(angles)
    sine = jnp.sin(angles)
    core_index = core.astype(jnp.int32).reshape(1)

    late = jnp.concatenate([out_bias, in_bias, down_bias, gain_two, shift_two]).astype(BF16)
    late = late.reshape(-1, model_width)
    hidden_part = hidden_width // groups
    share = hidden_part // 3
    last = jnp.concatenate([out_weight.astype(BF16), late], axis=0)
    last = jnp.pad(last, ((0, share - last.shape[0]), (0, 0)))
    rep = lax.axis_index("rep")
    tail_packet = lax.dynamic_slice_in_dim(
        jnp.concatenate([down_weight.astype(BF16), last], axis=0), rep * share, share, 0
    )
    tokens, w_turned, b_own, cosine, sine, mix, tail_packet, in_packet = after(
        (tokens, w_turned, b_own, cosine, sine, mix, tail_packet, in_weight.astype(BF16)),
        grad_earlier,
        depth_sums,
    )
    tail_parts = [tail_packet] + [shift_owner(tail_packet, k) for k in range(1, owners)]
    states = project(tokens, w_turned, b_own, g_one, s_one, cosine, sine)
    plain_all, qt, kt, vt, kv, *tail_parts = lax.optimization_barrier(
        (*states, *tail_parts)
    )
    tail_stack = jnp.stack(tail_parts)
    qt, tail_stack, in_packet = lax.optimization_barrier((qt, tail_stack, in_packet))
    w_in = lax.all_gather(in_packet, "shard", axis=0, tiled=True)
    tail_mine = [tail_stack] + [cross_rep(tail_stack, m) for m in range(1, 4)]
    mixed_own, attended, stats = attend(core_index, qt, kv, vt)
    mixed_own, attended, stats, *tail_mine = lax.optimization_barrier(
        (mixed_own, attended, stats, *tail_mine)
    )
    mixed_two = lax.all_to_all(mixed_own, "shard", 0, 0)
    tail_other = [swap_core(value) for value in tail_mine]
    w_down, w_out, late = assemble(
        jnp.stack([member, rep]).astype(jnp.int32), tail_mine, tail_other, part
    )
    late = late[:, 0].astype(F32)
    grad_result = depth_weights[4] * cotangent
    down_grad = grad_result.astype(BF16)
    grad_active = contract(down_grad, w_down, 1, 1)
    mixed_two, grad_active = lax.optimization_barrier((mixed_two, grad_active))
    row = lambda first, size: late[:, first : first + size].reshape(1, groups * size)
    b_out = row(0, part)
    b_in = row(part, hidden_part)
    b_down = row(part + hidden_part, part)
    g_two = row(2 * part + hidden_part, part)
    s_two = row(3 * part + hidden_part, part)

    inputs = block_in.astype(F32)
    (
        middle, normed_two_low, active, grad_hidden, grad_middle, branch_grad, grad_own,
        token_sums, grad_in_b,
    ) = middle_part(
        core_index, depth_weights, mixed_two, block_in, cotangent, w_out, b_out, g_two, s_two,
        w_in, b_in, grad_active,
    )
    grad_out_b, grad_gain_two, grad_shift_two = (token_sums[i] for i in range(3))
    grad_in_b = grad_in_b[0]
    grad_own = lax.all_to_all(grad_own, "shard", 0, 0)
    folded, twin = pair_sums(core_index, normed_two_low, grad_hidden, mixed_two, branch_grad)
    folded = add_low(folded, swap_core(twin))
    grad_down_w = contract(active, down_grad, 0, 0)
    grad_down_b = jnp.sum(down_grad.astype(F32), axis=0)
    grad_own, folded, down_sums = lax.optimization_barrier(
        (grad_own, folded, grad_down_w.astype(BF16))
    )
    sent = send_rep(folded)
    down_sums = lax.psum_scatter(down_sums, "shard", scatter_dimension=0, tiled=True)
    joint_t = retrace(core_index, qt, grad_own, attended, stats, cosine, sine, kv, kt)
    joint_t, folded, *sent = lax.optimization_barrier((joint_t, folded, *sent))
    grad_normed = contract(joint_t, w_own, 0, 1).astype(BF16)
    joint_t, folded, plain_all, down_sums, *sent = after(
        (joint_t, folded, plain_all, down_sums, *sent), grad_normed
    )
    grad_normed = lax.psum_scatter(
        grad_normed, "shard", scatter_dimension=0, tiled=True
    )
    folded = join_rep(folded, sent)

    product = contract(plain_all, joint_t, 0, 1)
    joint_sums = jnp.sum(joint_t.astype(F32), axis=1)
    arrived = exchange_owner(folded, owner)
    product, joint_sums, *arrived = lax.optimization_barrier((product, joint_sums, *arrived))
    pair_pieces = every_rep(add_low(*arrived))
    w_wide = w_own.astype(F32)
    grad_gain_one = jnp.sum(product * w_wide, axis=1)
    grad_shift_one = jnp.sum(joint_sums[None, :] * w_wide, axis=1)
    grad_qkv = g_one.reshape(-1, 1) * product + s_one.reshape(-1, 1) * joint_sums[None, :]
    grad_qkv = grad_qkv.astype(BF16).reshape(groups, part, 3 * width)
    spread_sums = lax.dynamic_update_slice(
        jnp.zeros((3, model_width), F32), joint_sums.reshape(3, width), (0, owner * width)
    ).reshape(3 * model_width)
    vectors = (
        spread_sums[: 2 * model_width],
        spread_sums[2 * model_width :],
        grad_out_b,
        grad_in_b,
        grad_down_b,
        grad_gain_one,
        grad_shift_one,
        grad_gain_two,
        grad_shift_two,
    )
    small = jnp.concatenate([vector.reshape(groups, -1) for vector in vectors], axis=1)
    small = jnp.pad(small, ((0, 0), (0, part * 128 - small.shape[1]))).astype(BF16)
    small = jnp.transpose(small.reshape(groups, 128, part), (0, 2, 1))
    mixed_sums = fold_core(jnp.concatenate([grad_qkv, small], axis=2), core)
    down_parts = pick_parts(down_sums[None])
    down_rows = part // 4
    columns = 3 * width + 128
    sums_parts = pick_parts(mixed_sums)
    received = [
        cross_rep(
            jnp.concatenate([sums, down.reshape(owners, down_rows, model_width)], axis=2), k
        )
        for k, (sums, down) in enumerate(zip(sums_parts[1:], down_parts[1:]), 1)
    ]
    (active,) = after((active,), *sums_parts)
    result = middle + contract(active, w_down, 1, 0) + b_down
    layer_out = depth_weights[4] * result + mix
    local_depth = jnp.concatenate(
        [jnp.sum(depth_sums, axis=(1, 2)), jnp.sum(result * cotangent)[None]]
    )
    layer_out, local_depth, *arrived = lax.optimization_barrier(
        (layer_out, local_depth, *received, *pair_pieces)
    )
    received, pair_pieces = arrived[:3], arrived[3:]
    depth = local_depth + swap_core(local_depth)
    depth = depth + cross_rep(depth, 1)
    depth = depth + cross_rep(depth, 2)
    mixed_sums = add_low(sums_parts[0], *[value[:, :, :columns] for value in received])
    down_sums = add_low(
        down_parts[0].reshape(owners, down_rows, model_width),
        *[value[:, :, columns:] for value in received],
    )
    down_pieces = every_rep(jnp.concatenate([down_sums[k] for k in range(owners)], axis=1))
    arrived = exchange_owner(mixed_sums, owner)
    depth = depth + lax.ppermute(depth, "shard", [(i, i ^ 2) for i in range(groups)])
    grad_depth = depth + lax.ppermute(depth, "shard", [(i, i ^ 4) for i in range(groups)])
    grad_depth, *arrived = lax.optimization_barrier((grad_depth, *arrived, *down_pieces))
    arrived, down_pieces = arrived[:owners], arrived[owners:]
    small = add_low(*[value[:, 3 * width :] for value in arrived])
    by_distance = jnp.stack([value[:, : 3 * width] for value in arrived])
    by_owner = [pick(by_distance, (owner - k) % owners) for k in range(owners)]
    sum_in, sum_out, sum_qkv, small, sum_down = unpack(
        lax.axis_index("rep").astype(jnp.int32).reshape(1),
        pair_pieces,
        every_rep(jnp.concatenate([*by_owner, small], axis=1)),
        down_pieces,
        (hidden_width, model_width, 3 * width),
    )
    small = jnp.transpose(small).reshape(-1)
    small_outs = []
    start = 0
    for vector in vectors:
        size = vector.shape[0] // groups
        small_outs.append(small[start : start + size])
        start += size
    finished = (layer_out, sum_qkv, sum_out, sum_in, sum_down, grad_depth, *small_outs)
    grad_normed, layer_out, sum_qkv, sum_out, sum_in, sum_down, grad_depth, *small_outs = (
        lax.optimization_barrier((grad_normed, *finished))
    )
    grad_normed = grad_normed.astype(F32)
    center = inputs - jnp.mean(inputs, axis=-1, keepdims=True)
    scale = lax.rsqrt(jnp.mean(center * center, axis=-1, keepdims=True) + EPSILON)
    plain = center * scale
    scaled = grad_normed * g_one
    grad_block = grad_middle + scale * (
        scaled
        - jnp.mean(scaled, axis=-1, keepdims=True)
        - plain * jnp.mean(scaled * plain, axis=-1, keepdims=True)
    )

    return (
        layer_out,
        grad_block,
        grad_earlier,
        sum_qkv,
        sum_out,
        sum_in,
        sum_down,
        *small_outs,
        grad_depth,
    )


def per_device(*args):
    block_in = args[0]
    row_count, model_width = block_in.shape
    groups = lax.axis_size("shard")
    head_count = model_width // HEAD_DIM
    late_size = (4 * model_width + args[5].shape[1]) // groups
    if (
        groups == 8
        and lax.axis_size("rep") == 4
        and row_count == CHUNK
        and head_count % (groups // 2) == 0
        and head_count // (groups // 2) <= 8
        and late_size % model_width == 0
        and args[5].shape[1] % (3 * groups) == 0
        and model_width // groups + late_size // model_width
        <= args[5].shape[1] // (3 * groups)
    ):
        return head_split_device(*args)
    return generic_device(*args)


def solution(mesh):
    placed = (
        P(("rep", "shard"), None),
        P(None, ("rep", "shard"), None),
        P(("rep", "shard"), None),
        P("shard", None),
        P("shard", None),
        P("shard", None),
        P("shard", None),
        P("shard"),
        P("shard"),
        P("shard"),
        P("shard"),
        P("shard"),
        P("shard"),
        P("shard"),
        P("shard"),
        P("shard"),
        P(),
    )
    return jax.shard_map(
        per_device,
        mesh=mesh,
        in_specs=placed,
        out_specs=(
            P(("rep", "shard"), None),
            P(("rep", "shard"), None),
            P(None, ("rep", "shard"), None),
            P("shard", None),
            P("shard", None),
            P("shard", None),
            P("shard", None),
            P("shard"),
            P("shard"),
            P("shard"),
            P("shard"),
            P("shard"),
            P("shard"),
            P("shard"),
            P("shard"),
            P("shard"),
            P(),
        ),
        check_vma=False,
    )
```

profile of v0, /device:TPU:0, one launch (start us, length us, event | category | flops | bytes accessed | tf_op | source)
XLA Modules:
  0.0 412.7 jit_solution(3299967195387149044)
XLA Ops:
  13.0 3.1 collective-permute-start
  16.1 2.6 collective-permute-start.1
  20.0 2.8 multiply_sine_fusion
  22.9 12.8 %collective-permute-done.1 = bf16[104,576]{0,1:T(8,128)(2,1)S(1)} collective-permute-done((bf16[104,576]{0,1:T(8,128)(2,1)S(1)}, bf16[104,576]{0,1:T(8,128)(2,1)S(1)}, u32[]{:S(2)}, u32[]{:S(2)}) %collective-permute-start.1) | collective-permute-done | bytes 119840 | tf_op jit(solution)/shard_map/ppermute | solution.py:789
  40.9 7.4 %average.1 = (f32[4,512,768]{2,1,0:T(8,128)}, f32[512,768]{1,0:T(8,128)}, f32[4,8,768]{2,1,0:T(8,128)}) custom-call(f32[5]{0:T(128)} %weights_ref.3, bf16[4,512,768]{2,1,0:T(8,128)(2,1)} %earlier_ref.1, f32[512,768]{1,0:T(8,128)} %cotangent_ref.3), custom_call_target="tpu_custom_call" | custom-call | flops 9437184 | bytes 12582912 | tf_op jit(solution)/shard_map/average/pallas_call | solution.py:462
  55.9 27.9 %all-gather.3.cloned.1.call-done.x_ref = bf16[4096,768]{1,0:T(8,128)(2,1)} async-done(((bf16[512,768]{1,0:T(8,128)(2,1)}), bf16[4096,768]{1,0:T(8,128)(2,1)}) %all-gather.3.cloned.1.call-update) | async-done | bytes 6291472 | tf_op jit(solution)/shard_map/all_gather | solution.py:1127
  83.8 1.8 collective-permute-start.6
  87.2 13.5 %project.1 = (bf16[4096,768]{1,0:T(8,128)(2,1)}, bf16[192,4096]{1,0:T(8,128)(2,1)}, bf16[192,4096]{1,0:T(8,128)(2,1)}, bf16[192,4096]{1,0:T(8,128)(2,1)}, bf16[3,4096,128]{2,1,0:T(8,128)(2,1)}) custom-call(bf16[4096,768]{1,0:T(8,128)(2,1)} %all-gather.3.cloned.1.call-done.x_ref, bf16[576,768]{1,0:T(8,128)(2,1)} %bitcast.161, f32[576,1]{1,0:T(8,128)} %copy.85.bias_ref, ...), custom_call_target="tpu_custom_call" | custom-call | flops 3623878656 | bytes 37748736 | tf_op jit(solution)/shard_map/project/pallas_call | solution.py:410
  101.9 2.5 collective-permute-start.9
  105.4 26.0 %attend.1 = (bf16[8,192,256]{2,1,0:T(8,128)(2,1)}, f32[8,192,256]{2,1,0:T(8,128)}, f32[8,8,256]{2,1,0:T(8,128)}) custom-call(s32[1]{0:T(128)} %bitcast.core_ref, bf16[192,4096]{1,0:T(8,128)(2,1)} %get-tuple-element.152.qt_ref, bf16[3,4096,128]{2,1,0:T(8,128)(2,1)} %get-tuple-element.153.kv_ref, bf16[192,4096]{1,0:T(8,128)(2,1)} %get-tuple-element.154.vt_ref), custom_call_target="tpu_custom_call" | custom-call | flops 14495514624 | bytes 9437184 | tf_op jit(solution)/shard_map/attend/pallas_call | solution.py:561
  131.5 6.8 %collective-permute-done.8.refs_2_ = bf16[4,128,768]{2,1,0:T(8,128)(2,1)S(1)} collective-permute-done((bf16[4,128,768]{2,1,0:T(8,128)(2,1)S(1)}, bf16[4,128,768]{2,1,0:T(8,128)(2,1)S(1)}, u32[]{:S(2)}, u32[]{:S(2)}) %collective-permute-start.8) | collective-permute-done | bytes 786464 | tf_op jit(solution)/shard_map/ppermute | solution.py:793
  141.8 5.5 %all-to-all-start = ((bf16[8,192,256]{2,1,0:T(8,128)(2,1)}), bf16[8,192,256]{2,1,0:T(8,128)(2,1)S(1)}, u32[]{:S(2)}, u32[]{:S(2)}) async-start(bf16[8,192,256]{2,1,0:T(8,128)(2,1)} %get-tuple-element.159), calls=%async_computation | async-start | bytes 1572864 | tf_op jit(solution)/shard_map/all_to_all | solution.py:1185
  147.9 9.5 %assemble.1 = (bf16[3072,768]{1,0:T(8,128)(2,1)}, bf16[768,768]{1,0:T(8,128)(2,1)}, bf16[8,8,768]{2,1,0:T(8,128)(2,1)}) custom-call(s32[2]{0:T(128)} %pad_add_fusion.place_ref, bf16[4,128,768]{2,1,0:T(8,128)(2,1)} %copy-done.11, bf16[4,128,768]{2,1,0:T(8,128)(2,1)} %collective-permute-done.7.refs_1_, bf16[4,128,768]{2,1,0:T(8,128)(2,1)} %copy-done.22, ...), custom_call_target="tpu_custom_call" | custom-call | bytes 12582912 | tf_op jit(solution)/shard_map/assemble/pallas_call | solution.py:756
  161.1 6.9 %fusion.52.grad_ref = f32[512,3072]{1,0:T(8,128)} fusion(bf16[512,768]{1,0:T(8,128)(2,1)S(1)} %copy-done.23, bf16[3072,768]{1,0:T(8,128)(2,1)} %get-tuple-element.164), kind=kOutput, calls=%fused_computation.183 | convolution fusion | flops 2415919104 | bytes 11796480 | tf_op jit(solution)/shard_map/dot_general | solution.py:361
  168.0 2.3 all-to-all-done.mixed_ref
  171.2 19.2 %middle.1 = (f32[512,768]{1,0:T(8,128)}, bf16[512,768]{1,0:T(8,128)(2,1)}, bf16[512,3072]{1,0:T(8,128)(2,1)}, bf16[512,3072]{1,0:T(8,128)(2,1)}, f32[512,768]{1,...) custom-call(s32[1]{0:T(128)} %bitcast.core_ref, ...), custom_call_target="tpu_custom_call" | custom-call | flops 6039797760 | bytes 17301504 | tf_op jit(solution)/shard_map/middle/pallas_call | solution.py:992
  190.4 8.5 %pair_sums.1 = (bf16[4,96,3840]{2,1,0:T(8,128)(2,1)}, bf16[4,96,3840]{2,1,0:T(8,128)(2,1)}) custom-call(s32[1]{0:T(128)} %bitcast.core_ref, bf16[512,768]{1,0:T(8,128)(2,1)} %get-tuple-element.171.low_ref, bf16[512,3072]{1,0:T(8,128)(2,1)} %get-tuple-element.172.hidden_ref, bf16[8,192,256]{2,1,0:T(8,128)(2,1)} %copy-done.13, ...), custom_call_target="tpu_custom_call" | custom-call | tf_op jit(solution)/shard_map/pair_sums/pallas_call | solution.py:1065
  198.9 4.2 %all-to-all-start.1 = ((bf16[8,192,256]{2,1,0:T(8,128)(2,1)}), bf16[8,192,256]{2,1,0:T(8,128)(2,1)}, u32[]{:S(2)}, u32[]{:S(2)}) async-start(bf16[8,192,256]{2,1,0:T(8,128)(2,1)} %get-tuple-element.170), calls=%async_computation.1 | async-start | bytes 1572864 | tf_op jit(solution)/shard_map/all_to_all | solution.py:1212
  203.2 6.9 %convolution_convert_fusion.1 = bf16[3072,768]{1,0:T(8,128)(2,1)} fusion(bf16[512,3072]{1,0:T(8,128)(2,1)} %get-tuple-element.200, bf16[512,768]{1,0:T(8,128)(2,1)} %get-tuple-element.260), kind=kOutput, calls=%fused_computation.3 | convolution fusion | flops 2418278400 | bytes 8650752 | tf_op jit(solution)/shard_map/dot_general | solution.py:361
  211.8 3.4 add_convert_fusion
  215.2 9.0 %all-to-all-done.1.grad_ref = bf16[8,192,256]{2,1,0:T(8,128)(2,1)} async-done(((bf16[8,192,256]{2,1,0:T(8,128)(2,1)}), bf16[8,192,256]{2,1,0:T(8,128)(2,1)}, u32[]{:S(2)}, u32[]{:S(2)}) %all-to-all-start.1) | async-done | bytes 786464 | tf_op jit(solution)/shard_map/all_to_all | solution.py:1212
  224.1 12.7 %reduce-scatter.3.cloned.1.call-start = ((), (), s32[]{:S(2)}) async-start(), calls=%async_computation.6 | async-start | bytes 7077888 | tf_op jit(solution)/shard_map/reduce_scatter | solution.py:1228
  237.2 2.2 collective-permute-start.17
  240.7 43.9 %retrace.1 = bf16[576,4096]{1,0:T(8,128)(2,1)} custom-call(s32[1]{0:T(128)} %bitcast.core_ref, bf16[192,4096]{1,0:T(8,128)(2,1)} %get-tuple-element.152.qt_ref, bf16[8,192,256]{2,1,0:T(8,128)(2,1)} %all-to-all-done.1.grad_ref, f32[8,192,256]{2,1,0:T(8,128)} %get-tuple-element.178.full_ref, f32[8,8,256]{2,1,0:T(8,128)} %get-tuple-element.179.stat_ref, ...), custom_call_target="tpu_custom_call" | custom-call | flops 36238786560 | bytes 11010048 | tf_op jit(solution)/shard_map/retrace/pallas_call | solution.py:684
  284.6 9.6 %convolution_convert_fusion = bf16[4096,768]{1,0:T(8,128)(2,1)} fusion(bf16[576,4096]{1,0:T(8,128)(2,1)} %retrace.1, bf16[768,576]{1,0:T(8,128)(2,1)S(1)} %bitcast.160), kind=kOutput, calls=%fused_computation.1 | convolution fusion | flops 3627024384 | bytes 11894784 | tf_op jit(solution)/shard_map/dot_general | solution.py:361
  300.0 7.1 %fusion.54 = f32[768,576]{0,1:T(8,128)} fusion(bf16[576,4096]{1,0:T(8,128)(2,1)S(1)} %copy-done.4, bf16[4096,768]{1,0:T(8,128)(2,1)} %get-tuple-element.190), kind=kOutput, calls=%fused_computation.185 | convolution fusion | flops 3623878656 | bytes 12779520 | tf_op jit(solution)/shard_map/dot_general | solution.py:361
  309.2 11.1 %collective-permute-done.19 = bf16[24,3840]{1,0:T(8,128)(2,1)S(1)} collective-permute-done((bf16[24,3840]{1,0:T(8,128)(2,1)S(1)}, bf16[24,3840]{1,0:T(8,128)(2,1)S(1)}, u32[]{:S(2)}, u32[]{:S(2)}) %collective-permute-start.19) | collective-permute-done | bytes 184352 | tf_op jit(solution)/shard_map/ppermute | solution.py:789
  320.3 2.8 collective-permute-done.18
  323.8 2.9 multiply_reduce_fusion.1
  329.9 1.8 collective-permute-start.27
  336.5 5.1 %fusion.53 = f32[512,768]{1,0:T(8,128)S(1)} fusion(bf16[512,3072]{1,0:T(8,128)(2,1)S(1)} %copy-done.54, bf16[3072,768]{1,0:T(8,128)(2,1)} %get-tuple-element.164), kind=kOutput, calls=%fused_computation.184 | convolution fusion | flops 2415919104 | bytes 9437184 | tf_op jit(solution)/shard_map/dot_general | solution.py:361
  343.1 2.8 multiply_reduce_fusion.2
  346.6 2.0 collective-permute-done.22
  348.7 5.0 %collective-permute-done.24 = bf16[4,24,1472]{2,1,0:T(8,128)(2,1)S(1)} collective-permute-done((bf16[4,24,1472]{2,1,0:T(8,128)(2,1)S(1)}, bf16[4,24,1472]{2,1,0:T(8,128)(2,1)S(1)}, u32[]{:S(2)}, u32[]{:S(2)}) %collective-permute-start.24) | collective-permute-done | bytes 282656 | tf_op jit(solution)/shard_map/ppermute | solution.py:793
  354.2 1.8 collective-permute-start.38
  360.0 2.8 collective-permute-done.29
  363.8 2.6 collective-permute-done.30
  366.4 2.6 collective-permute-start.31
  370.7 4.1 %collective-permute-start.32 = (f32[5]{0:T(128)S(1)}, f32[5]{0:T(128)S(1)}, u32[]{:S(2)}, u32[]{:S(2)}) collective-permute-start(f32[5]{0:T(128)S(1)} %add.305), channel_id=1, source_target_pairs={{0,4},{1,5},{2,6},{3,7},{4,0},{5,1},{6,2},{7,3},{8,12},{9,13},{10,... | collective-permute-start | bytes 68 | tf_op jit(solution)/shard_map/ppermute | solution.py:1292
  376.3 2.9 collective-permute-start.34
  379.2 2.1 collective-permute-start.33
  382.3 2.7 collective-permute-done.33
  385.4 1.8 collective-permute-start.41
  388.9 2.3 collective-permute-done.41.refs_7_
  393.8 3.5 unpack.1
  400.4 2.0 slice_reduce_fusion
  402.4 1.8 fusion.9
  404.3 1.7 fusion.7
  (322 shorter events, 71.2 us)
Async XLA Ops:
  7.2 76.6 %all-gather.3.cloned.1.call-start = ((), (), s32[]{:S(2)}) async-start(), calls=%async_computation.4 | async-start | bytes 7077888 | tf_op jit(solution)/shard_map/all_gather | solution.py:1127
  7.9 162.3 %all-gather.5.cloned.1.call-start = ((), (), s32[]{:S(2)}) async-start(), calls=%async_computation.5 | async-start | bytes 5308416 | tf_op jit(solution)/shard_map/all_gather | solution.py:1179
  13.0 9.9 %collective-permute-start = (bf16[104,576]{0,1:T(8,128)(2,1)S(1)}, bf16[104,576]{0,1:T(8,128)(2,1)S(1)}, u32[]{:S(2)}, u32[]{:S(2)}) collective-permute-start(bf16[104,576]{0,1:T(8,128)(2,1)S(1)} %get-tuple-element.277), channel_id=1, source_target_pairs={{0,2},{1,3},{2,4},{3,5},{4,6},{5,7},{6,0},{7,1},{8,10},{9,11},{10,... | collective-permute-start | bytes 359432 | tf_op jit(solution)/shard_map/ppermute | solution.py:789
  16.1 19.6 %collective-permute-start.1 = (bf16[104,576]{0,1:T(8,128)(2,1)S(1)}, bf16[104,576]{0,1:T(8,128)(2,1)S(1)}, u32[]{:S(2)}, u32[]{:S(2)}) collective-permute-start(bf16[104,576]{0,1:T(8,128)(2,1)S(1)} %get-tuple-element.278), channel_id=1, source_target_pairs={{0,4},{1,5},{2,6},{3,7},{4,0},{5,1},{6,2},{7,3},{8,12},{9,13},{10,... | collective-permute-start | bytes 359432 | tf_op jit(solution)/shard_map/ppermute | solution.py:789
  18.6 17.0 %collective-permute-start.2 = (bf16[104,576]{0,1:T(8,128)(2,1)S(1)}, bf16[104,576]{0,1:T(8,128)(2,1)S(1)}, u32[]{:S(2)}, u32[]{:S(2)}) collective-permute-start(bf16[104,576]{0,1:T(8,128)(2,1)S(1)} %get-tuple-element.279), channel_id=1, source_target_pairs={{0,6},{1,7},{2,0},{3,1},{4,2},{5,3},{6,4},{7,5},{8,14},{9,15},{10,... | collective-permute-start | bytes 359432 | tf_op jit(solution)/shard_map/ppermute | solution.py:789
  36.9 11.5 %collective-permute-start.3 = (bf16[4,104,576]{2,1,0:T(8,128)(2,1)}, bf16[4,104,576]{2,1,0:T(8,128)(2,1)}, u32[]{:S(2)}, u32[]{:S(2)}) collective-permute-start(bf16[4,104,576]{2,1,0:T(8,128)(2,1)} %copy.74), channel_id=1, source_target_pairs={{0,1},{1,0},{2,3},{3,2},{4,5},{5,4},{6,7},{7,6},{8,9},{9,8},{10,11... | collective-permute-start | bytes 1437704 | tf_op jit(solution)/shard_map/ppermute | solution.py:783
  83.8 16.9 %collective-permute-start.6 = (bf16[128,768]{1,0:T(8,128)(2,1)S(1)}, bf16[128,768]{1,0:T(8,128)(2,1)S(1)}, u32[]{:S(2)}, u32[]{:S(2)}) collective-permute-start(bf16[128,768]{1,0:T(8,128)(2,1)S(1)} %fusion.24), channel_id=1, source_target_pairs={{0,6},{1,7},{2,0},{3,1},{4,2},{5,3},{6,4},{7,5},{8,14},{9,15},{10,... | collective-permute-start | bytes 589832 | tf_op jit(solution)/shard_map/ppermute | solution.py:789
  85.6 16.1 %collective-permute-start.5 = (bf16[128,768]{1,0:T(8,128)(2,1)S(1)}, bf16[128,768]{1,0:T(8,128)(2,1)S(1)}, u32[]{:S(2)}, u32[]{:S(2)}) collective-permute-start(bf16[128,768]{1,0:T(8,128)(2,1)S(1)} %fusion.24), channel_id=1, source_target_pairs={{0,4},{1,5},{2,6},{3,7},{4,0},{5,1},{6,2},{7,3},{8,12},{9,13},{10,... | collective-permute-start | bytes 589832 | tf_op jit(solution)/shard_map/ppermute | solution.py:789
  85.6 16.1 %collective-permute-start.4 = (bf16[128,768]{1,0:T(8,128)(2,1)S(1)}, bf16[128,768]{1,0:T(8,128)(2,1)S(1)}, u32[]{:S(2)}, u32[]{:S(2)}) collective-permute-start(bf16[128,768]{1,0:T(8,128)(2,1)S(1)} %fusion.24), channel_id=1, source_target_pairs={{0,2},{1,3},{2,4},{3,5},{4,6},{5,7},{6,0},{7,1},{8,10},{9,11},{10,... | collective-permute-start | bytes 589832 | tf_op jit(solution)/shard_map/ppermute | solution.py:789
  101.9 29.6 %collective-permute-start.9 = (bf16[4,128,768]{2,1,0:T(8,128)(2,1)S(1)}, bf16[4,128,768]{2,1,0:T(8,128)(2,1)S(1)}, u32[]{:S(2)}, u32[]{:S(2)}) collective-permute-start(bf16[4,128,768]{2,1,0:T(8,128)(2,1)S(1)} %pad_maximum_fusion.refs_0_), channel_id=1, source_target_pairs={{0,24},{8,16},{16,8},{24,0},{1,25},{9,17},{17,9},{25,1},{2,26},{10... | collective-permute-start | bytes 2359304 | tf_op jit(solution)/shard_map/ppermute | solution.py:793
  104.4 33.9 %collective-permute-start.8 = (bf16[4,128,768]{2,1,0:T(8,128)(2,1)S(1)}, bf16[4,128,768]{2,1,0:T(8,128)(2,1)S(1)}, u32[]{:S(2)}, u32[]{:S(2)}) collective-permute-start(bf16[4,128,768]{2,1,0:T(8,128)(2,1)S(1)} %pad_maximum_fusion.refs_0_), channel_id=1, source_target_pairs={{0,16},{8,24},{16,0},{24,8},{1,17},{9,25},{17,1},{25,9},{2,18},{10... | collective-permute-start | bytes 2359304 | tf_op jit(solution)/shard_map/ppermute | solution.py:793
  104.9 33.6 %collective-permute-start.7 = (bf16[4,128,768]{2,1,0:T(8,128)(2,1)S(1)}, bf16[4,128,768]{2,1,0:T(8,128)(2,1)}, u32[]{:S(2)}, u32[]{:S(2)}) collective-permute-start(bf16[4,128,768]{2,1,0:T(8,128)(2,1)S(1)} %pad_maximum_fusion.refs_0_), channel_id=1, source_target_pairs={{0,8},{8,0},{16,24},{24,16},{1,9},{9,1},{17,25},{25,17},{2,10},{10... | collective-permute-start | bytes 2359304 | tf_op jit(solution)/shard_map/ppermute | solution.py:793
  138.5 9.4 %collective-permute-start.10 = (bf16[4,128,768]{2,1,0:T(8,128)(2,1)S(1)}, bf16[4,128,768]{2,1,0:T(8,128)(2,1)}, u32[]{:S(2)}, u32[]{:S(2)}) collective-permute-start(bf16[4,128,768]{2,1,0:T(8,128)(2,1)S(1)} %pad_maximum_fusion.refs_0_), channel_id=1, source_target_pairs={{0,1},{1,0},{2,3},{3,2},{4,5},{5,4},{6,7},{7,6},{8,9},{9,8},{10,11... | collective-permute-start | bytes 2359304 | tf_op jit(solution)/shard_map/ppermute | solution.py:783
  138.5 9.4 %collective-permute-start.11 = (bf16[4,128,768]{2,1,0:T(8,128)(2,1)}, bf16[4,128,768]{2,1,0:T(8,128)(2,1)}, u32[]{:S(2)}, u32[]{:S(2)}) collective-permute-start(bf16[4,128,768]{2,1,0:T(8,128)(2,1)} %collective-permute-done.7.refs_1_), channel_id=1, source_target_pairs={{0,1},{1,0},{2,3},{3,2},{4,5},{5,4},{6,7},{7,6},{8,9},{9,8},{10,11... | collective-permute-start | bytes 2359304 | tf_op jit(solution)/shard_map/ppermute | solution.py:783
  139.0 8.9 %collective-permute-start.12 = (bf16[4,128,768]{2,1,0:T(8,128)(2,1)S(1)}, bf16[4,128,768]{2,1,0:T(8,128)(2,1)}, u32[]{:S(2)}, u32[]{:S(2)}) collective-permute-start(bf16[4,128,768]{2,1,0:T(8,128)(2,1)S(1)} %collective-permute-done.8.refs_2_), channel_id=1, source_target_pairs={{0,1},{1,0},{2,3},{3,2},{4,5},{5,4},{6,7},{7,6},{8,9},{9,8},{10,11... | collective-permute-start | bytes 2359304 | tf_op jit(solution)/shard_map/ppermute | solution.py:783
  139.0 8.9 %collective-permute-start.13 = (bf16[4,128,768]{2,1,0:T(8,128)(2,1)S(1)}, bf16[4,128,768]{2,1,0:T(8,128)(2,1)}, u32[]{:S(2)}, u32[]{:S(2)}) collective-permute-start(bf16[4,128,768]{2,1,0:T(8,128)(2,1)S(1)} %collective-permute-done.9.refs_3_), channel_id=1, source_target_pairs={{0,1},{1,0},{2,3},{3,2},{4,5},{5,4},{6,7},{7,6},{8,9},{9,8},{10,11... | collective-permute-start | bytes 2359304 | tf_op jit(solution)/shard_map/ppermute | solution.py:783
  141.8 28.5 %all-to-all-start = ((bf16[8,192,256]{2,1,0:T(8,128)(2,1)}), bf16[8,192,256]{2,1,0:T(8,128)(2,1)S(1)}, u32[]{:S(2)}, u32[]{:S(2)}) async-start(bf16[8,192,256]{2,1,0:T(8,128)(2,1)} %get-tuple-element.159), calls=%async_computation | async-start | bytes 1572864 | tf_op jit(solution)/shard_map/all_to_all | solution.py:1185
  198.8 11.3 %collective-permute-start.14 = (bf16[4,96,3840]{2,1,0:T(8,128)(2,1)}, bf16[4,96,3840]{2,1,0:T(8,128)(2,1)S(1)}, u32[]{:S(2)}, u32[]{:S(2)}) collective-permute-start(bf16[4,96,3840]{2,1,0:T(8,128)(2,1)} %get-tuple-element.175), channel_id=1, source_target_pairs={{0,1},{1,0},{2,3},{3,2},{4,5},{5,4},{6,7},{7,6},{8,9},{9,8},{10,11... | collective-permute-start | bytes 8847368 | tf_op jit(solution)/shard_map/ppermute | solution.py:783
  198.9 25.2 %all-to-all-start.1 = ((bf16[8,192,256]{2,1,0:T(8,128)(2,1)}), bf16[8,192,256]{2,1,0:T(8,128)(2,1)}, u32[]{:S(2)}, u32[]{:S(2)}) async-start(bf16[8,192,256]{2,1,0:T(8,128)(2,1)} %get-tuple-element.170), calls=%async_computation.1 | async-start | bytes 1572864 | tf_op jit(solution)/shard_map/all_to_all | solution.py:1212
  203.1 93.1 %reduce-scatter.5.cloned.1.call-start = ((), (), s32[]{:S(2)}) async-start(), calls=%async_computation.7 | async-start | bytes 5308416 | tf_op jit(solution)/shard_map/reduce_scatter | solution.py:1221
  224.1 178.3 %reduce-scatter.3.cloned.1.call-start = ((), (), s32[]{:S(2)}) async-start(), calls=%async_computation.6 | async-start | bytes 7077888 | tf_op jit(solution)/shard_map/reduce_scatter | solution.py:1228
  237.2 47.4 %collective-permute-start.17 = (bf16[4,24,3840]{2,1,0:T(8,128)(2,1)S(1)}, bf16[4,24,3840]{2,1,0:T(8,128)(2,1)S(1)}, u32[]{:S(2)}, u32[]{:S(2)}) collective-permute-start(bf16[4,24,3840]{2,1,0:T(8,128)(2,1)S(1)} %get-tuple-element.263), channel_id=1, source_target_pairs={{0,24},{8,16},{16,8},{24,0},{1,25},{9,17},{17,9},{25,1},{2,26},{10... | collective-permute-start | bytes 2211848 | tf_op jit(solution)/shard_map/ppermute | solution.py:793
  239.4 45.2 %collective-permute-start.16 = (bf16[4,24,3840]{2,1,0:T(8,128)(2,1)S(1)}, bf16[4,24,3840]{2,1,0:T(8,128)(2,1)S(1)}, u32[]{:S(2)}, u32[]{:S(2)}) collective-permute-start(bf16[4,24,3840]{2,1,0:T(8,128)(2,1)S(1)} %get-tuple-element.264), channel_id=1, source_target_pairs={{0,16},{8,24},{16,0},{24,8},{1,17},{9,25},{17,1},{25,9},{2,18},{10... | collective-permute-start | bytes 2211848 | tf_op jit(solution)/shard_map/ppermute | solution.py:793
  240.1 44.5 %collective-permute-start.15 = (bf16[4,24,3840]{2,1,0:T(8,128)(2,1)S(1)}, bf16[4,24,3840]{2,1,0:T(8,128)(2,1)S(1)}, u32[]{:S(2)}, u32[]{:S(2)}) collective-permute-start(bf16[4,24,3840]{2,1,0:T(8,128)(2,1)S(1)} %get-tuple-element.265), channel_id=1, source_target_pairs={{0,8},{8,0},{16,24},{24,16},{1,9},{9,1},{17,25},{25,17},{2,10},{10... | collective-permute-start | bytes 2211848 | tf_op jit(solution)/shard_map/ppermute | solution.py:793
  297.9 11.3 %collective-permute-start.20 = (bf16[24,3840]{1,0:T(8,128)(2,1)S(1)}, bf16[24,3840]{1,0:T(8,128)(2,1)S(1)}, u32[]{:S(2)}, u32[]{:S(2)}) collective-permute-start(bf16[24,3840]{1,0:T(8,128)(2,1)S(1)} %get-tuple-element.280), channel_id=1, source_target_pairs={{0,6},{1,7},{2,0},{3,1},{4,2},{5,3},{6,4},{7,5},{8,14},{9,15},{10,... | collective-permute-start | bytes 552968 | tf_op jit(solution)/shard_map/ppermute | solution.py:789
  299.2 21.1 %collective-permute-start.19 = (bf16[24,3840]{1,0:T(8,128)(2,1)S(1)}, bf16[24,3840]{1,0:T(8,128)(2,1)S(1)}, u32[]{:S(2)}, u32[]{:S(2)}) collective-permute-start(bf16[24,3840]{1,0:T(8,128)(2,1)S(1)} %get-tuple-element.281), channel_id=1, source_target_pairs={{0,4},{1,5},{2,6},{3,7},{4,0},{5,1},{6,2},{7,3},{8,12},{9,13},{10,... | collective-permute-start | bytes 552968 | tf_op jit(solution)/shard_map/ppermute | solution.py:789
  299.2 23.9 %collective-permute-start.18 = (bf16[24,3840]{1,0:T(8,128)(2,1)S(1)}, bf16[24,3840]{1,0:T(8,128)(2,1)S(1)}, u32[]{:S(2)}, u32[]{:S(2)}) collective-permute-start(bf16[24,3840]{1,0:T(8,128)(2,1)S(1)} %get-tuple-element.282), channel_id=1, source_target_pairs={{0,2},{1,3},{2,4},{3,5},{4,6},{5,7},{6,0},{7,1},{8,10},{9,11},{10,... | collective-permute-start | bytes 552968 | tf_op jit(solution)/shard_map/ppermute | solution.py:789
  328.8 4.6 %collective-permute-start.21 = (bf16[4,96,704]{2,1,0:T(8,128)(2,1)S(1)}, bf16[4,96,704]{2,1,0:T(8,128)(2,1)S(1)}, u32[]{:S(2)}, u32[]{:S(2)}) collective-permute-start(bf16[4,96,704]{2,1,0:T(8,128)(2,1)S(1)} %fusion.15), channel_id=1, source_target_pairs={{0,1},{1,0},{2,3},{3,2},{4,5},{5,4},{6,7},{7,6},{8,9},{9,8},{10,11... | collective-permute-start | bytes 1622024 | tf_op jit(solution)/shard_map/ppermute | solution.py:783
  329.9 11.8 %collective-permute-start.27 = (bf16[24,3840]{1,0:T(8,128)(2,1)S(1)}, bf16[24,3840]{1,0:T(8,128)(2,1)S(1)}, u32[]{:S(2)}, u32[]{:S(2)}) collective-permute-start(bf16[24,3840]{1,0:T(8,128)(2,1)S(1)} %add_convert_fusion.2.refs_0_), channel_id=1, source_target_pairs={{0,24},{8,16},{16,8},{24,0},{1,25},{9,17},{17,9},{25,1},{2,26},{10... | collective-permute-start | bytes 552968 | tf_op jit(solution)/shard_map/ppermute | solution.py:793
  331.7 14.8 %collective-permute-start.26 = (bf16[24,3840]{1,0:T(8,128)(2,1)S(1)}, bf16[24,3840]{1,0:T(8,128)(2,1)S(1)}, u32[]{:S(2)}, u32[]{:S(2)}) collective-permute-start(bf16[24,3840]{1,0:T(8,128)(2,1)S(1)} %add_convert_fusion.2.refs_0_), channel_id=1, source_target_pairs={{0,16},{8,24},{16,0},{24,8},{1,17},{9,25},{17,1},{25,9},{2,18},{10... | collective-permute-start | bytes 552968 | tf_op jit(solution)/shard_map/ppermute | solution.py:793
  332.6 14.0 %collective-permute-start.25 = (bf16[24,3840]{1,0:T(8,128)(2,1)S(1)}, bf16[24,3840]{1,0:T(8,128)(2,1)S(1)}, u32[]{:S(2)}, u32[]{:S(2)}) collective-permute-start(bf16[24,3840]{1,0:T(8,128)(2,1)S(1)} %add_convert_fusion.2.refs_0_), channel_id=1, source_target_pairs={{0,8},{8,0},{16,24},{24,16},{1,9},{9,1},{17,25},{25,17},{2,10},{10... | collective-permute-start | bytes 552968 | tf_op jit(solution)/shard_map/ppermute | solution.py:793
  333.9 14.7 %collective-permute-start.22 = (bf16[4,24,1472]{2,1,0:T(8,128)(2,1)S(1)}, bf16[4,24,1472]{2,1,0:T(8,128)(2,1)S(1)}, u32[]{:S(2)}, u32[]{:S(2)}) collective-permute-start(bf16[4,24,1472]{2,1,0:T(8,128)(2,1)S(1)} %pad_maximum_fusion.2), channel_id=1, source_target_pairs={{0,8},{8,0},{16,24},{24,16},{1,9},{9,1},{17,25},{25,17},{2,10},{10... | collective-permute-start | bytes 847880 | tf_op jit(solution)/shard_map/ppermute | solution.py:793
  335.2 13.5 %collective-permute-start.23 = (bf16[4,24,1472]{2,1,0:T(8,128)(2,1)S(1)}, bf16[4,24,1472]{2,1,0:T(8,128)(2,1)S(1)}, u32[]{:S(2)}, u32[]{:S(2)}) collective-permute-start(bf16[4,24,1472]{2,1,0:T(8,128)(2,1)S(1)} %pad_maximum_fusion.3), channel_id=1, source_target_pairs={{0,16},{8,24},{16,0},{24,8},{1,17},{9,25},{17,1},{25,9},{2,18},{10... | collective-permute-start | bytes 847880 | tf_op jit(solution)/shard_map/ppermute | solution.py:793
  341.7 12.0 %collective-permute-start.24 = (bf16[4,24,1472]{2,1,0:T(8,128)(2,1)S(1)}, bf16[4,24,1472]{2,1,0:T(8,128)(2,1)S(1)}, u32[]{:S(2)}, u32[]{:S(2)}) collective-permute-start(bf16[4,24,1472]{2,1,0:T(8,128)(2,1)S(1)} %pad_maximum_fusion.4), channel_id=1, source_target_pairs={{0,24},{8,16},{16,8},{24,0},{1,25},{9,17},{17,9},{25,1},{2,26},{10... | collective-permute-start | bytes 847880 | tf_op jit(solution)/shard_map/ppermute | solution.py:793
  353.8 25.4 %collective-permute-start.35 = (bf16[24,704]{1,0:T(8,128)(2,1)S(1)}, bf16[24,704]{1,0:T(8,128)(2,1)S(1)}, u32[]{:S(2)}, u32[]{:S(2)}) collective-permute-start(bf16[24,704]{1,0:T(8,128)(2,1)S(1)} %get-tuple-element.298), channel_id=1, source_target_pairs={{0,6},{1,7},{2,0},{3,1},{4,2},{5,3},{6,4},{7,5},{8,14},{9,15},{10,... | collective-permute-start | bytes 101384 | tf_op jit(solution)/shard_map/ppermute | solution.py:789
  354.2 30.8 %collective-permute-start.38 = (bf16[24,3072]{1,0:T(8,128)(2,1)S(1)}, bf16[24,3072]{1,0:T(8,128)(2,1)S(1)}, u32[]{:S(2)}, u32[]{:S(2)}) collective-permute-start(bf16[24,3072]{1,0:T(8,128)(2,1)S(1)} %pad_maximum_fusion.5.refs_8_), channel_id=1, source_target_pairs={{0,24},{8,16},{16,8},{24,0},{1,25},{9,17},{17,9},{25,1},{2,26},{10... | collective-permute-start | bytes 442376 | tf_op jit(solution)/shard_map/ppermute | solution.py:793
  356.0 29.0 %collective-permute-start.37 = (bf16[24,3072]{1,0:T(8,128)(2,1)S(1)}, bf16[24,3072]{1,0:T(8,128)(2,1)S(1)}, u32[]{:S(2)}, u32[]{:S(2)}) collective-permute-start(bf16[24,3072]{1,0:T(8,128)(2,1)S(1)} %pad_maximum_fusion.5.refs_8_), channel_id=1, source_target_pairs={{0,16},{8,24},{16,0},{24,8},{1,17},{9,25},{17,1},{25,9},{2,18},{10... | collective-permute-start | bytes 442376 | tf_op jit(solution)/shard_map/ppermute | solution.py:793
  356.8 28.2 %collective-permute-start.36 = (bf16[24,3072]{1,0:T(8,128)(2,1)S(1)}, bf16[24,3072]{1,0:T(8,128)(2,1)S(1)}, u32[]{:S(2)}, u32[]{:S(2)}) collective-permute-start(bf16[24,3072]{1,0:T(8,128)(2,1)S(1)} %pad_maximum_fusion.5.refs_8_), channel_id=1, source_target_pairs={{0,8},{8,0},{16,24},{24,16},{1,9},{9,1},{17,25},{25,17},{2,10},{10... | collective-permute-start | bytes 442376 | tf_op jit(solution)/shard_map/ppermute | solution.py:793
  357.7 1.1 collective-permute-start.28
  358.9 4.0 collective-permute-start.29
  362.8 3.5 collective-permute-start.30
  366.4 4.3 %collective-permute-start.31 = (f32[5]{0:T(128)S(1)}, f32[5]{0:T(128)S(1)}, u32[]{:S(2)}, u32[]{:S(2)}) collective-permute-start(f32[5]{0:T(128)S(1)} %add.304), channel_id=1, source_target_pairs={{0,2},{1,3},{2,0},{3,1},{4,6},{5,7},{6,4},{7,5},{8,10},{9,11},{10,... | collective-permute-start | bytes 68 | tf_op jit(solution)/shard_map/ppermute | solution.py:1291
  370.7 5.7 %collective-permute-start.32 = (f32[5]{0:T(128)S(1)}, f32[5]{0:T(128)S(1)}, u32[]{:S(2)}, u32[]{:S(2)}) collective-permute-start(f32[5]{0:T(128)S(1)} %add.305), channel_id=1, source_target_pairs={{0,4},{1,5},{2,6},{3,7},{4,0},{5,1},{6,2},{7,3},{8,12},{9,13},{10,... | collective-permute-start | bytes 68 | tf_op jit(solution)/shard_map/ppermute | solution.py:1292
  376.3 5.9 %collective-permute-start.34 = (bf16[24,704]{1,0:T(8,128)(2,1)S(1)}, bf16[24,704]{1,0:T(8,128)(2,1)S(1)}, u32[]{:S(2)}, u32[]{:S(2)}) collective-permute-start(bf16[24,704]{1,0:T(8,128)(2,1)S(1)} %get-tuple-element.299), channel_id=1, source_target_pairs={{0,4},{1,5},{2,6},{3,7},{4,0},{5,1},{6,2},{7,3},{8,12},{9,13},{10,... | collective-permute-start | bytes 101384 | tf_op jit(solution)/shard_map/ppermute | solution.py:789
  379.2 5.8 %collective-permute-start.33 = (bf16[24,704]{1,0:T(8,128)(2,1)S(1)}, bf16[24,704]{1,0:T(8,128)(2,1)S(1)}, u32[]{:S(2)}, u32[]{:S(2)}) collective-permute-start(bf16[24,704]{1,0:T(8,128)(2,1)S(1)} %get-tuple-element.300), channel_id=1, source_target_pairs={{0,2},{1,3},{2,4},{3,5},{4,6},{5,7},{6,0},{7,1},{8,10},{9,11},{10,... | collective-permute-start | bytes 101384 | tf_op jit(solution)/shard_map/ppermute | solution.py:789
  385.4 5.8 %collective-permute-start.41 = (bf16[24,2432]{1,0:T(8,128)(2,1)S(1)}, bf16[24,2432]{1,0:T(8,128)(2,1)S(1)}, u32[]{:S(2)}, u32[]{:S(2)}) collective-permute-start(bf16[24,2432]{1,0:T(8,128)(2,1)S(1)} %concatenate.87.refs_4_), channel_id=1, source_target_pairs={{0,24},{8,16},{16,8},{24,0},{1,25},{9,17},{17,9},{25,1},{2,26},{10... | collective-permute-start | bytes 350216 | tf_op jit(solution)/shard_map/ppermute | solution.py:793
  387.1 5.3 %collective-permute-start.40 = (bf16[24,2432]{1,0:T(8,128)(2,1)S(1)}, bf16[24,2432]{1,0:T(8,128)(2,1)S(1)}, u32[]{:S(2)}, u32[]{:S(2)}) collective-permute-start(bf16[24,2432]{1,0:T(8,128)(2,1)S(1)} %concatenate.87.refs_4_), channel_id=1, source_target_pairs={{0,16},{8,24},{16,0},{24,8},{1,17},{9,25},{17,1},{25,9},{2,18},{10... | collective-permute-start | bytes 350216 | tf_op jit(solution)/shard_map/ppermute | solution.py:793
  388.2 4.8 %collective-permute-start.39 = (bf16[24,2432]{1,0:T(8,128)(2,1)S(1)}, bf16[24,2432]{1,0:T(8,128)(2,1)S(1)}, u32[]{:S(2)}, u32[]{:S(2)}) collective-permute-start(bf16[24,2432]{1,0:T(8,128)(2,1)S(1)} %concatenate.87.refs_4_), channel_id=1, source_target_pairs={{0,8},{8,0},{16,24},{24,16},{1,9},{9,1},{17,25},{25,17},{2,10},{10... | collective-permute-start | bytes 350216 | tf_op jit(solution)/shard_map/ppermute | solution.py:793
  (55 other events, 549.4 us)
Sparse Core Ops, SparseCore 0:
  9.7 74.0 all-gather.2
  102.0 54.9 all-gather.4
  224.3 53.6 reduce-scatter.4
  294.4 77.6 reduce-scatter.2
where the time goes:
time: 414 us; the launch traced here: 413 us
  Pallas kernels  131 us (32%)
  waiting for transfers between devices  98.6 us (24%)
  starting transfers between devices  70.8 us (17%)
  matrix products  35.7 us (9%)
  other arithmetic  31.8 us (8%)
  local copies, waits for them, and re-layouts  29.4 us (7%)
  between operations  15.1 us (4%)
    pallas_call x1, Pallas kernels, retrace(): pl.pallas_call(retrace_kernel, name='retrace', cost_estimate=cost(5 * 2 *...  43.9 us
    dot_general x5, matrix products, contract(): lax.dot_general(left, right, (((left_dim,), (right_dim,)), ((), ())), pre...  35.7 us
    ppermute x12, waiting for transfers between devices, shift_owner(): lax.ppermute(value, 'shard', [(i, (i + step) % groups) for i in range(gro...  30.7 us
    all_gather x1, waiting for transfers between devices, head_split_device(): tokens = lax.all_gather(block_in, 'shard', axis=0, tiled=True)  27.9 us
    pallas_call x1, Pallas kernels, attend(): pl.pallas_call(attend_kernel, name='attend', cost_estimate=cost(2 * 2 * B...  26 us
    ppermute x20, waiting for transfers between devices, cross_rep(): lax.ppermute(value, 'rep', [(i, i ^ mask) for i in range(lax.axis_size('r...  23.7 us
    ppermute x20, starting transfers between devices, cross_rep(): lax.ppermute(value, 'rep', [(i, i ^ mask) for i in range(lax.axis_size('r...  23.6 us
    pallas_call x1, Pallas kernels, middle_part(): pl.pallas_call(middle_kernel, name='middle', cost_estimate=cost(4 * rows...  19.2 us
  transfers between devices with their start and end apart: 48, of which 22 were waited for; matrix products, arithmetic and copies ran while one was open for 21% of the time, Pallas kernels for 25%

commit v1 on v0

--- a/solution.py
+++ b/solution.py
@@ -363,10 +363,8 @@
     )
 
 
-def qkv_kernel(
-    x_ref, weight_ref, bias_ref, gain_ref, shift_ref, cos_ref, sin_ref,
-    plain_ref, qt_ref, kt_ref, vt_ref, kv_ref,
-):
+def qkv_kernel(x_ref, weight_ref, bias_ref, gain_ref, shift_ref, cos_ref, sin_ref, *refs):
+    plain_ref, qt_ref, kt_ref, vt_ref, kv_ref = refs[-5:]
     x = x_ref[...].astype(F32)
     center = x - jnp.mean(x, axis=-1, keepdims=True)
     spread = jnp.mean(center * center, axis=-1, keepdims=True)
@@ -398,7 +396,7 @@
         kv_ref[head] = jnp.transpose(jnp.concatenate([key, value], axis=0)).astype(BF16)
 
 
-def project(tokens, weight_t, bias, gain, shift, cosine, sine):
+def project(tokens, weight_t, bias, gain, shift, cosine, sine, first, count, held):
     length, model_width = tokens.shape
     columns = weight_t.shape[0]
     width = columns // 3
@@ -406,27 +404,30 @@
     half = HEAD_DIM // 2
     tile = CHUNK
     fixed = lambda i: (0, 0)
-    across = lambda i: (0, i)
+    down = lambda i: (first + i, 0)
+    across = lambda i: (0, first + i)
+    inputs = [tokens, weight_t, bias, gain, shift, cosine, sine]
     return pl.pallas_call(
         qkv_kernel,
         name="project",
-        cost_estimate=cost(2 * length * model_width * columns, 12 * length * model_width),
-        grid=(length // tile,),
+        cost_estimate=cost(2 * count * tile * model_width * columns, 12 * count * tile * model_width),
+        grid=(count,),
         in_specs=[
-            pl.BlockSpec((tile, model_width), lambda i: (i, 0)),
+            pl.BlockSpec((tile, model_width), down),
             pl.BlockSpec((columns, model_width), fixed),
             pl.BlockSpec((columns, 1), fixed),
             pl.BlockSpec((1, model_width), fixed),
             pl.BlockSpec((1, model_width), fixed),
             pl.BlockSpec((half, tile), across),
             pl.BlockSpec((half, tile), across),
-        ],
+        ]
+        + [pl.BlockSpec(memory_space=pl.ANY)] * len(held),
         out_specs=[
-            pl.BlockSpec((tile, model_width), lambda i: (i, 0)),
+            pl.BlockSpec((tile, model_width), down),
             pl.BlockSpec((width, tile), across),
             pl.BlockSpec((width, tile), across),
             pl.BlockSpec((width, tile), across),
-            pl.BlockSpec((heads, tile, 2 * HEAD_DIM), lambda i: (0, i, 0)),
+            pl.BlockSpec((heads, tile, 2 * HEAD_DIM), lambda i: (0, first + i, 0)),
         ],
         out_shape=[
             jax.ShapeDtypeStruct((length, model_width), BF16),
@@ -435,8 +436,9 @@
             jax.ShapeDtypeStruct((width, length), BF16),
             jax.ShapeDtypeStruct((heads, length, 2 * HEAD_DIM), BF16),
         ],
+        input_output_aliases={len(inputs) + i: i for i in range(len(held))},
         compiler_params=pltpu.CompilerParams(vmem_limit_bytes=VMEM_LIMIT),
-    )(tokens, weight_t, bias, gain, shift, cosine, sine)
+    )(*inputs, *held)
 
 
 def average_kernel(weights_ref, earlier_ref, cotangent_ref, grad_ref, mix_ref, sums_ref):
@@ -592,7 +594,7 @@
 
 def retrace_kernel(
     core_ref, qt_ref, grad_ref, full_ref, stat_ref, cos_ref, sin_ref, kv_ref, kt_ref,
-    joint_ref, dkv_ref,
+    weight_ref, joint_ref, normed_ref, dkv_ref,
 ):
     step_id = pl.program_id(0)
     pair = pl.num_programs(0) - 1 - step_id
@@ -670,9 +672,10 @@
             joint_ref[start : start + HEAD_DIM, :] = turned.astype(BF16)
         start = 2 * width + base
         joint_ref[start : start + HEAD_DIM, :] = turned_back[HEAD_DIM:].astype(BF16)
-
-
-def retrace(core, qt, grads, full, stats, cosine, sine, kv, kt):
+    normed_ref[...] = contract(joint_ref[...], weight_ref[...], 0, 0).astype(BF16)
+
+
+def retrace(core, qt, grads, full, stats, cosine, sine, kv, kt, weight):
     width, length = qt.shape
     heads = width // HEAD_DIM
     half = HEAD_DIM // 2
@@ -701,13 +704,20 @@
                 pl.BlockSpec((half, CHUNK), across),
                 pl.BlockSpec(kv.shape, lambda j, core: (0, 0, 0)),
                 pl.BlockSpec(kt.shape, lambda j, core: (0, 0)),
+                pl.BlockSpec(weight.shape, lambda j, core: (0, 0)),
             ],
-            out_specs=pl.BlockSpec((3 * width, CHUNK), across),
+            out_specs=[
+                pl.BlockSpec((3 * width, CHUNK), across),
+                pl.BlockSpec((CHUNK, weight.shape[1]), lambda j, core: (back(j), 0)),
+            ],
             scratch_shapes=[pltpu.VMEM((heads, length, 2 * HEAD_DIM), F32)],
         ),
-        out_shape=jax.ShapeDtypeStruct((3 * width, length), BF16),
+        out_shape=[
+            jax.ShapeDtypeStruct((3 * width, length), BF16),
+            jax.ShapeDtypeStruct((length, weight.shape[1]), BF16),
+        ],
         compiler_params=pltpu.CompilerParams(vmem_limit_bytes=VMEM_LIMIT),
-    )(core, qt, grads, full, stats, cosine, sine, kv, kt)
+    )(core, qt, grads, full, stats, cosine, sine, kv, kt, weight)
 
 
 def after(values, *earlier_values):
@@ -716,9 +726,9 @@
 
 
 def assemble_kernel(place_ref, *refs):
-    down_ref, out_ref, late_ref = refs[-3:]
+    down_ref, out_ref = refs[-2:]
     rep = place_ref[1]
-    reps = (len(refs) - 3) // 2
+    reps = (len(refs) - 2) // 2
     part = out_ref.shape[0]
     for side in range(2):
         @pl.when(pl.program_id(0) == side)
@@ -735,7 +745,6 @@
                 @pl.when(target == reps - 1)
                 def _():
                     out_ref[...] = piece[0, :part]
-                    late_ref[0] = piece[0, part : part + 8]
 
 
 def assemble(place, mine, twin, part):
@@ -756,7 +765,6 @@
     return pl.pallas_call(
         assemble_kernel,
         name="assemble",
-        cost_estimate=cost(0, 4 * 2 * reps * owners * rows * columns),
         grid_spec=pltpu.PrefetchScalarGridSpec(
             num_scalar_prefetch=1,
             grid=(2, owners),
@@ -764,15 +772,11 @@
             out_specs=[
                 pl.BlockSpec(((reps - 1) * rows, columns), target),
                 pl.BlockSpec((part, columns), target),
-                pl.BlockSpec(
-                    (1, 8, columns), lambda which, z, place: (device(which, z, place), 0, 0)
-                ),
             ],
         ),
         out_shape=[
             jax.ShapeDtypeStruct((groups * (reps - 1) * rows, columns), BF16),
             jax.ShapeDtypeStruct((groups * part, columns), BF16),
-            jax.ShapeDtypeStruct((groups, 8, columns), BF16),
         ],
         compiler_params=pltpu.CompilerParams(vmem_limit_bytes=VMEM_LIMIT),
     )(place, *mine, *twin)
@@ -833,9 +837,10 @@
 
 
 def unpack_kernel(rep_ref, *refs):
-    in_ref, out_ref, qkv_ref, small_ref, down_ref = refs[-5:]
-    pieces = refs[:-5]
-    reps = len(pieces) // 3
+    reps = 4
+    pieces = refs[: 3 * reps]
+    in_ref, out_ref, qkv_ref, down_ref = refs[3 * reps : 3 * reps + 4]
+    line_refs = refs[3 * reps + 4 :]
     hidden_width = in_ref.shape[1]
     model_width = out_ref.shape[1]
     columns = qkv_ref.shape[1] // 3
@@ -857,13 +862,25 @@
                 ],
                 axis=1,
             )
-        small_ref[own, :] = joint[:, 3 * columns :].astype(F32)
+
+        @pl.when(rep_ref[0] == k)
+        def _():
+            part = line_refs[0].shape[1] // 2
+            lines = joint[:, 3 * columns :].astype(F32)
+            row = 0
+            for line_ref in line_refs:
+                count = line_ref.shape[1] // part
+                line_ref[...] = jnp.concatenate(
+                    [lines[row + i : row + i + 1, :part] for i in range(count)], axis=1
+                )
+                row += count
+
         for z in range(owners):
             block = pl.ds(pl.multiple_of(owners * first + z * rows, 8), rows)
             down_ref[block, :] = down[:, z * model_width : (z + 1) * model_width].astype(F32)
 
 
-def unpack(rep, pair, joint, down, widths):
+def unpack(rep, pair, joint, down, widths, counts):
     hidden_width, model_width, columns = widths
     pieces = [*pair, *joint, *down]
     rows = len(pair) * pair[0].shape[0]
@@ -872,19 +889,36 @@
         (rows, hidden_width),
         (rows, model_width),
         (rows, 3 * model_width),
-        (rows, 128),
         (owners * rows, model_width),
-    ]
+    ] + [(1, count * rows) for count in counts]
     whole = pl.BlockSpec(memory_space=pltpu.VMEM)
     return pl.pallas_call(
         unpack_kernel,
         name="unpack",
-        cost_estimate=cost(0, 6 * sum(a * b for a, b in shapes)),
         in_specs=[pl.BlockSpec(memory_space=pltpu.SMEM)] + [whole] * len(pieces),
-        out_specs=[whole] * 5,
+        out_specs=[whole] * len(shapes),
         out_shape=[jax.ShapeDtypeStruct(shape, F32) for shape in shapes],
         compiler_params=pltpu.CompilerParams(vmem_limit_bytes=VMEM_LIMIT),
     )(rep, *pieces)
+
+
+def split_depth(value):
+    high = lax.reduce_precision(value, 8, 7)
+    return jnp.concatenate([high, value - high]).astype(BF16)
+
+
+def join_depth(value):
+    value = value.astype(F32)
+    half = value.shape[0] // 2
+    return value[:half] + value[half:]
+
+
+def add_ordered(values, index_of):
+    stacked = jnp.stack(values)
+    total = pick(stacked, index_of(0))
+    for sender in range(1, len(values)):
+        total = total + pick(stacked, index_of(sender))
+    return total
 
 
 def every_rep(value):
@@ -935,7 +969,7 @@
     share = 0.5 + 0.5 * turned
     active_ref[...] = (hidden * share).astype(BF16)
     slope = (0.5 * hidden) * (1.0 - turned * turned) * (bend + (3 * bend * 0.044715) * square)
-    grad = (grad_ref[...] * (share + slope)).astype(BF16)
+    grad = (grad_ref[...].astype(F32) * (share + slope)).astype(BF16)
     hidden_ref[...] = grad
     hidden_sums_ref[...] = jnp.sum(grad.astype(F32), axis=0, keepdims=True)
     back_ref[...] += contract(grad, w_in_ref[...], 1, 1)
@@ -1027,61 +1061,163 @@
     )
 
 
-def pair_kernel(core_ref, low_ref, hidden_ref, mixed_ref, branch_ref, own_ref, other_ref, full_ref):
+def weight_kernel(
+    core_ref, weights_ref, low_ref, hidden_ref, mixed_ref, branch_ref, active_ref, down_grad_ref,
+    w_down_ref, b_down_ref, middle_ref, mix_ref, cotangent_ref,
+    own_ref, other_ref, down_ref, layer_ref, depth_ref, full_ref, turned_ref, total_ref,
+):
     step = pl.program_id(0)
     core = core_ref[0]
     owners, part, _ = own_ref.shape
 
+    @pl.when(step == 0)
+    def _():
+        turned_ref[...] = jnp.transpose(low_ref[...].astype(F32)).astype(BF16)
+        total_ref[...] = middle_ref[...] + b_down_ref[...]
+
     @pl.when(step < pl.num_programs(0) - 1)
     def _():
-        full_ref[...] = contract(low_ref[...], hidden_ref[...], 0, 0)
+        full_ref[...] = contract(turned_ref[...], hidden_ref[...], 1, 0).astype(BF16)
+        total_ref[...] += contract(active_ref[...], w_down_ref[...], 1, 0)
+        down_ref[...] = contract(active_ref[...], down_grad_ref[...], 0, 0).astype(BF16)
 
     @pl.when(step == pl.num_programs(0) - 1)
     def _():
+        product = 0.0
         for half in range(2):
             mixed = jnp.concatenate(
                 [mixed_ref[2 * z + (core ^ half)] for z in range(owners)], axis=0
             )
-            product = contract(mixed, branch_ref[half * BLOCK : (half + 1) * BLOCK, :], 1, 0)
-            if half == 0:
-                full_ref[...] = product
-            else:
-                full_ref[...] += product
+            rows = slice(half * BLOCK, (half + 1) * BLOCK)
+            product = product + contract(mixed, branch_ref[rows, :], 1, 0)
+        full_ref[...] = product.astype(BF16)
+        result = total_ref[...]
+        layer_ref[...] = weights_ref[4] * result + mix_ref[...]
+        depth = (result * cotangent_ref[...]).reshape(-1, 8, result.shape[1])
+        depth_ref[...] = jnp.sum(depth, axis=0)
 
     for z in range(owners):
         for side, ref in ((0, own_ref), (1, other_ref)):
             start = pl.multiple_of((2 * z + (core ^ side)) * part, part)
-            ref[z] = full_ref[pl.ds(start, part), :].astype(BF16)
-
-
-def pair_sums(core, low, hidden, mixed, branch):
+            ref[z] = full_ref[pl.ds(start, part), :]
+
+
+def weight_sums(
+    core, depth_weights, low, hidden, mixed, branch, active, down_grad, w_down, b_down, middle,
+    mix, cotangent,
+):
     rows, model_width = low.shape
     owners = mixed.shape[0] // 2
     part = model_width // (2 * owners)
     steps = hidden.shape[1] // model_width
+    whole = lambda value: pl.BlockSpec(value.shape, lambda j, *_: (0,) * value.ndim)
+    chunk = pl.BlockSpec((rows, model_width), lambda j, *_: (0, jnp.minimum(j, steps - 1)))
+    square = pl.BlockSpec(
+        (model_width, model_width), lambda j, *_: (jnp.minimum(j, steps - 1), 0)
+    )
+    target = pl.BlockSpec((owners, part, model_width), lambda j, *_: (0, 0, j))
+    shape = jax.ShapeDtypeStruct((owners, part, (steps + 1) * model_width), BF16)
+    depth = jax.ShapeDtypeStruct((8, model_width), F32)
+    return pl.pallas_call(
+        weight_kernel,
+        name="weight_sums",
+        grid_spec=pltpu.PrefetchScalarGridSpec(
+            num_scalar_prefetch=2,
+            grid=(steps + 1,),
+            in_specs=[
+                whole(low), chunk, whole(mixed), whole(branch), chunk, whole(down_grad),
+                square, whole(b_down), whole(middle), whole(mix), whole(cotangent),
+            ],
+            out_specs=[target, target, square, whole(middle), whole(depth)],
+            scratch_shapes=[
+                pltpu.VMEM((model_width, model_width), BF16),
+                pltpu.VMEM((model_width, rows), BF16),
+                pltpu.VMEM((rows, model_width), F32),
+            ],
+        ),
+        out_shape=[
+            shape,
+            shape,
+            jax.ShapeDtypeStruct((steps * model_width, model_width), BF16),
+            jax.ShapeDtypeStruct(middle.shape, F32),
+            depth,
+        ],
+        compiler_params=pltpu.CompilerParams(vmem_limit_bytes=VMEM_LIMIT),
+    )(
+        core, depth_weights, low, hidden, mixed, branch, active, down_grad, w_down, b_down,
+        middle, mix, cotangent,
+    )
+
+
+def joint_kernel(
+    core_ref, plain_ref, joint_ref, weight_ref, gain_ref, shift_ref,
+    own_ref, other_ref, sums_ref, lines_ref, product_ref, full_ref,
+):
+    step = pl.program_id(0)
+    core = core_ref[0]
+    owners, part, columns = own_ref.shape
+    joint = joint_ref[...]
+    product = contract(joint, plain_ref[...], 1, 0)
+    line = contract(jnp.ones((8, joint.shape[1]), BF16), joint, 1, 1)
+
+    @pl.when(step == 0)
+    def _():
+        product_ref[...] = product
+        lines_ref[...] = line
+
+    @pl.when(step > 0)
+    def _():
+        product_ref[...] += product
+        lines_ref[...] += line
+
+    @pl.when(step == pl.num_programs(0) - 1)
+    def _():
+        total = product_ref[...]
+        sums = jnp.transpose(lines_ref[...])[:, :1]
+        weight = weight_ref[...].astype(F32)
+        sums_ref[0:1, :] = jnp.sum(total * weight, axis=0, keepdims=True)
+        sums_ref[1:2, :] = jnp.sum(sums * weight, axis=0, keepdims=True)
+        full_ref[...] = jnp.transpose(gain_ref[...] * total + shift_ref[...] * sums).astype(BF16)
+        for z in range(owners):
+            for side, ref in ((0, own_ref), (1, other_ref)):
+                start = pl.multiple_of((2 * z + (core ^ side)) * part, part)
+                ref[z] = full_ref[pl.ds(start, part), :]
+
+
+def joint_part(core, plain, joint_t, weight_t, gain, shift):
+    length, model_width = plain.shape
+    columns = joint_t.shape[0]
+    owners = length // CHUNK // 2
+    part = model_width // (2 * owners)
     whole = lambda value: pl.BlockSpec(value.shape, lambda j, core: (0,) * value.ndim)
-    target = pl.BlockSpec((owners, part, model_width), lambda j, core: (0, 0, j))
-    shape = jax.ShapeDtypeStruct((owners, part, (steps + 1) * model_width), BF16)
+    shapes = [
+        jax.ShapeDtypeStruct((owners, part, columns), BF16),
+        jax.ShapeDtypeStruct((owners, part, columns), BF16),
+        jax.ShapeDtypeStruct((8, model_width), F32),
+        jax.ShapeDtypeStruct((8, columns), F32),
+    ]
     return pl.pallas_call(
-        pair_kernel,
-        name="pair_sums",
+        joint_kernel,
+        name="joint_part",
         grid_spec=pltpu.PrefetchScalarGridSpec(
             num_scalar_prefetch=1,
-            grid=(steps + 1,),
+            grid=(length // CHUNK,),
             in_specs=[
-                whole(low),
-                pl.BlockSpec(
-                    (rows, model_width), lambda j, core: (0, jnp.minimum(j, steps - 1))
-                ),
-                whole(mixed),
-                whole(branch),
+                pl.BlockSpec((CHUNK, model_width), lambda j, core: (j, 0)),
+                pl.BlockSpec((columns, CHUNK), lambda j, core: (0, j)),
+                whole(weight_t),
+                whole(gain),
+                whole(shift),
             ],
-            out_specs=[target, target],
-            scratch_shapes=[pltpu.VMEM((model_width, model_width), F32)],
+            out_specs=[whole(shape) for shape in shapes],
+            scratch_shapes=[
+                pltpu.VMEM((columns, model_width), F32),
+                pltpu.VMEM((model_width, columns), BF16),
+            ],
         ),
-        out_shape=[shape, shape],
+        out_shape=shapes,
         compiler_params=pltpu.CompilerParams(vmem_limit_bytes=VMEM_LIMIT),
-    )(core, low, hidden, mixed, branch)
+    )(core, plain, joint_t, weight_t, gain, shift)
 
 
 def head_split_device(
@@ -1117,8 +1253,16 @@
 
     pieces = qkv_weight.astype(BF16).reshape(part, 3, owners, width)
     pieces = jnp.transpose(pieces, (2, 0, 1, 3)).reshape(owners, part, 3 * width)
-    early = jnp.concatenate([qk_bias, value_bias, gain_one, shift_one]).astype(BF16)
-    early = jnp.pad(early, (0, 8 * 3 * width - early.shape[0])).reshape(8, 3 * width)
+    vectors = (
+        qk_bias, value_bias, gain_one, shift_one,
+        out_bias, in_bias, down_bias, gain_two, shift_two,
+    )
+    late = lax.optimization_barrier(jnp.concatenate(vectors))
+    early, late = late[: 5 * part], late[5 * part :]
+    half_late = late.shape[0] // 2
+    rows = [early, late[:half_late], late[half_late:]]
+    rows = jnp.stack([jnp.pad(row, (0, 3 * width - row.shape[0])) for row in rows])
+    early = jnp.pad(rows.astype(BF16), ((0, 5), (0, 0)))
     early = jnp.broadcast_to(early, (owners, 8, 3 * width))
     packets = exchange_owner(jnp.concatenate([pieces, early], axis=1), owner)
     packet = jnp.stack(packets)
@@ -1140,6 +1284,7 @@
     )
     w_own = packet[:, :part].reshape(model_width, 3 * width)
     early = packet[:, part].astype(F32)
+    late = packet[:, part + 1 : part + 3, :half_late].astype(F32).reshape(groups, -1)
     b_qk = early[:, : 2 * part].reshape(2 * model_width)
     b_value = early[:, 2 * part : 3 * part].reshape(model_width)
     g_one = early[:, 3 * part : 4 * part].reshape(1, model_width)
@@ -1154,50 +1299,44 @@
     sine = jnp.sin(angles)
     core_index = core.astype(jnp.int32).reshape(1)
 
-    late = jnp.concatenate([out_bias, in_bias, down_bias, gain_two, shift_two]).astype(BF16)
-    late = late.reshape(-1, model_width)
     hidden_part = hidden_width // groups
     share = hidden_part // 3
-    last = jnp.concatenate([out_weight.astype(BF16), late], axis=0)
-    last = jnp.pad(last, ((0, share - last.shape[0]), (0, 0)))
-    rep = lax.axis_index("rep")
-    tail_packet = lax.dynamic_slice_in_dim(
-        jnp.concatenate([down_weight.astype(BF16), last], axis=0), rep * share, share, 0
-    )
-    tokens, w_turned, b_own, cosine, sine, mix, tail_packet, in_packet = after(
-        (tokens, w_turned, b_own, cosine, sine, mix, tail_packet, in_weight.astype(BF16)),
-        grad_earlier,
-        depth_sums,
-    )
-    tail_parts = [tail_packet] + [shift_owner(tail_packet, k) for k in range(1, owners)]
-    states = project(tokens, w_turned, b_own, g_one, s_one, cosine, sine)
-    plain_all, qt, kt, vt, kv, *tail_parts = lax.optimization_barrier(
-        (*states, *tail_parts)
-    )
-    tail_stack = jnp.stack(tail_parts)
-    qt, tail_stack, in_packet = lax.optimization_barrier((qt, tail_stack, in_packet))
-    w_in = lax.all_gather(in_packet, "shard", axis=0, tiled=True)
-    tail_mine = [tail_stack] + [cross_rep(tail_stack, m) for m in range(1, 4)]
-    mixed_own, attended, stats = attend(core_index, qt, kv, vt)
-    mixed_own, attended, stats, *tail_mine = lax.optimization_barrier(
-        (mixed_own, attended, stats, *tail_mine)
-    )
-    mixed_two = lax.all_to_all(mixed_own, "shard", 0, 0)
-    tail_other = [swap_core(value) for value in tail_mine]
-    w_down, w_out, late = assemble(
-        jnp.stack([member, rep]).astype(jnp.int32), tail_mine, tail_other, part
-    )
-    late = late[:, 0].astype(F32)
-    grad_result = depth_weights[4] * cotangent
-    down_grad = grad_result.astype(BF16)
-    grad_active = contract(down_grad, w_down, 1, 1)
-    mixed_two, grad_active = lax.optimization_barrier((mixed_two, grad_active))
     row = lambda first, size: late[:, first : first + size].reshape(1, groups * size)
     b_out = row(0, part)
     b_in = row(part, hidden_part)
     b_down = row(part + hidden_part, part)
     g_two = row(2 * part + hidden_part, part)
     s_two = row(3 * part + hidden_part, part)
+    last = jnp.pad(out_weight.astype(BF16), ((0, share - part), (0, 0)))
+    rep = lax.axis_index("rep")
+    tail_packet = lax.dynamic_slice_in_dim(
+        jnp.concatenate([down_weight.astype(BF16), last], axis=0), rep * share, share, 0
+    )
+    tokens, w_turned, b_own, cosine, sine, mix, tail_packet, in_packet = after(
+        (tokens, w_turned, b_own, cosine, sine, mix, tail_packet, in_weight.astype(BF16)),
+        grad_earlier,
+        depth_sums,
+    )
+    tail_parts = [tail_packet] + [shift_owner(tail_packet, k) for k in range(1, owners)]
+    states = project(tokens, w_turned, b_own, g_one, s_one, cosine, sine, 0, groups, ())
+    plain_all, qt, kt, vt, kv, *tail_parts = lax.optimization_barrier((*states, *tail_parts))
+    grad_result = depth_weights[4] * cotangent
+    down_grad = grad_result.astype(BF16)
+    tail_stack = jnp.stack(tail_parts)
+    qt, tail_stack, in_packet, down_grad = lax.optimization_barrier(
+        (qt, tail_stack, in_packet, down_grad)
+    )
+    w_in = lax.all_gather(in_packet, "shard", axis=0, tiled=True)
+    tail_mine = every_rep(tail_stack)
+    mixed_own, attended, stats = attend(core_index, qt, kv, vt)
+    stats, *tail_mine = lax.optimization_barrier((stats, *tail_mine))
+    mixed_two = lax.all_to_all(mixed_own, "shard", 0, 0)
+    tail_other = [swap_core(value) for value in tail_mine]
+    w_down, w_out = assemble(
+        jnp.stack([member, rep]).astype(jnp.int32), tail_mine, tail_other, part
+    )
+    grad_active = contract(down_grad, w_down, 1, 1).astype(BF16)
+    mixed_two, grad_active = lax.optimization_barrier((mixed_two, grad_active))
 
     inputs = block_in.astype(F32)
     (
@@ -1210,36 +1349,40 @@
     grad_out_b, grad_gain_two, grad_shift_two = (token_sums[i] for i in range(3))
     grad_in_b = grad_in_b[0]
     grad_own = lax.all_to_all(grad_own, "shard", 0, 0)
-    folded, twin = pair_sums(core_index, normed_two_low, grad_hidden, mixed_two, branch_grad)
-    folded = add_low(folded, swap_core(twin))
-    grad_down_w = contract(active, down_grad, 0, 0)
+    folded, twin, grad_down_w, layer_out, last_depth = weight_sums(
+        core_index, depth_weights, normed_two_low, grad_hidden, mixed_two, branch_grad, active,
+        down_grad, w_down, b_down, middle, mix, cotangent,
+    )
     grad_down_b = jnp.sum(down_grad.astype(F32), axis=0)
-    grad_own, folded, down_sums = lax.optimization_barrier(
-        (grad_own, folded, grad_down_w.astype(BF16))
-    )
-    sent = send_rep(folded)
-    down_sums = lax.psum_scatter(down_sums, "shard", scatter_dimension=0, tiled=True)
-    joint_t = retrace(core_index, qt, grad_own, attended, stats, cosine, sine, kv, kt)
-    joint_t, folded, *sent = lax.optimization_barrier((joint_t, folded, *sent))
-    grad_normed = contract(joint_t, w_own, 0, 1).astype(BF16)
-    joint_t, folded, plain_all, down_sums, *sent = after(
-        (joint_t, folded, plain_all, down_sums, *sent), grad_normed
+    grad_own, folded, twin, grad_down_w, last_depth = lax.optimization_barrier(
+        (grad_own, folded, twin, grad_down_w, last_depth)
+    )
+    depth = jnp.concatenate([depth_sums, last_depth[None]], axis=0).sum(axis=(1, 2))
+    twin = swap_core(twin)
+    down_sums = lax.psum_scatter(grad_down_w, "shard", scatter_dimension=0, tiled=True)
+    joint_t, grad_normed = retrace(
+        core_index, qt, grad_own, attended, stats, cosine, sine, kv, kt, w_turned
+    )
+    joint_t, grad_normed, folded, twin, plain_all, depth = lax.optimization_barrier(
+        (joint_t, grad_normed, folded, twin, plain_all, depth)
     )
     grad_normed = lax.psum_scatter(
         grad_normed, "shard", scatter_dimension=0, tiled=True
     )
+    folded = add_low(folded, twin)
+    sent = send_rep(folded)
+
+    own_sums, other_sums, first_sums, joint_sums = joint_part(
+        core_index, plain_all, joint_t, w_turned, g_one, s_one
+    )
+    own_sums, other_sums, first_sums, joint_sums, *sent = lax.optimization_barrier(
+        (own_sums, other_sums, first_sums, joint_sums, *sent)
+    )
     folded = join_rep(folded, sent)
-
-    product = contract(plain_all, joint_t, 0, 1)
-    joint_sums = jnp.sum(joint_t.astype(F32), axis=1)
     arrived = exchange_owner(folded, owner)
-    product, joint_sums, *arrived = lax.optimization_barrier((product, joint_sums, *arrived))
-    pair_pieces = every_rep(add_low(*arrived))
-    w_wide = w_own.astype(F32)
-    grad_gain_one = jnp.sum(product * w_wide, axis=1)
-    grad_shift_one = jnp.sum(joint_sums[None, :] * w_wide, axis=1)
-    grad_qkv = g_one.reshape(-1, 1) * product + s_one.reshape(-1, 1) * joint_sums[None, :]
-    grad_qkv = grad_qkv.astype(BF16).reshape(groups, part, 3 * width)
+    grad_gain_one, grad_shift_one = first_sums[0], first_sums[1]
+    joint_sums = joint_sums[0]
+
     spread_sums = lax.dynamic_update_slice(
         jnp.zeros((3, model_width), F32), joint_sums.reshape(3, width), (0, owner * width)
     ).reshape(3 * model_width)
@@ -1254,65 +1397,77 @@
         grad_gain_two,
         grad_shift_two,
     )
-    small = jnp.concatenate([vector.reshape(groups, -1) for vector in vectors], axis=1)
-    small = jnp.pad(small, ((0, 0), (0, part * 128 - small.shape[1]))).astype(BF16)
-    small = jnp.transpose(small.reshape(groups, 128, part), (0, 2, 1))
-    mixed_sums = fold_core(jnp.concatenate([grad_qkv, small], axis=2), core)
+    counts = [vector.shape[0] // model_width for vector in vectors]
+    small = jnp.concatenate(
+        [
+            vector.reshape(groups, count, part).astype(BF16)
+            for vector, count in zip(vectors, counts)
+        ],
+        axis=1,
+    )
+    small = jnp.pad(small, ((0, 0), (0, part - small.shape[1]), (0, 128 - part)))
+    depth = split_depth(depth)
+    mark = (part // 4 - 8, 3 * width)
+    marked = jnp.zeros((4, part // 4, 128), BF16).at[:, mark[0], : depth.shape[0]].set(depth)
+    small = small + marked.reshape(1, part, 128)
+    small = small.reshape(owners, 2, part, 128)
+    depth_of = lambda value: join_depth(
+        value[mark[0], mark[1] : mark[1] + depth.shape[0]]
+    )
+    with_depth = lambda value, sums: value.at[
+        :, mark[0], mark[1] : mark[1] + depth.shape[0]
+    ].set(split_depth(sums))
+    received = swap_core(
+        jnp.concatenate([other_sums, pick(small, 1 - core, 1)], axis=2)
+    )
+    mixed_sums = add_low(
+        jnp.concatenate([own_sums, pick(small, core, 1)], axis=2), received
+    )
+    depth_sum = join_depth(depth) + depth_of(received[0])
     down_parts = pick_parts(down_sums[None])
     down_rows = part // 4
     columns = 3 * width + 128
-    sums_parts = pick_parts(mixed_sums)
+    sums_parts = [with_depth(value, depth_sum) for value in pick_parts(mixed_sums)]
     received = [
         cross_rep(
             jnp.concatenate([sums, down.reshape(owners, down_rows, model_width)], axis=2), k
         )
         for k, (sums, down) in enumerate(zip(sums_parts[1:], down_parts[1:]), 1)
     ]
-    (active,) = after((active,), *sums_parts)
-    result = middle + contract(active, w_down, 1, 0) + b_down
-    layer_out = depth_weights[4] * result + mix
-    local_depth = jnp.concatenate(
-        [jnp.sum(depth_sums, axis=(1, 2)), jnp.sum(result * cotangent)[None]]
-    )
-    layer_out, local_depth, *arrived = lax.optimization_barrier(
-        (layer_out, local_depth, *received, *pair_pieces)
-    )
-    received, pair_pieces = arrived[:3], arrived[3:]
-    depth = local_depth + swap_core(local_depth)
-    depth = depth + cross_rep(depth, 1)
-    depth = depth + cross_rep(depth, 2)
+    arrived = lax.optimization_barrier((*arrived, *received))
+    arrived, received = arrived[:owners], arrived[owners:]
+    pair_pieces = every_rep(add_low(*arrived))
     mixed_sums = add_low(sums_parts[0], *[value[:, :, :columns] for value in received])
+    depth_sum = add_ordered(
+        [depth_of(value[0]) for value in (sums_parts[0], *received)], lambda k: rep ^ k
+    )
+    mixed_sums = with_depth(mixed_sums, depth_sum)
     down_sums = add_low(
         down_parts[0].reshape(owners, down_rows, model_width),
         *[value[:, :, columns:] for value in received],
     )
     down_pieces = every_rep(jnp.concatenate([down_sums[k] for k in range(owners)], axis=1))
     arrived = exchange_owner(mixed_sums, owner)
-    depth = depth + lax.ppermute(depth, "shard", [(i, i ^ 2) for i in range(groups)])
-    grad_depth = depth + lax.ppermute(depth, "shard", [(i, i ^ 4) for i in range(groups)])
-    grad_depth, *arrived = lax.optimization_barrier((grad_depth, *arrived, *down_pieces))
-    arrived, down_pieces = arrived[:owners], arrived[owners:]
+    grad_normed, *arrived = lax.optimization_barrier(
+        (grad_normed, *arrived, *pair_pieces, *down_pieces)
+    )
+    pair_pieces, down_pieces = arrived[owners : 2 * owners], arrived[2 * owners :]
+    arrived = arrived[:owners]
+    grad_depth = add_ordered(
+        [depth_of(value) for value in arrived], lambda k: (owner - k) % owners
+    )
     small = add_low(*[value[:, 3 * width :] for value in arrived])
     by_distance = jnp.stack([value[:, : 3 * width] for value in arrived])
     by_owner = [pick(by_distance, (owner - k) % owners) for k in range(owners)]
-    sum_in, sum_out, sum_qkv, small, sum_down = unpack(
+    sum_in, sum_out, sum_qkv, sum_down, *small_outs = unpack(
         lax.axis_index("rep").astype(jnp.int32).reshape(1),
         pair_pieces,
         every_rep(jnp.concatenate([*by_owner, small], axis=1)),
         down_pieces,
         (hidden_width, model_width, 3 * width),
-    )
-    small = jnp.transpose(small).reshape(-1)
-    small_outs = []
-    start = 0
-    for vector in vectors:
-        size = vector.shape[0] // groups
-        small_outs.append(small[start : start + size])
-        start += size
-    finished = (layer_out, sum_qkv, sum_out, sum_in, sum_down, grad_depth, *small_outs)
-    grad_normed, layer_out, sum_qkv, sum_out, sum_in, sum_down, grad_depth, *small_outs = (
-        lax.optimization_barrier((grad_normed, *finished))
-    )
+        counts,
+    )
+    small_outs = [value[0] for value in small_outs]
     grad_normed = grad_normed.astype(F32)
     center = inputs - jnp.mean(inputs, axis=-1, keepdims=True)
     scale = lax.rsqrt(jnp.mean(center * center, axis=-1, keepdims=True) + EPSILON)
@@ -1349,10 +1504,9 @@
         and row_count == CHUNK
         and head_count % (groups // 2) == 0
         and head_count // (groups // 2) <= 8
-        and late_size % model_width == 0
+        and late_size <= 12 * model_width // groups
         and args[5].shape[1] % (3 * groups) == 0
-        and model_width // groups + late_size // model_width
-        <= args[5].shape[1] // (3 * groups)
+        and model_width // groups <= args[5].shape[1] // (3 * groups)
     ):
         return head_split_device(*args)
     return generic_device(*args)

time: 414 us -> 410 us (level); the launches traced: 413 us -> 403 us
  Pallas kernels: 131 us -> 161 us
  matrix products: 35.7 us -> 6.36 us
  starting transfers between devices: 70.8 us -> 52.3 us
  local copies, waits for them, and re-layouts: 29.4 us -> 36.8 us
    dot_general x5 -> x1, matrix products: 35.7 us -> 6.36 us  [contract(): lax.dot_general(left, right, (((left_dim,), (right_dim,)), ((), ())), pre...]
    pallas_call x4 -> x5, Pallas kernels: 34.9 us -> 56.6 us  [the longest x1 17.7 us: weight_sums(): pl.pallas_call(weight_kernel, name='weight_sums', grid_spec=pltpu.Prefetc...]
    reduce_scatter x1, starting transfers between devices: 12.7 us -> 0.01 us  [head_split_device(): lax.psum_scatter(grad_normed, 'shard', scatter_dimension=0, tiled=True)]
    pallas_call x1, Pallas kernels: 43.9 us -> 52.1 us  [retrace(): pl.pallas_call(retrace_kernel, name='retrace', cost_estimate=cost(5 * 2 *...]
    ppermute x2 -> x0, starting transfers between devices: 6.74 us -> none  [the longest x1 4.13 us: head_split_device(): lax.ppermute(depth, 'shard', [(i, i ^ 4) for i in range(groups)])]
    all_to_all x1, waiting for transfers between devices: 8.96 us -> 2.26 us  [head_split_device(): grad_own = lax.all_to_all(grad_own, 'shard', 0, 0)]
    reduce_sum x5 -> x1, other arithmetic: 6.76 us -> 0.13 us  [head_split_device(): jnp.concatenate([depth_sums, last_depth[None]], axis=0).sum(axis=(1, 2))]
    all_to_all x1, waiting for transfers between devices: 2.27 us -> 8.26 us  [head_split_device(): mixed_two = lax.all_to_all(mixed_own, 'shard', 0, 0)]
  transfers between devices with their start and end apart: 48 -> 43, of which waited for: 22 -> 18; matrix products, arithmetic and copies ran while one was open for 21% -> 16% of each run, Pallas kernels for 25% -> 34%
where the time goes in v1:
time: 410 us; the launch traced here: 403 us
  Pallas kernels  161 us (39%)
  waiting for transfers between devices  95.4 us (23%)
  starting transfers between devices  52.3 us (13%)
  local copies, waits for them, and re-layouts  36.8 us (9%)
  other arithmetic  35.9 us (9%)
  between operations  15.2 us (4%)
  matrix products  6.36 us (2%)
    pallas_call x1, Pallas kernels, retrace(): pl.pallas_call(retrace_kernel, name='retrace', cost_estimate=cost(5 * 2 *...  52.1 us
    ppermute x12, waiting for transfers between devices, shift_owner(): lax.ppermute(value, 'shard', [(i, (i + step) % groups) for i in range(gro...  30.9 us
    ppermute x18, waiting for transfers between devices, cross_rep(): lax.ppermute(value, 'rep', [(i, i ^ mask) for i in range(lax.axis_size('r...  28.7 us
    pallas_call x1, Pallas kernels, attend(): pl.pallas_call(attend_kernel, name='attend', cost_estimate=cost(2 * 2 * B...  25.9 us
    all_gather x1, waiting for transfers between devices, head_split_device(): tokens = lax.all_gather(block_in, 'shard', axis=0, tiled=True)  22.7 us
    ppermute x12, starting transfers between devices, shift_owner(): lax.ppermute(value, 'shard', [(i, (i + step) % groups) for i in range(gro...  21.8 us
    ppermute x18, starting transfers between devices, cross_rep(): lax.ppermute(value, 'rep', [(i, i ^ mask) for i in range(lax.axis_size('r...  21.4 us
    pallas_call x1, Pallas kernels, middle_part(): pl.pallas_call(middle_kernel, name='middle', cost_estimate=cost(4 * rows...  18.6 us
  transfers between devices with their start and end apart: 43, of which 18 were waited for; matrix products, arithmetic and copies ran while one was open for 16% of the time, Pallas kernels for 34%

profile of v1, /device:TPU:0, one launch (start us, length us, event | category | flops | bytes accessed | tf_op | source)
XLA Modules:
  0.0 402.6 jit_solution(9909459483706819714)
XLA Ops:
  11.9 3.1 collective-permute-start
  15.0 2.6 collective-permute-start.1
  18.9 2.8 collective-permute-done
  21.8 12.3 %collective-permute-done.1 = bf16[104,576]{0,1:T(8,128)(2,1)S(1)} collective-permute-done((bf16[104,576]{0,1:T(8,128)(2,1)S(1)}, bf16[104,576]{0,1:T(8,128)(2,1)S(1)}, u32[]{:S(2)}, u32[]{:S(2)}) %collective-permute-start.1) | collective-permute-done | bytes 119840 | tf_op jit(solution)/shard_map/ppermute | solution.py:793
  35.3 2.8 multiply_sine_fusion
  38.2 2.1 convert_element_type.300
  41.0 7.5 %average.1 = (f32[4,512,768]{2,1,0:T(8,128)}, f32[512,768]{1,0:T(8,128)}, f32[4,8,768]{2,1,0:T(8,128)}) custom-call(f32[5]{0:T(128)} %weights_ref.5, bf16[4,512,768]{2,1,0:T(8,128)(2,1)} %earlier_ref.1, f32[512,768]{1,0:T(8,128)} %cotangent_ref.5), custom_call_target="tpu_custom_call" | custom-call | flops 9437184 | bytes 12582912 | tf_op jit(solution)/shard_map/average/pallas_call | solution.py:464
  49.4 1.6 copy.95
  60.1 22.7 %all-gather.3.cloned.1.call-done.x_ref = bf16[4096,768]{1,0:T(8,128)(2,1)} async-done(((bf16[512,768]{1,0:T(8,128)(2,1)}), bf16[4096,768]{1,0:T(8,128)(2,1)}) %all-gather.3.cloned.1.call-update) | async-done | bytes 6291472 | tf_op jit(solution)/shard_map/all_gather | solution.py:1271
  82.7 2.4 collective-permute-start.5
  85.1 1.6 collective-permute-start.6
  87.6 13.5 %project.1 = (bf16[4096,768]{1,0:T(8,128)(2,1)}, bf16[192,4096]{1,0:T(8,128)(2,1)}, bf16[192,4096]{1,0:T(8,128)(2,1)}, bf16[192,4096]{1,0:T(8,128)(2,1)}, bf16[3,4096,128]{2,1,0:T(8,128)(2,1)}) custom-call(bf16[4096,768]{1,0:T(8,128)(2,1)} %all-gather.3.cloned.1.call-done.x_ref, bf16[576,768]{1,0:T(8,128)(2,1)} %bitcast.170, f32[576,1]{1,0:T(8,128)} %copy.105.bias_ref, ...), custom_call_target="tpu_custom_call" | custom-call | flops 3623878656 | bytes 37748736 | tf_op jit(solution)/shard_map/project/pallas_call | solution.py:410
  101.3 1.6 collective-permute-start.7
  102.9 1.5 collective-permute-start.8
  104.8 25.9 %attend.1 = (bf16[8,192,256]{2,1,0:T(8,128)(2,1)}, f32[8,192,256]{2,1,0:T(8,128)}, f32[8,8,256]{2,1,0:T(8,128)}) custom-call(s32[1]{0:T(128)} %bitcast.core_ref, bf16[192,4096]{1,0:T(8,128)(2,1)} %get-tuple-element.221.qt_ref, bf16[3,4096,128]{2,1,0:T(8,128)(2,1)} %get-tuple-element.222.kv_ref, bf16[192,4096]{1,0:T(8,128)(2,1)} %get-tuple-element.223.vt_ref), custom_call_target="tpu_custom_call" | custom-call | flops 14495514624 | bytes 9437184 | tf_op jit(solution)/shard_map/attend/pallas_call | solution.py:563
  130.7 4.1 %all-to-all-start = ((bf16[8,192,256]{2,1,0:T(8,128)(2,1)}), bf16[8,192,256]{2,1,0:T(8,128)(2,1)S(1)}, u32[]{:S(2)}, u32[]{:S(2)}) async-start(bf16[8,192,256]{2,1,0:T(8,128)(2,1)} %get-tuple-element.224), calls=%async_computation | async-start | bytes 1572864 | tf_op jit(solution)/shard_map/all_to_all | solution.py:1333
  134.8 3.9 collective-permute-done.8.refs_2_
  144.9 9.2 %assemble.1 = (bf16[3072,768]{1,0:T(8,128)(2,1)}, bf16[768,768]{1,0:T(8,128)(2,1)}) custom-call(s32[2]{0:T(128)} %pad_add_fusion.1.place_ref, bf16[4,128,768]{2,1,0:T(8,128)(2,1)} %copy-done.6, bf16[4,128,768]{2,1,0:T(8,128)(2,1)} %collective-permute-done.7.refs_1_, bf16[4,128,768]{2,1,0:T(8,128)(2,1)} %collective-permute-done.8.refs_2_, ...), custom_call_target="tpu_custom_call" | custom-call | tf_op jit(solution)/shard_map/assemble/pallas_call | solution.py:765
  154.1 6.4 %convolution_convert_fusion.grad_ref = bf16[512,3072]{1,0:T(8,128)(2,1)} fusion(bf16[512,768]{1,0:T(8,128)(2,1)S(1)} %multiply_convert_fusion.down_grad_ref, bf16[3072,768]{1,0:T(8,128)(2,1)} %get-tuple-element.232.w_down_ref), kind=kOutput, calls=%fused_computation.1 | convolution fusion | flops 2417491968 | bytes 8650752 | tf_op jit(solution)/shard_map/dot_general | solution.py:361
  160.5 8.3 %all-to-all-done.mixed_ref = bf16[8,192,256]{2,1,0:T(8,128)(2,1)S(1)} async-done(((bf16[8,192,256]{2,1,0:T(8,128)(2,1)}), bf16[8,192,256]{2,1,0:T(8,128)(2,1)S(1)}, u32[]{:S(2)}, u32[]{:S(2)}) %all-to-all-start) | async-done | bytes 786464 | tf_op jit(solution)/shard_map/all_to_all | solution.py:1333
  169.6 18.6 %middle.1 = (f32[512,768]{1,0:T(8,128)}, bf16[512,768]{1,0:T(8,128)(2,1)}, bf16[512,3072]{1,0:T(8,128)(2,1)}, bf16[512,3072]{1,0:T(8,128)(2,1)}, f32[512,768]{1,...) custom-call(s32[1]{0:T(128)} %bitcast.core_ref, ...), custom_call_target="tpu_custom_call" | custom-call | flops 6039797760 | bytes 17301504 | tf_op jit(solution)/shard_map/middle/pallas_call | solution.py:1026
  188.3 3.6 all-to-all-start.1
  192.8 17.7 %weight_sums.1 = (bf16[4,96,3840]{2,1,0:T(8,128)(2,1)}, bf16[4,96,3840]{2,1,0:T(8,128)(2,1)}, bf16[3072,768]{1,0:T(8,128)(2,1)}, f32[512,768]{1,0:T(8,128)}, f32[8,768]{1,0:T(8,128)}) custom-call(s32[1]{0:T(128)} %bitcast.core_ref, f32[5]{0:T(128)} %weights_ref.5, bf16[512,768]{1,0:T(8,128)(2,1)} %get-tuple-element.237.low_ref, ...), custom_call_target="tpu_custom_call" | custom-call | tf_op jit(solution)/shard_map/weight_sums/pallas_call | solution.py:1121
  210.5 2.3 all-to-all-done.1.grad_ref
  214.6 52.1 %retrace.1 = (bf16[576,4096]{1,0:T(8,128)(2,1)}, bf16[4096,768]{1,0:T(8,128)(2,1)}) custom-call(s32[1]{0:T(128)} %bitcast.core_ref, bf16[192,4096]{1,0:T(8,128)(2,1)} %get-tuple-element.221.qt_ref, bf16[8,192,256]{2,1,0:T(8,128)(2,1)} %copy-done.11, f32[8,192,256]{2,1,0:T(8,128)} %get-tuple-element.251.full_ref, f32[8,8,256]{2,1,0:T(8,128)} %get-tuple-element.252.stat_ref, ...), custom_call_target="tpu_custom_call" | custom-call | flops 36238786560 | bytes 11010048 | tf_op jit(solution)/shard_map/retrace/pallas_call | solution.py:687
  266.7 3.4 add_convert_fusion
  271.9 1.5 collective-permute-start.15
  273.4 1.5 collective-permute-start.16
  277.1 12.4 %joint_part.1 = (bf16[4,96,576]{2,1,0:T(8,128)(2,1)}, bf16[4,96,576]{2,1,0:T(8,128)(2,1)}, f32[8,768]{1,0:T(8,128)}, f32[8,576]{1,0:T(8,128)}) custom-call(s32[1]{0:T(128)} %bitcast.core_ref, bf16[4096,768]{1,0:T(8,128)(2,1)} %get-tuple-element.261.plain_ref, bf16[576,4096]{1,0:T(8,128)(2,1)} %get-tuple-element.262.joint_ref, bf16[576,768]{1,0:T(8,128)(2,1)} %bitcast.172, ...), custom_call_target="tpu_custom_call" | custom-call | tf_op jit(solution)/shard_map/joint_part/pallas_call | solution.py:1199
  289.6 2.0 collective-permute-done.15
  291.5 15.3 %collective-permute-done.16 = bf16[4,24,3840]{2,1,0:T(8,128)(2,1)} collective-permute-done((bf16[4,24,3840]{2,1,0:T(8,128)(2,1)S(1)}, bf16[4,24,3840]{2,1,0:T(8,128)(2,1)}, u32[]{:S(2)}, u32[]{:S(2)}) %collective-permute-start.16) | collective-permute-done | bytes 737312 | tf_op jit(solution)/shard_map/ppermute | solution.py:797
  311.5 2.2 fusion.12
  314.8 2.1 collective-permute-start.20
  321.8 1.5 collective-permute-start.24
  323.4 1.5 collective-permute-start.23
  325.7 2.5 collective-permute-done.19
  328.3 9.8 %collective-permute-done.20 = bf16[24,3840]{1,0:T(8,128)(2,1)S(1)} collective-permute-done((bf16[24,3840]{1,0:T(8,128)(2,1)}, bf16[24,3840]{1,0:T(8,128)(2,1)S(1)}, u32[]{:S(2)}, u32[]{:S(2)}) %collective-permute-start.20) | collective-permute-done | bytes 184352 | tf_op jit(solution)/shard_map/ppermute | solution.py:793
  338.1 3.4 collective-permute-done.21
  342.5 1.5 collective-permute-start.31
  346.1 6.0 %collective-permute-start.25 = (bf16[24,704]{1,0:T(8,128)(2,1)S(1)}, bf16[24,704]{1,0:T(8,128)(2,1)S(1)}, u32[]{:S(2)}, u32[]{:S(2)}) collective-permute-start(bf16[24,704]{1,0:T(8,128)(2,1)S(1)} %get-tuple-element.361), channel_id=1, source_target_pairs={{0,2},{1,3},{2,4},{3,5},{4,6},{5,7},{6,0},{7,1},{8,10},{9,11},{10,... | collective-permute-start | bytes 101384 | tf_op jit(solution)/shard_map/ppermute | solution.py:793
  352.7 1.9 collective-permute-start.27
  355.8 1.5 collective-permute-start.33
  359.4 1.4 collective-permute-start.30
  363.6 3.4 collective-permute-done.28.refs_1_
  367.3 2.0 collective-permute-done.30.refs_3_
  380.1 1.6 collective-permute-start.36
  386.3 2.4 fusion.7
  390.6 3.8 unpack.1
  (300 shorter events, 72.8 us)
Async XLA Ops:
  7.2 75.5 %all-gather.3.cloned.1.call-start = ((), (), s32[]{:S(2)}) async-start(), calls=%async_computation.4 | async-start | bytes 7077888 | tf_op jit(solution)/shard_map/all_gather | solution.py:1271
  7.9 160.8 %all-gather.5.cloned.1.call-start = ((), (), s32[]{:S(2)}) async-start(), calls=%async_computation.5 | async-start | bytes 5308416 | tf_op jit(solution)/shard_map/all_gather | solution.py:1329
  11.9 9.9 %collective-permute-start = (bf16[104,576]{0,1:T(8,128)(2,1)S(1)}, bf16[104,576]{0,1:T(8,128)(2,1)S(1)}, u32[]{:S(2)}, u32[]{:S(2)}) collective-permute-start(bf16[104,576]{0,1:T(8,128)(2,1)S(1)} %get-tuple-element.336), channel_id=1, source_target_pairs={{0,2},{1,3},{2,4},{3,5},{4,6},{5,7},{6,0},{7,1},{8,10},{9,11},{10,... | collective-permute-start | bytes 359432 | tf_op jit(solution)/shard_map/ppermute | solution.py:793
  15.0 19.1 %collective-permute-start.1 = (bf16[104,576]{0,1:T(8,128)(2,1)S(1)}, bf16[104,576]{0,1:T(8,128)(2,1)S(1)}, u32[]{:S(2)}, u32[]{:S(2)}) collective-permute-start(bf16[104,576]{0,1:T(8,128)(2,1)S(1)} %get-tuple-element.337), channel_id=1, source_target_pairs={{0,4},{1,5},{2,6},{3,7},{4,0},{5,1},{6,2},{7,3},{8,12},{9,13},{10,... | collective-permute-start | bytes 359432 | tf_op jit(solution)/shard_map/ppermute | solution.py:793
  17.6 16.5 %collective-permute-start.2 = (bf16[104,576]{0,1:T(8,128)(2,1)S(1)}, bf16[104,576]{0,1:T(8,128)(2,1)S(1)}, u32[]{:S(2)}, u32[]{:S(2)}) collective-permute-start(bf16[104,576]{0,1:T(8,128)(2,1)S(1)} %get-tuple-element.338), channel_id=1, source_target_pairs={{0,6},{1,7},{2,0},{3,1},{4,2},{5,3},{6,4},{7,5},{8,14},{9,15},{10,... | collective-permute-start | bytes 359432 | tf_op jit(solution)/shard_map/ppermute | solution.py:793
  35.3 14.2 %collective-permute-start.3 = (bf16[4,104,576]{2,1,0:T(8,128)(2,1)}, bf16[4,104,576]{2,1,0:T(8,128)(2,1)}, u32[]{:S(2)}, u32[]{:S(2)}) collective-permute-start(bf16[4,104,576]{2,1,0:T(8,128)(2,1)} %copy.94), channel_id=1, source_target_pairs={{0,1},{1,0},{2,3},{3,2},{4,5},{5,4},{6,7},{7,6},{8,9},{9,8},{10,11... | collective-permute-start | bytes 1437704 | tf_op jit(solution)/shard_map/ppermute | solution.py:787
  49.4 104.7 %copy-start.3 = (bf16[512,768]{1,0:T(8,128)(2,1)}, bf16[512,768]{1,0:T(8,128)(2,1)S(1)}, u32[]{:S(2)}) copy-start(bf16[512,768]{1,0:T(8,128)(2,1)S(1)} %multiply_convert_fusion.down_grad_ref) | copy-start | bytes 2359300
  82.7 18.4 %collective-permute-start.4 = (bf16[128,768]{1,0:T(8,128)(2,1)S(1)}, bf16[128,768]{1,0:T(8,128)(2,1)S(1)}, u32[]{:S(2)}, u32[]{:S(2)}) collective-permute-start(bf16[128,768]{1,0:T(8,128)(2,1)S(1)} %fusion.17), channel_id=1, source_target_pairs={{0,2},{1,3},{2,4},{3,5},{4,6},{5,7},{6,0},{7,1},{8,10},{9,11},{10,... | collective-permute-start | bytes 589832 | tf_op jit(solution)/shard_map/ppermute | solution.py:793
  82.7 18.4 %collective-permute-start.5 = (bf16[128,768]{1,0:T(8,128)(2,1)S(1)}, bf16[128,768]{1,0:T(8,128)(2,1)S(1)}, u32[]{:S(2)}, u32[]{:S(2)}) collective-permute-start(bf16[128,768]{1,0:T(8,128)(2,1)S(1)} %fusion.17), channel_id=1, source_target_pairs={{0,4},{1,5},{2,6},{3,7},{4,0},{5,1},{6,2},{7,3},{8,12},{9,13},{10,... | collective-permute-start | bytes 589832 | tf_op jit(solution)/shard_map/ppermute | solution.py:793
  85.1 16.0 %collective-permute-start.6 = (bf16[128,768]{1,0:T(8,128)(2,1)S(1)}, bf16[128,768]{1,0:T(8,128)(2,1)S(1)}, u32[]{:S(2)}, u32[]{:S(2)}) collective-permute-start(bf16[128,768]{1,0:T(8,128)(2,1)S(1)} %fusion.17), channel_id=1, source_target_pairs={{0,6},{1,7},{2,0},{3,1},{4,2},{5,3},{6,4},{7,5},{8,14},{9,15},{10,... | collective-permute-start | bytes 589832 | tf_op jit(solution)/shard_map/ppermute | solution.py:793
  101.2 37.4 %copy-start.6 = (bf16[4,128,768]{2,1,0:T(8,128)(2,1)}, bf16[4,128,768]{2,1,0:T(8,128)(2,1)S(1)}, u32[]{:S(2)}) copy-start(bf16[4,128,768]{2,1,0:T(8,128)(2,1)S(1)} %pad_maximum_fusion.refs_0_) | copy-start | bytes 2359300
  101.3 33.5 %collective-permute-start.7 = (bf16[4,128,768]{2,1,0:T(8,128)(2,1)S(1)}, bf16[4,128,768]{2,1,0:T(8,128)(2,1)}, u32[]{:S(2)}, u32[]{:S(2)}) collective-permute-start(bf16[4,128,768]{2,1,0:T(8,128)(2,1)S(1)} %pad_maximum_fusion.refs_0_), channel_id=1, source_target_pairs={{0,8},{8,0},{16,24},{24,16},{1,9},{9,1},{17,25},{25,17},{2,10},{10... | collective-permute-start | bytes 2359304 | tf_op jit(solution)/shard_map/ppermute | solution.py:797
  102.9 35.8 %collective-permute-start.8 = (bf16[4,128,768]{2,1,0:T(8,128)(2,1)S(1)}, bf16[4,128,768]{2,1,0:T(8,128)(2,1)}, u32[]{:S(2)}, u32[]{:S(2)}) collective-permute-start(bf16[4,128,768]{2,1,0:T(8,128)(2,1)S(1)} %pad_maximum_fusion.refs_0_), channel_id=1, source_target_pairs={{0,16},{8,24},{16,0},{24,8},{1,17},{9,25},{17,1},{25,9},{2,18},{10... | collective-permute-start | bytes 2359304 | tf_op jit(solution)/shard_map/ppermute | solution.py:797
  104.4 34.3 %collective-permute-start.9 = (bf16[4,128,768]{2,1,0:T(8,128)(2,1)S(1)}, bf16[4,128,768]{2,1,0:T(8,128)(2,1)}, u32[]{:S(2)}, u32[]{:S(2)}) collective-permute-start(bf16[4,128,768]{2,1,0:T(8,128)(2,1)S(1)} %pad_maximum_fusion.refs_0_), channel_id=1, source_target_pairs={{0,24},{8,16},{16,8},{24,0},{1,25},{9,17},{17,9},{25,1},{2,26},{10... | collective-permute-start | bytes 2359304 | tf_op jit(solution)/shard_map/ppermute | solution.py:797
  130.7 38.0 %all-to-all-start = ((bf16[8,192,256]{2,1,0:T(8,128)(2,1)}), bf16[8,192,256]{2,1,0:T(8,128)(2,1)S(1)}, u32[]{:S(2)}, u32[]{:S(2)}) async-start(bf16[8,192,256]{2,1,0:T(8,128)(2,1)} %get-tuple-element.224), calls=%async_computation | async-start | bytes 1572864 | tf_op jit(solution)/shard_map/all_to_all | solution.py:1333
  138.7 4.4 %collective-permute-start.10 = (bf16[4,128,768]{2,1,0:T(8,128)(2,1)S(1)}, bf16[4,128,768]{2,1,0:T(8,128)(2,1)}, u32[]{:S(2)}, u32[]{:S(2)}) collective-permute-start(bf16[4,128,768]{2,1,0:T(8,128)(2,1)S(1)} %pad_maximum_fusion.refs_0_), channel_id=1, source_target_pairs={{0,1},{1,0},{2,3},{3,2},{4,5},{5,4},{6,7},{7,6},{8,9},{9,8},{10,11... | collective-permute-start | bytes 2359304 | tf_op jit(solution)/shard_map/ppermute | solution.py:787
  138.7 4.4 %collective-permute-start.11 = (bf16[4,128,768]{2,1,0:T(8,128)(2,1)}, bf16[4,128,768]{2,1,0:T(8,128)(2,1)}, u32[]{:S(2)}, u32[]{:S(2)}) collective-permute-start(bf16[4,128,768]{2,1,0:T(8,128)(2,1)} %collective-permute-done.7.refs_1_), channel_id=1, source_target_pairs={{0,1},{1,0},{2,3},{3,2},{4,5},{5,4},{6,7},{7,6},{8,9},{9,8},{10,11... | collective-permute-start | bytes 2359304 | tf_op jit(solution)/shard_map/ppermute | solution.py:787
  139.2 4.6 %collective-permute-start.12 = (bf16[4,128,768]{2,1,0:T(8,128)(2,1)}, bf16[4,128,768]{2,1,0:T(8,128)(2,1)}, u32[]{:S(2)}, u32[]{:S(2)}) collective-permute-start(bf16[4,128,768]{2,1,0:T(8,128)(2,1)} %collective-permute-done.8.refs_2_), channel_id=1, source_target_pairs={{0,1},{1,0},{2,3},{3,2},{4,5},{5,4},{6,7},{7,6},{8,9},{9,8},{10,11... | collective-permute-start | bytes 2359304 | tf_op jit(solution)/shard_map/ppermute | solution.py:787
  139.3 5.6 %collective-permute-start.13 = (bf16[4,128,768]{2,1,0:T(8,128)(2,1)}, bf16[4,128,768]{2,1,0:T(8,128)(2,1)}, u32[]{:S(2)}, u32[]{:S(2)}) collective-permute-start(bf16[4,128,768]{2,1,0:T(8,128)(2,1)} %collective-permute-done.9.refs_3_), channel_id=1, source_target_pairs={{0,1},{1,0},{2,3},{3,2},{4,5},{5,4},{6,7},{7,6},{8,9},{9,8},{10,11... | collective-permute-start | bytes 2359304 | tf_op jit(solution)/shard_map/ppermute | solution.py:787
  188.3 24.5 %all-to-all-start.1 = ((bf16[8,192,256]{2,1,0:T(8,128)(2,1)}), bf16[8,192,256]{2,1,0:T(8,128)(2,1)S(1)}, u32[]{:S(2)}, u32[]{:S(2)}) async-start(bf16[8,192,256]{2,1,0:T(8,128)(2,1)} %get-tuple-element.245), calls=%async_computation.1 | async-start | bytes 1572864 | tf_op jit(solution)/shard_map/all_to_all | solution.py:1351
  191.8 128.7 %reduce-scatter.5.cloned.1.call-start = ((), (), s32[]{:S(2)}) async-start(), calls=%async_computation.7 | async-start | bytes 5308416 | tf_op jit(solution)/shard_map/reduce_scatter | solution.py:1362
  213.6 156.3 %reduce-scatter.3.cloned.1.call-start = ((), (), s32[]{:S(2)}) async-start(), calls=%async_computation.6 | async-start | bytes 7077888 | tf_op jit(solution)/shard_map/reduce_scatter | solution.py:1369
  214.3 52.3 %collective-permute-start.14 = (bf16[4,96,3840]{2,1,0:T(8,128)(2,1)}, bf16[4,96,3840]{2,1,0:T(8,128)(2,1)}, u32[]{:S(2)}, u32[]{:S(2)}) collective-permute-start(bf16[4,96,3840]{2,1,0:T(8,128)(2,1)} %get-tuple-element.257), channel_id=1, source_target_pairs={{0,1},{1,0},{2,3},{3,2},{4,5},{5,4},{6,7},{7,6},{8,9},{9,8},{10,11... | collective-permute-start | bytes 8847368 | tf_op jit(solution)/shard_map/ppermute | solution.py:787
  271.9 19.6 %collective-permute-start.15 = (bf16[4,24,3840]{2,1,0:T(8,128)(2,1)}, bf16[4,24,3840]{2,1,0:T(8,128)(2,1)}, u32[]{:S(2)}, u32[]{:S(2)}) collective-permute-start(bf16[4,24,3840]{2,1,0:T(8,128)(2,1)} %get-tuple-element.326), channel_id=1, source_target_pairs={{0,8},{8,0},{16,24},{24,16},{1,9},{9,1},{17,25},{25,17},{2,10},{10... | collective-permute-start | bytes 2211848 | tf_op jit(solution)/shard_map/ppermute | solution.py:797
  273.4 33.4 %collective-permute-start.16 = (bf16[4,24,3840]{2,1,0:T(8,128)(2,1)S(1)}, bf16[4,24,3840]{2,1,0:T(8,128)(2,1)}, u32[]{:S(2)}, u32[]{:S(2)}) collective-permute-start(bf16[4,24,3840]{2,1,0:T(8,128)(2,1)S(1)} %get-tuple-element.325), channel_id=1, source_target_pairs={{0,16},{8,24},{16,0},{24,8},{1,17},{9,25},{17,1},{25,9},{2,18},{10... | collective-permute-start | bytes 2211848 | tf_op jit(solution)/shard_map/ppermute | solution.py:797
  274.9 33.0 %collective-permute-start.17 = (bf16[4,24,3840]{2,1,0:T(8,128)(2,1)S(1)}, bf16[4,24,3840]{2,1,0:T(8,128)(2,1)}, u32[]{:S(2)}, u32[]{:S(2)}) collective-permute-start(bf16[4,24,3840]{2,1,0:T(8,128)(2,1)S(1)} %get-tuple-element.324), channel_id=1, source_target_pairs={{0,24},{8,16},{16,8},{24,0},{1,25},{9,17},{17,9},{25,1},{2,26},{10... | collective-permute-start | bytes 2211848 | tf_op jit(solution)/shard_map/ppermute | solution.py:797
  311.4 5.5 %collective-permute-start.18 = (bf16[4,96,704]{2,1,0:T(8,128)(2,1)S(1)}, bf16[4,96,704]{2,1,0:T(8,128)(2,1)S(1)}, u32[]{:S(2)}, u32[]{:S(2)}) collective-permute-start(bf16[4,96,704]{2,1,0:T(8,128)(2,1)S(1)} %pad_maximum_fusion.2), channel_id=1, source_target_pairs={{0,1},{1,0},{2,3},{3,2},{4,5},{5,4},{6,7},{7,6},{8,9},{9,8},{10,11... | collective-permute-start | bytes 1622024 | tf_op jit(solution)/shard_map/ppermute | solution.py:787
  314.5 13.7 %collective-permute-start.19 = (bf16[24,3840]{1,0:T(8,128)(2,1)}, bf16[24,3840]{1,0:T(8,128)(2,1)S(1)}, u32[]{:S(2)}, u32[]{:S(2)}) collective-permute-start(bf16[24,3840]{1,0:T(8,128)(2,1)} %get-tuple-element.341), channel_id=1, source_target_pairs={{0,2},{1,3},{2,4},{3,5},{4,6},{5,7},{6,0},{7,1},{8,10},{9,11},{10,... | collective-permute-start | bytes 552968 | tf_op jit(solution)/shard_map/ppermute | solution.py:793
  314.8 23.4 %collective-permute-start.20 = (bf16[24,3840]{1,0:T(8,128)(2,1)}, bf16[24,3840]{1,0:T(8,128)(2,1)S(1)}, u32[]{:S(2)}, u32[]{:S(2)}) collective-permute-start(bf16[24,3840]{1,0:T(8,128)(2,1)} %get-tuple-element.340), channel_id=1, source_target_pairs={{0,4},{1,5},{2,6},{3,7},{4,0},{5,1},{6,2},{7,3},{8,12},{9,13},{10,... | collective-permute-start | bytes 552968 | tf_op jit(solution)/shard_map/ppermute | solution.py:793
  321.8 19.8 %collective-permute-start.24 = (bf16[4,24,1472]{2,1,0:T(8,128)(2,1)S(1)}, bf16[4,24,1472]{2,1,0:T(8,128)(2,1)S(1)}, u32[]{:S(2)}, u32[]{:S(2)}) collective-permute-start(bf16[4,24,1472]{2,1,0:T(8,128)(2,1)S(1)} %pad_maximum_fusion.5), channel_id=1, source_target_pairs={{0,24},{8,16},{16,8},{24,0},{1,25},{9,17},{17,9},{25,1},{2,26},{10... | collective-permute-start | bytes 847880 | tf_op jit(solution)/shard_map/ppermute | solution.py:797
  323.4 18.2 %collective-permute-start.23 = (bf16[4,24,1472]{2,1,0:T(8,128)(2,1)S(1)}, bf16[4,24,1472]{2,1,0:T(8,128)(2,1)S(1)}, u32[]{:S(2)}, u32[]{:S(2)}) collective-permute-start(bf16[4,24,1472]{2,1,0:T(8,128)(2,1)S(1)} %pad_maximum_fusion.4), channel_id=1, source_target_pairs={{0,16},{8,24},{16,0},{24,8},{1,17},{9,25},{17,1},{25,9},{2,18},{10... | collective-permute-start | bytes 847880 | tf_op jit(solution)/shard_map/ppermute | solution.py:797
  325.0 16.5 %collective-permute-start.22 = (bf16[4,24,1472]{2,1,0:T(8,128)(2,1)S(1)}, bf16[4,24,1472]{2,1,0:T(8,128)(2,1)S(1)}, u32[]{:S(2)}, u32[]{:S(2)}) collective-permute-start(bf16[4,24,1472]{2,1,0:T(8,128)(2,1)S(1)} %pad_maximum_fusion.3), channel_id=1, source_target_pairs={{0,8},{8,0},{16,24},{24,16},{1,9},{9,1},{17,25},{25,17},{2,10},{10... | collective-permute-start | bytes 847880 | tf_op jit(solution)/shard_map/ppermute | solution.py:797
  328.2 13.3 %collective-permute-start.21 = (bf16[24,3840]{1,0:T(8,128)(2,1)S(1)}, bf16[24,3840]{1,0:T(8,128)(2,1)S(1)}, u32[]{:S(2)}, u32[]{:S(2)}) collective-permute-start(bf16[24,3840]{1,0:T(8,128)(2,1)S(1)} %get-tuple-element.339), channel_id=1, source_target_pairs={{0,6},{1,7},{2,0},{3,1},{4,2},{5,3},{6,4},{7,5},{8,14},{9,15},{10,... | collective-permute-start | bytes 552968 | tf_op jit(solution)/shard_map/ppermute | solution.py:793
  342.5 34.8 %copy-start.13 = (bf16[24,3072]{1,0:T(8,128)(2,1)}, bf16[24,3072]{1,0:T(8,128)(2,1)S(1)}, u32[]{:S(2)}) copy-start(bf16[24,3072]{1,0:T(8,128)(2,1)S(1)} %pad_maximum_fusion.6.refs_8_) | copy-start | bytes 442372
  342.5 16.9 %collective-permute-start.31 = (bf16[24,3072]{1,0:T(8,128)(2,1)S(1)}, bf16[24,3072]{1,0:T(8,128)(2,1)}, u32[]{:S(2)}, u32[]{:S(2)}) collective-permute-start(bf16[24,3072]{1,0:T(8,128)(2,1)S(1)} %pad_maximum_fusion.6.refs_8_), channel_id=1, source_target_pairs={{0,8},{8,0},{16,24},{24,16},{1,9},{9,1},{17,25},{25,17},{2,10},{10... | collective-permute-start | bytes 442376 | tf_op jit(solution)/shard_map/ppermute | solution.py:797
  344.0 18.8 %collective-permute-start.32 = (bf16[24,3072]{1,0:T(8,128)(2,1)S(1)}, bf16[24,3072]{1,0:T(8,128)(2,1)}, u32[]{:S(2)}, u32[]{:S(2)}) collective-permute-start(bf16[24,3072]{1,0:T(8,128)(2,1)S(1)} %pad_maximum_fusion.6.refs_8_), channel_id=1, source_target_pairs={{0,16},{8,24},{16,0},{24,8},{1,17},{9,25},{17,1},{25,9},{2,18},{10... | collective-permute-start | bytes 442376 | tf_op jit(solution)/shard_map/ppermute | solution.py:797
  345.2 41.1 %copy-start.8 = (f32[512,768]{1,0:T(8,128)S(1)}, f32[512,768]{1,0:T(8,128)}, u32[]{:S(2)}) copy-start(f32[512,768]{1,0:T(8,128)} %get-tuple-element.244) | copy-start | bytes 4718596
  346.1 9.7 %collective-permute-start.25 = (bf16[24,704]{1,0:T(8,128)(2,1)S(1)}, bf16[24,704]{1,0:T(8,128)(2,1)S(1)}, u32[]{:S(2)}, u32[]{:S(2)}) collective-permute-start(bf16[24,704]{1,0:T(8,128)(2,1)S(1)} %get-tuple-element.361), channel_id=1, source_target_pairs={{0,2},{1,3},{2,4},{3,5},{4,6},{5,7},{6,0},{7,1},{8,10},{9,11},{10,... | collective-permute-start | bytes 101384 | tf_op jit(solution)/shard_map/ppermute | solution.py:793
  352.1 5.2 %collective-permute-start.26 = (bf16[24,704]{1,0:T(8,128)(2,1)S(1)}, bf16[24,704]{1,0:T(8,128)(2,1)S(1)}, u32[]{:S(2)}, u32[]{:S(2)}) collective-permute-start(bf16[24,704]{1,0:T(8,128)(2,1)S(1)} %get-tuple-element.360), channel_id=1, source_target_pairs={{0,4},{1,5},{2,6},{3,7},{4,0},{5,1},{6,2},{7,3},{8,12},{9,13},{10,... | collective-permute-start | bytes 101384 | tf_op jit(solution)/shard_map/ppermute | solution.py:793
  352.7 6.1 %collective-permute-start.27 = (bf16[24,704]{1,0:T(8,128)(2,1)S(1)}, bf16[24,704]{1,0:T(8,128)(2,1)S(1)}, u32[]{:S(2)}, u32[]{:S(2)}) collective-permute-start(bf16[24,704]{1,0:T(8,128)(2,1)S(1)} %get-tuple-element.359), channel_id=1, source_target_pairs={{0,6},{1,7},{2,0},{3,1},{4,2},{5,3},{6,4},{7,5},{8,14},{9,15},{10,... | collective-permute-start | bytes 101384 | tf_op jit(solution)/shard_map/ppermute | solution.py:793
  355.8 33.0 %copy-start.12 = (bf16[24,3840]{1,0:T(8,128)(2,1)}, bf16[24,3840]{1,0:T(8,128)(2,1)S(1)}, u32[]{:S(2)}) copy-start(bf16[24,3840]{1,0:T(8,128)(2,1)S(1)} %add_convert_fusion.2.refs_0_) | copy-start | bytes 552964
  355.8 7.8 %collective-permute-start.33 = (bf16[24,3072]{1,0:T(8,128)(2,1)S(1)}, bf16[24,3072]{1,0:T(8,128)(2,1)S(1)}, u32[]{:S(2)}, u32[]{:S(2)}) collective-permute-start(bf16[24,3072]{1,0:T(8,128)(2,1)S(1)} %pad_maximum_fusion.6.refs_8_), channel_id=1, source_target_pairs={{0,24},{8,16},{16,8},{24,0},{1,25},{9,17},{17,9},{25,1},{2,26},{10... | collective-permute-start | bytes 442376 | tf_op jit(solution)/shard_map/ppermute | solution.py:797
  357.3 9.7 %collective-permute-start.28 = (bf16[24,3840]{1,0:T(8,128)(2,1)S(1)}, bf16[24,3840]{1,0:T(8,128)(2,1)S(1)}, u32[]{:S(2)}, u32[]{:S(2)}) collective-permute-start(bf16[24,3840]{1,0:T(8,128)(2,1)S(1)} %add_convert_fusion.2.refs_0_), channel_id=1, source_target_pairs={{0,8},{8,0},{16,24},{24,16},{1,9},{9,1},{17,25},{25,17},{2,10},{10... | collective-permute-start | bytes 552968 | tf_op jit(solution)/shard_map/ppermute | solution.py:797
  358.7 8.5 %collective-permute-start.29 = (bf16[24,3840]{1,0:T(8,128)(2,1)S(1)}, bf16[24,3840]{1,0:T(8,128)(2,1)S(1)}, u32[]{:S(2)}, u32[]{:S(2)}) collective-permute-start(bf16[24,3840]{1,0:T(8,128)(2,1)S(1)} %add_convert_fusion.2.refs_0_), channel_id=1, source_target_pairs={{0,16},{8,24},{16,0},{24,8},{1,17},{9,25},{17,1},{25,9},{2,18},{10... | collective-permute-start | bytes 552968 | tf_op jit(solution)/shard_map/ppermute | solution.py:797
  359.4 9.9 %collective-permute-start.30 = (bf16[24,3840]{1,0:T(8,128)(2,1)S(1)}, bf16[24,3840]{1,0:T(8,128)(2,1)S(1)}, u32[]{:S(2)}, u32[]{:S(2)}) collective-permute-start(bf16[24,3840]{1,0:T(8,128)(2,1)S(1)} %add_convert_fusion.2.refs_0_), channel_id=1, source_target_pairs={{0,24},{8,16},{16,8},{24,0},{1,25},{9,17},{17,9},{25,1},{2,26},{10... | collective-permute-start | bytes 552968 | tf_op jit(solution)/shard_map/ppermute | solution.py:797
  378.2 11.1 %collective-permute-start.34 = (bf16[24,2432]{1,0:T(8,128)(2,1)S(1)}, bf16[24,2432]{1,0:T(8,128)(2,1)S(1)}, u32[]{:S(2)}, u32[]{:S(2)}) collective-permute-start(bf16[24,2432]{1,0:T(8,128)(2,1)S(1)} %concatenate.96.refs_4_), channel_id=1, source_target_pairs={{0,8},{8,0},{16,24},{24,16},{1,9},{9,1},{17,25},{25,17},{2,10},{10... | collective-permute-start | bytes 350216 | tf_op jit(solution)/shard_map/ppermute | solution.py:797
  379.6 9.7 %collective-permute-start.35 = (bf16[24,2432]{1,0:T(8,128)(2,1)S(1)}, bf16[24,2432]{1,0:T(8,128)(2,1)S(1)}, u32[]{:S(2)}, u32[]{:S(2)}) collective-permute-start(bf16[24,2432]{1,0:T(8,128)(2,1)S(1)} %concatenate.96.refs_4_), channel_id=1, source_target_pairs={{0,16},{8,24},{16,0},{24,8},{1,17},{9,25},{17,1},{25,9},{2,18},{10... | collective-permute-start | bytes 350216 | tf_op jit(solution)/shard_map/ppermute | solution.py:797
  380.1 9.2 %collective-permute-start.36 = (bf16[24,2432]{1,0:T(8,128)(2,1)S(1)}, bf16[24,2432]{1,0:T(8,128)(2,1)S(1)}, u32[]{:S(2)}, u32[]{:S(2)}) collective-permute-start(bf16[24,2432]{1,0:T(8,128)(2,1)S(1)} %concatenate.96.refs_4_), channel_id=1, source_target_pairs={{0,24},{8,16},{16,8},{24,0},{1,25},{9,17},{17,9},{25,1},{2,26},{10... | collective-permute-start | bytes 350216 | tf_op jit(solution)/shard_map/ppermute | solution.py:797
  (33 other events, 185.1 us)
Sparse Core Ops, SparseCore 0:
  9.7 73.0 all-gather.2
  101.4 67.2 all-gather.4
  212.9 54.0 reduce-scatter.4
  269.1 80.0 reduce-scatter.2

commit v2 on v1

--- a/solution.py
+++ b/solution.py
@@ -1061,92 +1061,127 @@
     )
 
 
-def weight_kernel(
-    core_ref, weights_ref, low_ref, hidden_ref, mixed_ref, branch_ref, active_ref, down_grad_ref,
-    w_down_ref, b_down_ref, middle_ref, mix_ref, cotangent_ref,
-    own_ref, other_ref, down_ref, layer_ref, depth_ref, full_ref, turned_ref, total_ref,
+def down_kernel(
+    weights_ref, active_ref, down_grad_ref, w_down_ref, b_down_ref, middle_ref, mix_ref,
+    cotangent_ref, down_ref, layer_ref, depth_ref, total_ref,
 ):
     step = pl.program_id(0)
-    core = core_ref[0]
-    owners, part, _ = own_ref.shape
 
     @pl.when(step == 0)
     def _():
-        turned_ref[...] = jnp.transpose(low_ref[...].astype(F32)).astype(BF16)
         total_ref[...] = middle_ref[...] + b_down_ref[...]
 
-    @pl.when(step < pl.num_programs(0) - 1)
-    def _():
-        full_ref[...] = contract(turned_ref[...], hidden_ref[...], 1, 0).astype(BF16)
-        total_ref[...] += contract(active_ref[...], w_down_ref[...], 1, 0)
-        down_ref[...] = contract(active_ref[...], down_grad_ref[...], 0, 0).astype(BF16)
+    total_ref[...] += contract(active_ref[...], w_down_ref[...], 1, 0)
+    down_ref[...] = contract(active_ref[...], down_grad_ref[...], 0, 0).astype(BF16)
 
     @pl.when(step == pl.num_programs(0) - 1)
     def _():
-        product = 0.0
-        for half in range(2):
-            mixed = jnp.concatenate(
-                [mixed_ref[2 * z + (core ^ half)] for z in range(owners)], axis=0
-            )
-            rows = slice(half * BLOCK, (half + 1) * BLOCK)
-            product = product + contract(mixed, branch_ref[rows, :], 1, 0)
-        full_ref[...] = product.astype(BF16)
         result = total_ref[...]
         layer_ref[...] = weights_ref[4] * result + mix_ref[...]
         depth = (result * cotangent_ref[...]).reshape(-1, 8, result.shape[1])
         depth_ref[...] = jnp.sum(depth, axis=0)
 
-    for z in range(owners):
-        for side, ref in ((0, own_ref), (1, other_ref)):
-            start = pl.multiple_of((2 * z + (core ^ side)) * part, part)
-            ref[z] = full_ref[pl.ds(start, part), :]
-
-
-def weight_sums(
-    core, depth_weights, low, hidden, mixed, branch, active, down_grad, w_down, b_down, middle,
-    mix, cotangent,
-):
-    rows, model_width = low.shape
-    owners = mixed.shape[0] // 2
-    part = model_width // (2 * owners)
-    steps = hidden.shape[1] // model_width
+
+def down_part(depth_weights, active, down_grad, w_down, b_down, middle, mix, cotangent):
+    rows, model_width = middle.shape
+    steps = active.shape[1] // model_width
     whole = lambda value: pl.BlockSpec(value.shape, lambda j, *_: (0,) * value.ndim)
-    chunk = pl.BlockSpec((rows, model_width), lambda j, *_: (0, jnp.minimum(j, steps - 1)))
-    square = pl.BlockSpec(
-        (model_width, model_width), lambda j, *_: (jnp.minimum(j, steps - 1), 0)
-    )
-    target = pl.BlockSpec((owners, part, model_width), lambda j, *_: (0, 0, j))
-    shape = jax.ShapeDtypeStruct((owners, part, (steps + 1) * model_width), BF16)
+    square = pl.BlockSpec((model_width, model_width), lambda j, *_: (j, 0))
     depth = jax.ShapeDtypeStruct((8, model_width), F32)
     return pl.pallas_call(
-        weight_kernel,
-        name="weight_sums",
+        down_kernel,
+        name="down_part",
         grid_spec=pltpu.PrefetchScalarGridSpec(
-            num_scalar_prefetch=2,
-            grid=(steps + 1,),
+            num_scalar_prefetch=1,
+            grid=(steps,),
             in_specs=[
-                whole(low), chunk, whole(mixed), whole(branch), chunk, whole(down_grad),
-                square, whole(b_down), whole(middle), whole(mix), whole(cotangent),
+                pl.BlockSpec((rows, model_width), lambda j, *_: (0, j)),
+                whole(down_grad), square, whole(b_down), whole(middle), whole(mix),
+                whole(cotangent),
             ],
-            out_specs=[target, target, square, whole(middle), whole(depth)],
-            scratch_shapes=[
-                pltpu.VMEM((model_width, model_width), BF16),
-                pltpu.VMEM((model_width, rows), BF16),
-                pltpu.VMEM((rows, model_width), F32),
-            ],
+            out_specs=[square, whole(middle), whole(depth)],
+            scratch_shapes=[pltpu.VMEM((rows, model_width), F32)],
         ),
         out_shape=[
-            shape,
-            shape,
             jax.ShapeDtypeStruct((steps * model_width, model_width), BF16),
             jax.ShapeDtypeStruct(middle.shape, F32),
             depth,
         ],
         compiler_params=pltpu.CompilerParams(vmem_limit_bytes=VMEM_LIMIT),
-    )(
-        core, depth_weights, low, hidden, mixed, branch, active, down_grad, w_down, b_down,
-        middle, mix, cotangent,
-    )
+    )(depth_weights, active, down_grad, w_down, b_down, middle, mix, cotangent)
+
+
+def pair_kernel(
+    core_ref, low_ref, hidden_ref, mixed_ref, branch_ref,
+    low_twin_ref, hidden_twin_ref, mixed_twin_ref, branch_twin_ref,
+    own_ref, turned_ref, rows_ref,
+):
+    step = pl.program_id(0)
+    core = core_ref[0]
+    owners, part, width = own_ref.shape
+    last = pl.num_programs(0) - 1
+
+    @pl.when(step == 0)
+    def _():
+        for side, ref in ((0, low_ref), (1, low_twin_ref)):
+            turned_ref[...] = jnp.transpose(ref[...].astype(F32)).astype(BF16)
+            for z in range(owners):
+                start = pl.multiple_of((2 * z + core) * part, part)
+                rows_ref[side, z * part : (z + 1) * part, :] = turned_ref[pl.ds(start, part), :]
+
+    @pl.when(step < last)
+    def _():
+        total = contract(rows_ref[0], hidden_ref[...], 1, 0)
+        total = total + contract(rows_ref[1], hidden_twin_ref[...], 1, 0)
+        own_ref[...] = total.astype(BF16).reshape(owners, part, width)
+
+    @pl.when(step == last)
+    def _():
+        total = 0.0
+        sides = ((core, mixed_ref, branch_ref), (1 - core, mixed_twin_ref, branch_twin_ref))
+        for member, ref, grad_ref in sides:
+            for half in range(2):
+                mixed = jnp.concatenate(
+                    [
+                        ref[
+                            2 * z + (member ^ half),
+                            pl.ds(pl.multiple_of(core * part, part), part),
+                            :,
+                        ]
+                        for z in range(owners)
+                    ],
+                    axis=0,
+                )
+                rows = slice(half * BLOCK, (half + 1) * BLOCK)
+                total = total + contract(mixed, grad_ref[rows, :], 1, 0)
+        own_ref[...] = total.astype(BF16).reshape(owners, part, width)
+
+
+def pair_sums(core, own, twin):
+    low, hidden, mixed, branch = own
+    rows, model_width = low.shape
+    owners = mixed.shape[0] // 2
+    part = model_width // (2 * owners)
+    steps = hidden.shape[1] // model_width
+    whole = lambda value: pl.BlockSpec(value.shape, lambda j, core: (0,) * value.ndim)
+    chunk = pl.BlockSpec((rows, model_width), lambda j, core: (0, jnp.minimum(j, steps - 1)))
+    one_side = [whole(low), chunk, whole(mixed), whole(branch)]
+    return pl.pallas_call(
+        pair_kernel,
+        name="pair_sums",
+        grid_spec=pltpu.PrefetchScalarGridSpec(
+            num_scalar_prefetch=1,
+            grid=(steps + 1,),
+            in_specs=one_side * 2,
+            out_specs=pl.BlockSpec((owners, part, model_width), lambda j, core: (0, 0, j)),
+            scratch_shapes=[
+                pltpu.VMEM((model_width, rows), BF16),
+                pltpu.VMEM((2, owners * part, rows), BF16),
+            ],
+        ),
+        out_shape=jax.ShapeDtypeStruct((owners, part, (steps + 1) * model_width), BF16),
+        compiler_params=pltpu.CompilerParams(vmem_limit_bytes=VMEM_LIMIT),
+    )(core, *own, *twin)
 
 
 def joint_kernel(
@@ -1349,37 +1384,38 @@
     grad_out_b, grad_gain_two, grad_shift_two = (token_sums[i] for i in range(3))
     grad_in_b = grad_in_b[0]
     grad_own = lax.all_to_all(grad_own, "shard", 0, 0)
-    folded, twin, grad_down_w, layer_out, last_depth = weight_sums(
-        core_index, depth_weights, normed_two_low, grad_hidden, mixed_two, branch_grad, active,
-        down_grad, w_down, b_down, middle, mix, cotangent,
-    )
+    pair_own = (normed_two_low, grad_hidden, mixed_two, branch_grad)
+    pair_twin = tuple(swap_core(value) for value in pair_own)
+    grad_down_w, layer_out, last_depth = down_part(
+        depth_weights, active, down_grad, w_down, b_down, middle, mix, cotangent
+    )
+    folded = pair_sums(core_index, pair_own, pair_twin)
     grad_down_b = jnp.sum(down_grad.astype(F32), axis=0)
-    grad_own, folded, twin, grad_down_w, last_depth = lax.optimization_barrier(
-        (grad_own, folded, twin, grad_down_w, last_depth)
+    grad_own, folded, grad_down_w, last_depth = lax.optimization_barrier(
+        (grad_own, folded, grad_down_w, last_depth)
     )
     depth = jnp.concatenate([depth_sums, last_depth[None]], axis=0).sum(axis=(1, 2))
-    twin = swap_core(twin)
+    sent = send_rep(folded)
     down_sums = lax.psum_scatter(grad_down_w, "shard", scatter_dimension=0, tiled=True)
     joint_t, grad_normed = retrace(
         core_index, qt, grad_own, attended, stats, cosine, sine, kv, kt, w_turned
     )
-    joint_t, grad_normed, folded, twin, plain_all, depth = lax.optimization_barrier(
-        (joint_t, grad_normed, folded, twin, plain_all, depth)
+    joint_t, grad_normed, folded, plain_all, depth, *sent = lax.optimization_barrier(
+        (joint_t, grad_normed, folded, plain_all, depth, *sent)
     )
     grad_normed = lax.psum_scatter(
         grad_normed, "shard", scatter_dimension=0, tiled=True
     )
-    folded = add_low(folded, twin)
-    sent = send_rep(folded)
+    folded = join_rep(folded, sent)
 
     own_sums, other_sums, first_sums, joint_sums = joint_part(
         core_index, plain_all, joint_t, w_turned, g_one, s_one
     )
-    own_sums, other_sums, first_sums, joint_sums, *sent = lax.optimization_barrier(
-        (own_sums, other_sums, first_sums, joint_sums, *sent)
-    )
-    folded = join_rep(folded, sent)
     arrived = exchange_owner(folded, owner)
+    own_sums, other_sums, first_sums, joint_sums, *arrived = lax.optimization_barrier(
+        (own_sums, other_sums, first_sums, joint_sums, *arrived)
+    )
+    pair_sum = add_low(*arrived)
     grad_gain_one, grad_shift_one = first_sums[0], first_sums[1]
     joint_sums = joint_sums[0]
 
@@ -1434,9 +1470,8 @@
         )
         for k, (sums, down) in enumerate(zip(sums_parts[1:], down_parts[1:]), 1)
     ]
-    arrived = lax.optimization_barrier((*arrived, *received))
-    arrived, received = arrived[:owners], arrived[owners:]
-    pair_pieces = every_rep(add_low(*arrived))
+    pair_sum, *received = lax.optimization_barrier((pair_sum, *received))
+    pair_pieces = every_rep(pair_sum)
     mixed_sums = add_low(sums_parts[0], *[value[:, :, :columns] for value in received])
     depth_sum = add_ordered(
         [depth_of(value[0]) for value in (sums_parts[0], *received)], lambda k: rep ^ k
@@ -1448,21 +1483,23 @@
     )
     down_pieces = every_rep(jnp.concatenate([down_sums[k] for k in range(owners)], axis=1))
     arrived = exchange_owner(mixed_sums, owner)
-    grad_normed, *arrived = lax.optimization_barrier(
-        (grad_normed, *arrived, *pair_pieces, *down_pieces)
-    )
-    pair_pieces, down_pieces = arrived[owners : 2 * owners], arrived[2 * owners :]
+    arrived = lax.optimization_barrier((*arrived, *pair_pieces, *down_pieces))
+    pair_pieces, down_pieces = arrived[owners : owners + 4], arrived[owners + 4 :]
     arrived = arrived[:owners]
-    grad_depth = add_ordered(
-        [depth_of(value) for value in arrived], lambda k: (owner - k) % owners
-    )
     small = add_low(*[value[:, 3 * width :] for value in arrived])
     by_distance = jnp.stack([value[:, : 3 * width] for value in arrived])
     by_owner = [pick(by_distance, (owner - k) % owners) for k in range(owners)]
+    joint_pieces = every_rep(jnp.concatenate([*by_owner, small], axis=1))
+    depth_sums = [value[mark[0], mark[1] : mark[1] + depth.shape[0]] for value in arrived]
+    grad_normed, *pieces = lax.optimization_barrier((grad_normed, *joint_pieces, *depth_sums))
+    joint_pieces, depth_sums = pieces[:4], pieces[4:]
+    grad_depth = add_ordered(
+        [join_depth(value) for value in depth_sums], lambda k: (owner - k) % owners
+    )
     sum_in, sum_out, sum_qkv, sum_down, *small_outs = unpack(
         lax.axis_index("rep").astype(jnp.int32).reshape(1),
         pair_pieces,
-        every_rep(jnp.concatenate([*by_owner, small], axis=1)),
+        joint_pieces,
         down_pieces,
         (hidden_width, model_width, 3 * width),
         counts,

time: 410 us -> 392 us (0.956)
  other arithmetic: 35.9 us -> 20.7 us
  waiting for transfers between devices: 95.4 us -> 85.2 us
  starting transfers between devices: 52.3 us -> 61.6 us
  local copies, waits for them, and re-layouts: 36.8 us -> 31.6 us
    ppermute x12, waiting for transfers between devices: 30.9 us -> 21 us  [shift_owner(): lax.ppermute(value, 'shard', [(i, (i + step) % groups) for i in range(gro...]
    ppermute x12, starting transfers between devices: 21.8 us -> 29.4 us  [shift_owner(): lax.ppermute(value, 'shard', [(i, (i + step) % groups) for i in range(gro...]
    convert_element_type x7 -> x6, other arithmetic: 8.7 us -> 2.17 us  [add_low(): return total.astype(BF16)]
    pallas_call x1 -> x2, Pallas kernels: 17.7 us -> 21.2 us  [the longest x1 12 us: down_part(): pl.pallas_call(down_kernel, name='down_part', grid_spec=pltpu.PrefetchSca...]
    unnamed x88 -> x74, local copies, waits for them, and re-layouts: 8.52 us -> 6.58 us
  transfers between devices with their start and end apart: 43 -> 46, of which waited for: 18 -> 19; matrix products, arithmetic and copies ran while one was open for 16% -> 13% of each run, Pallas kernels for 34% -> 37%
where the time goes in v2:
time: 392 us; the launch traced here: 385 us
  Pallas kernels  164 us (42%)
  waiting for transfers between devices  85.2 us (22%)
  starting transfers between devices  61.6 us (16%)
  local copies, waits for them, and re-layouts  31.6 us (8%)
  other arithmetic  20.7 us (5%)
  between operations  15.3 us (4%)
  matrix products  6.43 us (2%)
    pallas_call x1, Pallas kernels, retrace(): pl.pallas_call(retrace_kernel, name='retrace', cost_estimate=cost(5 * 2 *...  52.2 us
    ppermute x12, starting transfers between devices, shift_owner(): lax.ppermute(value, 'shard', [(i, (i + step) % groups) for i in range(gro...  29.4 us
    ppermute x18, waiting for transfers between devices, cross_rep(): lax.ppermute(value, 'rep', [(i, i ^ mask) for i in range(lax.axis_size('r...  28.9 us
    pallas_call x1, Pallas kernels, attend(): pl.pallas_call(attend_kernel, name='attend', cost_estimate=cost(2 * 2 * B...  25.9 us
    all_gather x1, waiting for transfers between devices, head_split_device(): tokens = lax.all_gather(block_in, 'shard', axis=0, tiled=True)  22.7 us
    ppermute x18, starting transfers between devices, cross_rep(): lax.ppermute(value, 'rep', [(i, i ^ mask) for i in range(lax.axis_size('r...  21.3 us
    ppermute x12, waiting for transfers between devices, shift_owner(): lax.ppermute(value, 'shard', [(i, (i + step) % groups) for i in range(gro...  21 us
    pallas_call x1, Pallas kernels, middle_part(): pl.pallas_call(middle_kernel, name='middle', cost_estimate=cost(4 * rows...  18.6 us
  transfers between devices with their start and end apart: 46, of which 19 were waited for; matrix products, arithmetic and copies ran while one was open for 13% of the time, Pallas kernels for 37%

profile of v2, /device:TPU:0, one launch (start us, length us, event | category | flops | bytes accessed | tf_op | source)
XLA Modules:
  0.0 385.0 jit_solution(9700803506279896078)
XLA Ops:
  11.9 3.1 collective-permute-start
  15.0 2.6 collective-permute-start.1
  18.9 2.8 collective-permute-done
  21.8 12.3 %collective-permute-done.1 = bf16[104,576]{0,1:T(8,128)(2,1)S(1)} collective-permute-done((bf16[104,576]{0,1:T(8,128)(2,1)S(1)}, bf16[104,576]{0,1:T(8,128)(2,1)S(1)}, u32[]{:S(2)}, u32[]{:S(2)}) %collective-permute-start.1) | collective-permute-done | bytes 119840 | tf_op jit(solution)/shard_map/ppermute | solution.py:793
  35.3 2.8 multiply_sine_fusion
  38.2 2.2 convert_element_type.287
  41.0 7.4 %average.1 = (f32[4,512,768]{2,1,0:T(8,128)}, f32[512,768]{1,0:T(8,128)}, f32[4,8,768]{2,1,0:T(8,128)}) custom-call(f32[5]{0:T(128)} %weights_ref.5, bf16[4,512,768]{2,1,0:T(8,128)(2,1)} %earlier_ref.1, f32[512,768]{1,0:T(8,128)} %cotangent_ref.5), custom_call_target="tpu_custom_call" | custom-call | flops 9437184 | bytes 12582912 | tf_op jit(solution)/shard_map/average/pallas_call | solution.py:464
  49.4 1.6 copy.95
  60.0 22.7 %all-gather.3.cloned.1.call-done.x_ref = bf16[4096,768]{1,0:T(8,128)(2,1)} async-done(((bf16[512,768]{1,0:T(8,128)(2,1)}), bf16[4096,768]{1,0:T(8,128)(2,1)}) %all-gather.3.cloned.1.call-update) | async-done | bytes 6291472 | tf_op jit(solution)/shard_map/all_gather | solution.py:1306
  82.7 2.4 collective-permute-start.5
  85.1 1.6 collective-permute-start.6
  87.6 13.5 %project.1 = (bf16[4096,768]{1,0:T(8,128)(2,1)}, bf16[192,4096]{1,0:T(8,128)(2,1)}, bf16[192,4096]{1,0:T(8,128)(2,1)}, bf16[192,4096]{1,0:T(8,128)(2,1)}, bf16[3,4096,128]{2,1,0:T(8,128)(2,1)}) custom-call(bf16[4096,768]{1,0:T(8,128)(2,1)} %all-gather.3.cloned.1.call-done.x_ref, bf16[576,768]{1,0:T(8,128)(2,1)} %bitcast.187, f32[576,1]{1,0:T(8,128)} %copy.105.bias_ref, ...), custom_call_target="tpu_custom_call" | custom-call | flops 3623878656 | bytes 37748736 | tf_op jit(solution)/shard_map/project/pallas_call | solution.py:410
  101.3 1.6 collective-permute-start.7
  102.9 1.5 collective-permute-start.8
  104.8 25.9 %attend.1 = (bf16[8,192,256]{2,1,0:T(8,128)(2,1)}, f32[8,192,256]{2,1,0:T(8,128)}, f32[8,8,256]{2,1,0:T(8,128)}) custom-call(s32[1]{0:T(128)} %bitcast.core_ref, bf16[192,4096]{1,0:T(8,128)(2,1)} %get-tuple-element.226.qt_ref, bf16[3,4096,128]{2,1,0:T(8,128)(2,1)} %get-tuple-element.227.kv_ref, bf16[192,4096]{1,0:T(8,128)(2,1)} %get-tuple-element.228.vt_ref), custom_call_target="tpu_custom_call" | custom-call | flops 14495514624 | bytes 9437184 | tf_op jit(solution)/shard_map/attend/pallas_call | solution.py:563
  130.7 4.1 %all-to-all-start = ((bf16[8,192,256]{2,1,0:T(8,128)(2,1)}), bf16[8,192,256]{2,1,0:T(8,128)(2,1)S(1)}, u32[]{:S(2)}, u32[]{:S(2)}) async-start(bf16[8,192,256]{2,1,0:T(8,128)(2,1)} %get-tuple-element.229), calls=%async_computation | async-start | bytes 1572864 | tf_op jit(solution)/shard_map/all_to_all | solution.py:1368
  134.8 3.9 %collective-permute-done.8.refs_2_ = bf16[4,128,768]{2,1,0:T(8,128)(2,1)} collective-permute-done((bf16[4,128,768]{2,1,0:T(8,128)(2,1)S(1)}, bf16[4,128,768]{2,1,0:T(8,128)(2,1)}, u32[]{:S(2)}, u32[]{:S(2)}) %collective-permute-start.8) | collective-permute-done | bytes 786464 | tf_op jit(solution)/shard_map/ppermute | solution.py:797
  144.9 9.3 %assemble.1 = (bf16[3072,768]{1,0:T(8,128)(2,1)}, bf16[768,768]{1,0:T(8,128)(2,1)}) custom-call(s32[2]{0:T(128)} %pad_add_fusion.1.place_ref, bf16[4,128,768]{2,1,0:T(8,128)(2,1)} %copy-done.4, bf16[4,128,768]{2,1,0:T(8,128)(2,1)} %collective-permute-done.7.refs_1_, bf16[4,128,768]{2,1,0:T(8,128)(2,1)} %collective-permute-done.8.refs_2_, ...), custom_call_target="tpu_custom_call" | custom-call | tf_op jit(solution)/shard_map/assemble/pallas_call | solution.py:765
  154.2 6.4 %convolution_convert_fusion.grad_ref = bf16[512,3072]{1,0:T(8,128)(2,1)} fusion(bf16[512,768]{1,0:T(8,128)(2,1)S(1)} %multiply_convert_fusion.down_grad_ref, bf16[3072,768]{1,0:T(8,128)(2,1)} %get-tuple-element.237.w_down_ref), kind=kOutput, calls=%fused_computation | convolution fusion | flops 2417491968 | bytes 8650752 | tf_op jit(solution)/shard_map/dot_general | solution.py:361
  160.6 8.2 %all-to-all-done.mixed_ref = bf16[8,192,256]{2,1,0:T(8,128)(2,1)S(1)} async-done(((bf16[8,192,256]{2,1,0:T(8,128)(2,1)}), bf16[8,192,256]{2,1,0:T(8,128)(2,1)S(1)}, u32[]{:S(2)}, u32[]{:S(2)}) %all-to-all-start) | async-done | bytes 786464 | tf_op jit(solution)/shard_map/all_to_all | solution.py:1368
  169.6 18.6 %middle.1 = (f32[512,768]{1,0:T(8,128)}, bf16[512,768]{1,0:T(8,128)(2,1)}, bf16[512,3072]{1,0:T(8,128)(2,1)}, bf16[512,3072]{1,0:T(8,128)(2,1)}, f32[512,768]{1,...) custom-call(s32[1]{0:T(128)} %bitcast.core_ref, ...), custom_call_target="tpu_custom_call" | custom-call | flops 6039797760 | bytes 17301504 | tf_op jit(solution)/shard_map/middle/pallas_call | solution.py:1026
  188.4 4.2 %all-to-all-start.1 = ((bf16[8,192,256]{2,1,0:T(8,128)(2,1)}), bf16[8,192,256]{2,1,0:T(8,128)(2,1)}, u32[]{:S(2)}, u32[]{:S(2)}) async-start(bf16[8,192,256]{2,1,0:T(8,128)(2,1)} %get-tuple-element.247), calls=%async_computation.1 | async-start | bytes 1572864 | tf_op jit(solution)/shard_map/all_to_all | solution.py:1386
  194.5 12.0 %down_part.1 = (bf16[3072,768]{1,0:T(8,128)(2,1)}, f32[512,768]{1,0:T(8,128)}, f32[8,768]{1,0:T(8,128)}) custom-call(f32[5]{0:T(128)} %weights_ref.5, bf16[512,3072]{1,0:T(8,128)(2,1)} %get-tuple-element.242.active_ref, bf16[512,768]{1,0:T(8,128)(2,1)} %copy-done.2, bf16[3072,768]{1,0:T(8,128)(2,1)} %get-tuple-element.237.w_down_ref, ...), custom_call_target="tpu_custom_call" | custom-call | tf_op jit(solution)/shard_map/down_part/pallas_call | solution.py:1091
  206.6 1.7 copy-done.5
  208.3 9.1 %pair_sums.1 = bf16[4,96,3840]{2,1,0:T(8,128)(2,1)} custom-call(s32[1]{0:T(128)} %bitcast.core_ref, bf16[512,768]{1,0:T(8,128)(2,1)} %get-tuple-element.248.low_ref, bf16[512,3072]{1,0:T(8,128)(2,1)} %get-tuple-element.249.hidden_ref, bf16[8,192,256]{2,1,0:T(8,128)(2,1)} %copy-done.7, bf16[512,768]{1,0:T(8,128)(2,1)} %get-tuple-element.250.branch_ref, ...), custom_call_target="tpu_custom_call" | custom-call | tf_op jit(solution)/shard_map/pair_sums/pallas_call | solution.py:1169
  219.5 1.7 dynamic-slice_bitcast_fusion
  221.2 1.5 collective-permute-start.18
  224.8 52.2 %retrace.1 = (bf16[576,4096]{1,0:T(8,128)(2,1)}, bf16[4096,768]{1,0:T(8,128)(2,1)}) custom-call(s32[1]{0:T(128)} %bitcast.core_ref, bf16[192,4096]{1,0:T(8,128)(2,1)} %get-tuple-element.226.qt_ref, bf16[8,192,256]{2,1,0:T(8,128)(2,1)} %all-to-all-done.1.grad_ref, f32[8,192,256]{2,1,0:T(8,128)} %get-tuple-element.254.full_ref, ...), custom_call_target="tpu_custom_call" | custom-call | flops 36238786560 | bytes 11010048 | tf_op jit(solution)/shard_map/retrace/pallas_call | solution.py:687
  278.7 1.7 collective-permute-start.21
  280.4 2.4 collective-permute-start.22
  282.7 1.7 collective-permute-start.23
  284.4 12.4 %joint_part.1 = (bf16[4,96,576]{2,1,0:T(8,128)(2,1)}, bf16[4,96,576]{2,1,0:T(8,128)(2,1)}, f32[8,768]{1,0:T(8,128)}, f32[8,576]{1,0:T(8,128)}) custom-call(s32[1]{0:T(128)} %bitcast.core_ref, bf16[4096,768]{1,0:T(8,128)(2,1)} %get-tuple-element.263.plain_ref, bf16[576,4096]{1,0:T(8,128)(2,1)} %get-tuple-element.264.joint_ref, bf16[576,768]{1,0:T(8,128)(2,1)} %bitcast.189, ...), custom_call_target="tpu_custom_call" | custom-call | tf_op jit(solution)/shard_map/joint_part/pallas_call | solution.py:1234
  297.0 2.7 collective-permute-done.22
  304.8 1.9 collective-permute-done.24
  311.7 2.2 collective-permute-start.27
  315.7 6.9 %collective-permute-done.27 = bf16[4,24,1472]{2,1,0:T(8,128)(2,1)S(1)} collective-permute-done((bf16[4,24,1472]{2,1,0:T(8,128)(2,1)S(1)}, bf16[4,24,1472]{2,1,0:T(8,128)(2,1)S(1)}, u32[]{:S(2)}, u32[]{:S(2)}) %collective-permute-start.27) | collective-permute-done | bytes 282656 | tf_op jit(solution)/shard_map/ppermute | solution.py:797
  322.5 5.5 %collective-permute-done.26 = bf16[4,24,1472]{2,1,0:T(8,128)(2,1)S(1)} collective-permute-done((bf16[4,24,1472]{2,1,0:T(8,128)(2,1)S(1)}, bf16[4,24,1472]{2,1,0:T(8,128)(2,1)S(1)}, u32[]{:S(2)}, u32[]{:S(2)}) %collective-permute-start.26) | collective-permute-done | bytes 282656 | tf_op jit(solution)/shard_map/ppermute | solution.py:797
  331.1 10.2 %collective-permute-start.28 = (bf16[24,704]{1,0:T(8,128)(2,1)S(1)}, bf16[24,704]{1,0:T(8,128)(2,1)S(1)}, u32[]{:S(2)}, u32[]{:S(2)}) collective-permute-start(bf16[24,704]{1,0:T(8,128)(2,1)S(1)} %get-tuple-element.371), channel_id=1, source_target_pairs={{0,2},{1,3},{2,4},{3,5},{4,6},{5,7},{6,0},{7,1},{8,10},{9,11},{10,... | collective-permute-start | bytes 101384 | tf_op jit(solution)/shard_map/ppermute | solution.py:793
  341.3 2.4 collective-permute-start.30
  346.2 1.7 collective-permute-done.29
  349.9 1.6 collective-permute-start.33
  351.5 1.6 collective-permute-done.35.refs_10_
  353.2 2.7 collective-permute-done.31.refs_1_
  355.9 4.3 %collective-permute-done.32.refs_2_ = bf16[24,3840]{1,0:T(8,128)(2,1)S(1)} collective-permute-done((bf16[24,3840]{1,0:T(8,128)(2,1)S(1)}, bf16[24,3840]{1,0:T(8,128)(2,1)S(1)}, u32[]{:S(2)}, u32[]{:S(2)}) %collective-permute-start.32) | collective-permute-done | bytes 184352 | tf_op jit(solution)/shard_map/ppermute | solution.py:797
  364.4 2.1 collective-permute-done.37.refs_5_
  369.3 1.9 fusion.9
  371.2 3.8 unpack.1
  376.3 1.7 fusion.7
  (296 shorter events, 61.4 us)
Async XLA Ops:
  7.2 75.5 %all-gather.3.cloned.1.call-start = ((), (), s32[]{:S(2)}) async-start(), calls=%async_computation.4 | async-start | bytes 7077888 | tf_op jit(solution)/shard_map/all_gather | solution.py:1306
  7.9 160.8 %all-gather.5.cloned.1.call-start = ((), (), s32[]{:S(2)}) async-start(), calls=%async_computation.5 | async-start | bytes 5308416 | tf_op jit(solution)/shard_map/all_gather | solution.py:1364
  11.9 9.9 %collective-permute-start = (bf16[104,576]{0,1:T(8,128)(2,1)S(1)}, bf16[104,576]{0,1:T(8,128)(2,1)S(1)}, u32[]{:S(2)}, u32[]{:S(2)}) collective-permute-start(bf16[104,576]{0,1:T(8,128)(2,1)S(1)} %get-tuple-element.346), channel_id=1, source_target_pairs={{0,2},{1,3},{2,4},{3,5},{4,6},{5,7},{6,0},{7,1},{8,10},{9,11},{10,... | collective-permute-start | bytes 359432 | tf_op jit(solution)/shard_map/ppermute | solution.py:793
  15.0 19.1 %collective-permute-start.1 = (bf16[104,576]{0,1:T(8,128)(2,1)S(1)}, bf16[104,576]{0,1:T(8,128)(2,1)S(1)}, u32[]{:S(2)}, u32[]{:S(2)}) collective-permute-start(bf16[104,576]{0,1:T(8,128)(2,1)S(1)} %get-tuple-element.347), channel_id=1, source_target_pairs={{0,4},{1,5},{2,6},{3,7},{4,0},{5,1},{6,2},{7,3},{8,12},{9,13},{10,... | collective-permute-start | bytes 359432 | tf_op jit(solution)/shard_map/ppermute | solution.py:793
  17.6 16.5 %collective-permute-start.2 = (bf16[104,576]{0,1:T(8,128)(2,1)S(1)}, bf16[104,576]{0,1:T(8,128)(2,1)S(1)}, u32[]{:S(2)}, u32[]{:S(2)}) collective-permute-start(bf16[104,576]{0,1:T(8,128)(2,1)S(1)} %get-tuple-element.348), channel_id=1, source_target_pairs={{0,6},{1,7},{2,0},{3,1},{4,2},{5,3},{6,4},{7,5},{8,14},{9,15},{10,... | collective-permute-start | bytes 359432 | tf_op jit(solution)/shard_map/ppermute | solution.py:793
  35.3 14.1 %collective-permute-start.3 = (bf16[4,104,576]{2,1,0:T(8,128)(2,1)}, bf16[4,104,576]{2,1,0:T(8,128)(2,1)}, u32[]{:S(2)}, u32[]{:S(2)}) collective-permute-start(bf16[4,104,576]{2,1,0:T(8,128)(2,1)} %copy.94), channel_id=1, source_target_pairs={{0,1},{1,0},{2,3},{3,2},{4,5},{5,4},{6,7},{7,6},{8,9},{9,8},{10,11... | collective-permute-start | bytes 1437704 | tf_op jit(solution)/shard_map/ppermute | solution.py:787
  49.4 104.8 %copy-start.2 = (bf16[512,768]{1,0:T(8,128)(2,1)}, bf16[512,768]{1,0:T(8,128)(2,1)S(1)}, u32[]{:S(2)}) copy-start(bf16[512,768]{1,0:T(8,128)(2,1)S(1)} %multiply_convert_fusion.down_grad_ref) | copy-start | bytes 2359300
  82.7 18.4 %collective-permute-start.4 = (bf16[128,768]{1,0:T(8,128)(2,1)S(1)}, bf16[128,768]{1,0:T(8,128)(2,1)S(1)}, u32[]{:S(2)}, u32[]{:S(2)}) collective-permute-start(bf16[128,768]{1,0:T(8,128)(2,1)S(1)} %fusion.17), channel_id=1, source_target_pairs={{0,2},{1,3},{2,4},{3,5},{4,6},{5,7},{6,0},{7,1},{8,10},{9,11},{10,... | collective-permute-start | bytes 589832 | tf_op jit(solution)/shard_map/ppermute | solution.py:793
  82.7 18.4 %collective-permute-start.5 = (bf16[128,768]{1,0:T(8,128)(2,1)S(1)}, bf16[128,768]{1,0:T(8,128)(2,1)S(1)}, u32[]{:S(2)}, u32[]{:S(2)}) collective-permute-start(bf16[128,768]{1,0:T(8,128)(2,1)S(1)} %fusion.17), channel_id=1, source_target_pairs={{0,4},{1,5},{2,6},{3,7},{4,0},{5,1},{6,2},{7,3},{8,12},{9,13},{10,... | collective-permute-start | bytes 589832 | tf_op jit(solution)/shard_map/ppermute | solution.py:793
  85.1 16.0 %collective-permute-start.6 = (bf16[128,768]{1,0:T(8,128)(2,1)S(1)}, bf16[128,768]{1,0:T(8,128)(2,1)S(1)}, u32[]{:S(2)}, u32[]{:S(2)}) collective-permute-start(bf16[128,768]{1,0:T(8,128)(2,1)S(1)} %fusion.17), channel_id=1, source_target_pairs={{0,6},{1,7},{2,0},{3,1},{4,2},{5,3},{6,4},{7,5},{8,14},{9,15},{10,... | collective-permute-start | bytes 589832 | tf_op jit(solution)/shard_map/ppermute | solution.py:793
  101.3 33.5 %collective-permute-start.7 = (bf16[4,128,768]{2,1,0:T(8,128)(2,1)S(1)}, bf16[4,128,768]{2,1,0:T(8,128)(2,1)}, u32[]{:S(2)}, u32[]{:S(2)}) collective-permute-start(bf16[4,128,768]{2,1,0:T(8,128)(2,1)S(1)} %pad_maximum_fusion.refs_0_), channel_id=1, source_target_pairs={{0,8},{8,0},{16,24},{24,16},{1,9},{9,1},{17,25},{25,17},{2,10},{10... | collective-permute-start | bytes 2359304 | tf_op jit(solution)/shard_map/ppermute | solution.py:797
  102.9 35.8 %collective-permute-start.8 = (bf16[4,128,768]{2,1,0:T(8,128)(2,1)S(1)}, bf16[4,128,768]{2,1,0:T(8,128)(2,1)}, u32[]{:S(2)}, u32[]{:S(2)}) collective-permute-start(bf16[4,128,768]{2,1,0:T(8,128)(2,1)S(1)} %pad_maximum_fusion.refs_0_), channel_id=1, source_target_pairs={{0,16},{8,24},{16,0},{24,8},{1,17},{9,25},{17,1},{25,9},{2,18},{10... | collective-permute-start | bytes 2359304 | tf_op jit(solution)/shard_map/ppermute | solution.py:797
  104.4 34.3 %collective-permute-start.9 = (bf16[4,128,768]{2,1,0:T(8,128)(2,1)S(1)}, bf16[4,128,768]{2,1,0:T(8,128)(2,1)}, u32[]{:S(2)}, u32[]{:S(2)}) collective-permute-start(bf16[4,128,768]{2,1,0:T(8,128)(2,1)S(1)} %pad_maximum_fusion.refs_0_), channel_id=1, source_target_pairs={{0,24},{8,16},{16,8},{24,0},{1,25},{9,17},{17,9},{25,1},{2,26},{10... | collective-permute-start | bytes 2359304 | tf_op jit(solution)/shard_map/ppermute | solution.py:797
  130.7 38.1 %all-to-all-start = ((bf16[8,192,256]{2,1,0:T(8,128)(2,1)}), bf16[8,192,256]{2,1,0:T(8,128)(2,1)S(1)}, u32[]{:S(2)}, u32[]{:S(2)}) async-start(bf16[8,192,256]{2,1,0:T(8,128)(2,1)} %get-tuple-element.229), calls=%async_computation | async-start | bytes 1572864 | tf_op jit(solution)/shard_map/all_to_all | solution.py:1368
  138.7 4.4 %collective-permute-start.10 = (bf16[4,128,768]{2,1,0:T(8,128)(2,1)S(1)}, bf16[4,128,768]{2,1,0:T(8,128)(2,1)}, u32[]{:S(2)}, u32[]{:S(2)}) collective-permute-start(bf16[4,128,768]{2,1,0:T(8,128)(2,1)S(1)} %pad_maximum_fusion.refs_0_), channel_id=1, source_target_pairs={{0,1},{1,0},{2,3},{3,2},{4,5},{5,4},{6,7},{7,6},{8,9},{9,8},{10,11... | collective-permute-start | bytes 2359304 | tf_op jit(solution)/shard_map/ppermute | solution.py:787
  138.7 4.4 %collective-permute-start.11 = (bf16[4,128,768]{2,1,0:T(8,128)(2,1)}, bf16[4,128,768]{2,1,0:T(8,128)(2,1)}, u32[]{:S(2)}, u32[]{:S(2)}) collective-permute-start(bf16[4,128,768]{2,1,0:T(8,128)(2,1)} %collective-permute-done.7.refs_1_), channel_id=1, source_target_pairs={{0,1},{1,0},{2,3},{3,2},{4,5},{5,4},{6,7},{7,6},{8,9},{9,8},{10,11... | collective-permute-start | bytes 2359304 | tf_op jit(solution)/shard_map/ppermute | solution.py:787
  139.2 4.6 %collective-permute-start.12 = (bf16[4,128,768]{2,1,0:T(8,128)(2,1)}, bf16[4,128,768]{2,1,0:T(8,128)(2,1)}, u32[]{:S(2)}, u32[]{:S(2)}) collective-permute-start(bf16[4,128,768]{2,1,0:T(8,128)(2,1)} %collective-permute-done.8.refs_2_), channel_id=1, source_target_pairs={{0,1},{1,0},{2,3},{3,2},{4,5},{5,4},{6,7},{7,6},{8,9},{9,8},{10,11... | collective-permute-start | bytes 2359304 | tf_op jit(solution)/shard_map/ppermute | solution.py:787
  139.3 5.6 %collective-permute-start.13 = (bf16[4,128,768]{2,1,0:T(8,128)(2,1)}, bf16[4,128,768]{2,1,0:T(8,128)(2,1)}, u32[]{:S(2)}, u32[]{:S(2)}) collective-permute-start(bf16[4,128,768]{2,1,0:T(8,128)(2,1)} %collective-permute-done.9.refs_3_), channel_id=1, source_target_pairs={{0,1},{1,0},{2,3},{3,2},{4,5},{5,4},{6,7},{7,6},{8,9},{9,8},{10,11... | collective-permute-start | bytes 2359304 | tf_op jit(solution)/shard_map/ppermute | solution.py:787
  188.3 18.3 %collective-permute-start.15 = (bf16[512,3072]{1,0:T(8,128)(2,1)}, bf16[512,3072]{1,0:T(8,128)(2,1)S(1)}, u32[]{:S(2)}, u32[]{:S(2)}) collective-permute-start(bf16[512,3072]{1,0:T(8,128)(2,1)} %get-tuple-element.249.hidden_ref), channel_id=1, source_target_pairs={{0,1},{1,0},{2,3},{3,2},{4,5},{5,4},{6,7},{7,6},{8,9},{9,8},{10,11... | collective-permute-start | bytes 9437192 | tf_op jit(solution)/shard_map/ppermute | solution.py:787
  188.4 29.1 %all-to-all-start.1 = ((bf16[8,192,256]{2,1,0:T(8,128)(2,1)}), bf16[8,192,256]{2,1,0:T(8,128)(2,1)}, u32[]{:S(2)}, u32[]{:S(2)}) async-start(bf16[8,192,256]{2,1,0:T(8,128)(2,1)} %get-tuple-element.247), calls=%async_computation.1 | async-start | bytes 1572864 | tf_op jit(solution)/shard_map/all_to_all | solution.py:1386
  192.6 117.7 %reduce-scatter.5.cloned.1.call-start = ((), (), s32[]{:S(2)}) async-start(), calls=%async_computation.7 | async-start | bytes 5308416 | tf_op jit(solution)/shard_map/reduce_scatter | solution.py:1399
  192.8 13.7 %collective-permute-start.16 = (bf16[8,192,256]{2,1,0:T(8,128)(2,1)}, bf16[8,192,256]{2,1,0:T(8,128)(2,1)}, u32[]{:S(2)}, u32[]{:S(2)}) collective-permute-start(bf16[8,192,256]{2,1,0:T(8,128)(2,1)} %copy-done.7), channel_id=1, source_target_pairs={{0,1},{1,0},{2,3},{3,2},{4,5},{5,4},{6,7},{7,6},{8,9},{9,8},{10,11... | collective-permute-start | bytes 2359304 | tf_op jit(solution)/shard_map/ppermute | solution.py:787
  193.3 13.2 %collective-permute-start.14 = (bf16[512,768]{1,0:T(8,128)(2,1)}, bf16[512,768]{1,0:T(8,128)(2,1)}, u32[]{:S(2)}, u32[]{:S(2)}) collective-permute-start(bf16[512,768]{1,0:T(8,128)(2,1)} %get-tuple-element.248.low_ref), channel_id=1, source_target_pairs={{0,1},{1,0},{2,3},{3,2},{4,5},{5,4},{6,7},{7,6},{8,9},{9,8},{10,11... | collective-permute-start | bytes 2359304 | tf_op jit(solution)/shard_map/ppermute | solution.py:787
  193.4 13.2 %collective-permute-start.17 = (bf16[512,768]{1,0:T(8,128)(2,1)}, bf16[512,768]{1,0:T(8,128)(2,1)}, u32[]{:S(2)}, u32[]{:S(2)}) collective-permute-start(bf16[512,768]{1,0:T(8,128)(2,1)} %get-tuple-element.250.branch_ref), channel_id=1, source_target_pairs={{0,1},{1,0},{2,3},{3,2},{4,5},{5,4},{6,7},{7,6},{8,9},{9,8},{10,11... | collective-permute-start | bytes 2359304 | tf_op jit(solution)/shard_map/ppermute | solution.py:787
  217.5 150.9 %reduce-scatter.3.cloned.1.call-start = ((), (), s32[]{:S(2)}) async-start(), calls=%async_computation.6 | async-start | bytes 7077888 | tf_op jit(solution)/shard_map/reduce_scatter | solution.py:1406
  221.2 55.9 %collective-permute-start.18 = (bf16[4,24,3840]{2,1,0:T(8,128)(2,1)S(1)}, bf16[4,24,3840]{2,1,0:T(8,128)(2,1)S(1)}, u32[]{:S(2)}, u32[]{:S(2)}) collective-permute-start(bf16[4,24,3840]{2,1,0:T(8,128)(2,1)S(1)} %get-tuple-element.336), channel_id=1, source_target_pairs={{0,8},{8,0},{16,24},{24,16},{1,9},{9,1},{17,25},{25,17},{2,10},{10... | collective-permute-start | bytes 2211848 | tf_op jit(solution)/shard_map/ppermute | solution.py:797
  222.8 54.3 %collective-permute-start.19 = (bf16[4,24,3840]{2,1,0:T(8,128)(2,1)S(1)}, bf16[4,24,3840]{2,1,0:T(8,128)(2,1)S(1)}, u32[]{:S(2)}, u32[]{:S(2)}) collective-permute-start(bf16[4,24,3840]{2,1,0:T(8,128)(2,1)S(1)} %get-tuple-element.335), channel_id=1, source_target_pairs={{0,16},{8,24},{16,0},{24,8},{1,17},{9,25},{17,1},{25,9},{2,18},{10... | collective-permute-start | bytes 2211848 | tf_op jit(solution)/shard_map/ppermute | solution.py:797
  224.3 52.8 %collective-permute-start.20 = (bf16[4,24,3840]{2,1,0:T(8,128)(2,1)S(1)}, bf16[4,24,3840]{2,1,0:T(8,128)(2,1)S(1)}, u32[]{:S(2)}, u32[]{:S(2)}) collective-permute-start(bf16[4,24,3840]{2,1,0:T(8,128)(2,1)S(1)} %get-tuple-element.334), channel_id=1, source_target_pairs={{0,24},{8,16},{16,8},{24,0},{1,25},{9,17},{17,9},{25,1},{2,26},{10... | collective-permute-start | bytes 2211848 | tf_op jit(solution)/shard_map/ppermute | solution.py:797
  224.8 52.2 %copy-start.28 = (f32[8,768]{1,0:T(8,128)S(1)}, f32[8,768]{1,0:T(8,128)}, u32[]{:S(2)}) copy-start(f32[8,768]{1,0:T(8,128)} %get-tuple-element.261) | copy-start | bytes 73732
  278.7 18.3 %collective-permute-start.21 = (bf16[24,3840]{1,0:T(8,128)(2,1)S(1)}, bf16[24,3840]{1,0:T(8,128)(2,1)S(1)}, u32[]{:S(2)}, u32[]{:S(2)}) collective-permute-start(bf16[24,3840]{1,0:T(8,128)(2,1)S(1)} %get-tuple-element.351), channel_id=1, source_target_pairs={{0,2},{1,3},{2,4},{3,5},{4,6},{5,7},{6,0},{7,1},{8,10},{9,11},{10,... | collective-permute-start | bytes 552968 | tf_op jit(solution)/shard_map/ppermute | solution.py:793
  280.4 19.3 %collective-permute-start.22 = (bf16[24,3840]{1,0:T(8,128)(2,1)S(1)}, bf16[24,3840]{1,0:T(8,128)(2,1)S(1)}, u32[]{:S(2)}, u32[]{:S(2)}) collective-permute-start(bf16[24,3840]{1,0:T(8,128)(2,1)S(1)} %get-tuple-element.350), channel_id=1, source_target_pairs={{0,4},{1,5},{2,6},{3,7},{4,0},{5,1},{6,2},{7,3},{8,12},{9,13},{10,... | collective-permute-start | bytes 552968 | tf_op jit(solution)/shard_map/ppermute | solution.py:793
  282.7 18.4 %collective-permute-start.23 = (bf16[24,3840]{1,0:T(8,128)(2,1)S(1)}, bf16[24,3840]{1,0:T(8,128)(2,1)S(1)}, u32[]{:S(2)}, u32[]{:S(2)}) collective-permute-start(bf16[24,3840]{1,0:T(8,128)(2,1)S(1)} %get-tuple-element.349), channel_id=1, source_target_pairs={{0,6},{1,7},{2,0},{3,1},{4,2},{5,3},{6,4},{7,5},{8,14},{9,15},{10,... | collective-permute-start | bytes 552968 | tf_op jit(solution)/shard_map/ppermute | solution.py:793
  304.6 2.1 collective-permute-start.24
  311.7 10.9 %collective-permute-start.27 = (bf16[4,24,1472]{2,1,0:T(8,128)(2,1)S(1)}, bf16[4,24,1472]{2,1,0:T(8,128)(2,1)S(1)}, u32[]{:S(2)}, u32[]{:S(2)}) collective-permute-start(bf16[4,24,1472]{2,1,0:T(8,128)(2,1)S(1)} %pad_maximum_fusion.5), channel_id=1, source_target_pairs={{0,24},{8,16},{16,8},{24,0},{1,25},{9,17},{17,9},{25,1},{2,26},{10... | collective-permute-start | bytes 847880 | tf_op jit(solution)/shard_map/ppermute | solution.py:797
  314.0 14.0 %collective-permute-start.26 = (bf16[4,24,1472]{2,1,0:T(8,128)(2,1)S(1)}, bf16[4,24,1472]{2,1,0:T(8,128)(2,1)S(1)}, u32[]{:S(2)}, u32[]{:S(2)}) collective-permute-start(bf16[4,24,1472]{2,1,0:T(8,128)(2,1)S(1)} %pad_maximum_fusion.4), channel_id=1, source_target_pairs={{0,16},{8,24},{16,0},{24,8},{1,17},{9,25},{17,1},{25,9},{2,18},{10... | collective-permute-start | bytes 847880 | tf_op jit(solution)/shard_map/ppermute | solution.py:797
  314.7 13.3 %collective-permute-start.25 = (bf16[4,24,1472]{2,1,0:T(8,128)(2,1)S(1)}, bf16[4,24,1472]{2,1,0:T(8,128)(2,1)S(1)}, u32[]{:S(2)}, u32[]{:S(2)}) collective-permute-start(bf16[4,24,1472]{2,1,0:T(8,128)(2,1)S(1)} %pad_maximum_fusion.3), channel_id=1, source_target_pairs={{0,8},{8,0},{16,24},{24,16},{1,9},{9,1},{17,25},{25,17},{2,10},{10... | collective-permute-start | bytes 847880 | tf_op jit(solution)/shard_map/ppermute | solution.py:797
  328.3 21.6 %collective-permute-start.34 = (bf16[24,3072]{1,0:T(8,128)(2,1)S(1)}, bf16[24,3072]{1,0:T(8,128)(2,1)S(1)}, u32[]{:S(2)}, u32[]{:S(2)}) collective-permute-start(bf16[24,3072]{1,0:T(8,128)(2,1)S(1)} %pad_maximum_fusion.6.refs_8_), channel_id=1, source_target_pairs={{0,8},{8,0},{16,24},{24,16},{1,9},{9,1},{17,25},{25,17},{2,10},{10... | collective-permute-start | bytes 442376 | tf_op jit(solution)/shard_map/ppermute | solution.py:797
  331.1 14.1 %collective-permute-start.28 = (bf16[24,704]{1,0:T(8,128)(2,1)S(1)}, bf16[24,704]{1,0:T(8,128)(2,1)S(1)}, u32[]{:S(2)}, u32[]{:S(2)}) collective-permute-start(bf16[24,704]{1,0:T(8,128)(2,1)S(1)} %get-tuple-element.371), channel_id=1, source_target_pairs={{0,2},{1,3},{2,4},{3,5},{4,6},{5,7},{6,0},{7,1},{8,10},{9,11},{10,... | collective-permute-start | bytes 101384 | tf_op jit(solution)/shard_map/ppermute | solution.py:793
  341.3 6.6 %collective-permute-start.29 = (bf16[24,704]{1,0:T(8,128)(2,1)S(1)}, bf16[24,704]{1,0:T(8,128)(2,1)S(1)}, u32[]{:S(2)}, u32[]{:S(2)}) collective-permute-start(bf16[24,704]{1,0:T(8,128)(2,1)S(1)} %get-tuple-element.370), channel_id=1, source_target_pairs={{0,4},{1,5},{2,6},{3,7},{4,0},{5,1},{6,2},{7,3},{8,12},{9,13},{10,... | collective-permute-start | bytes 101384 | tf_op jit(solution)/shard_map/ppermute | solution.py:793
  341.3 7.2 %collective-permute-start.30 = (bf16[24,704]{1,0:T(8,128)(2,1)S(1)}, bf16[24,704]{1,0:T(8,128)(2,1)S(1)}, u32[]{:S(2)}, u32[]{:S(2)}) collective-permute-start(bf16[24,704]{1,0:T(8,128)(2,1)S(1)} %get-tuple-element.369), channel_id=1, source_target_pairs={{0,6},{1,7},{2,0},{3,1},{4,2},{5,3},{6,4},{7,5},{8,14},{9,15},{10,... | collective-permute-start | bytes 101384 | tf_op jit(solution)/shard_map/ppermute | solution.py:793
  344.1 9.1 %collective-permute-start.35 = (bf16[24,3072]{1,0:T(8,128)(2,1)S(1)}, bf16[24,3072]{1,0:T(8,128)(2,1)S(1)}, u32[]{:S(2)}, u32[]{:S(2)}) collective-permute-start(bf16[24,3072]{1,0:T(8,128)(2,1)S(1)} %pad_maximum_fusion.6.refs_8_), channel_id=1, source_target_pairs={{0,16},{8,24},{16,0},{24,8},{1,17},{9,25},{17,1},{25,9},{2,18},{10... | collective-permute-start | bytes 442376 | tf_op jit(solution)/shard_map/ppermute | solution.py:797
  345.1 8.0 %collective-permute-start.36 = (bf16[24,3072]{1,0:T(8,128)(2,1)S(1)}, bf16[24,3072]{1,0:T(8,128)(2,1)S(1)}, u32[]{:S(2)}, u32[]{:S(2)}) collective-permute-start(bf16[24,3072]{1,0:T(8,128)(2,1)S(1)} %pad_maximum_fusion.6.refs_8_), channel_id=1, source_target_pairs={{0,24},{8,16},{16,8},{24,0},{1,25},{9,17},{17,9},{25,1},{2,26},{10... | collective-permute-start | bytes 442376 | tf_op jit(solution)/shard_map/ppermute | solution.py:797
  347.9 8.0 %collective-permute-start.31 = (bf16[24,3840]{1,0:T(8,128)(2,1)S(1)}, bf16[24,3840]{1,0:T(8,128)(2,1)S(1)}, u32[]{:S(2)}, u32[]{:S(2)}) collective-permute-start(bf16[24,3840]{1,0:T(8,128)(2,1)S(1)} %add_convert_fusion.1.refs_0_), channel_id=1, source_target_pairs={{0,8},{8,0},{16,24},{24,16},{1,9},{9,1},{17,25},{25,17},{2,10},{10... | collective-permute-start | bytes 552968 | tf_op jit(solution)/shard_map/ppermute | solution.py:797
  348.5 11.7 %collective-permute-start.32 = (bf16[24,3840]{1,0:T(8,128)(2,1)S(1)}, bf16[24,3840]{1,0:T(8,128)(2,1)S(1)}, u32[]{:S(2)}, u32[]{:S(2)}) collective-permute-start(bf16[24,3840]{1,0:T(8,128)(2,1)S(1)} %add_convert_fusion.1.refs_0_), channel_id=1, source_target_pairs={{0,16},{8,24},{16,0},{24,8},{1,17},{9,25},{17,1},{25,9},{2,18},{10... | collective-permute-start | bytes 552968 | tf_op jit(solution)/shard_map/ppermute | solution.py:797
  349.9 10.3 %collective-permute-start.33 = (bf16[24,3840]{1,0:T(8,128)(2,1)S(1)}, bf16[24,3840]{1,0:T(8,128)(2,1)S(1)}, u32[]{:S(2)}, u32[]{:S(2)}) collective-permute-start(bf16[24,3840]{1,0:T(8,128)(2,1)S(1)} %add_convert_fusion.1.refs_0_), channel_id=1, source_target_pairs={{0,24},{8,16},{16,8},{24,0},{1,25},{9,17},{17,9},{25,1},{2,26},{10... | collective-permute-start | bytes 552968 | tf_op jit(solution)/shard_map/ppermute | solution.py:797
  360.5 6.0 %collective-permute-start.37 = (bf16[24,2432]{1,0:T(8,128)(2,1)S(1)}, bf16[24,2432]{1,0:T(8,128)(2,1)S(1)}, u32[]{:S(2)}, u32[]{:S(2)}) collective-permute-start(bf16[24,2432]{1,0:T(8,128)(2,1)S(1)} %concatenate.96.refs_4_), channel_id=1, source_target_pairs={{0,8},{8,0},{16,24},{24,16},{1,9},{9,1},{17,25},{25,17},{2,10},{10... | collective-permute-start | bytes 350216 | tf_op jit(solution)/shard_map/ppermute | solution.py:797
  361.3 6.0 %collective-permute-start.38 = (bf16[24,2432]{1,0:T(8,128)(2,1)S(1)}, bf16[24,2432]{1,0:T(8,128)(2,1)S(1)}, u32[]{:S(2)}, u32[]{:S(2)}) collective-permute-start(bf16[24,2432]{1,0:T(8,128)(2,1)S(1)} %concatenate.96.refs_4_), channel_id=1, source_target_pairs={{0,16},{8,24},{16,0},{24,8},{1,17},{9,25},{17,1},{25,9},{2,18},{10... | collective-permute-start | bytes 350216 | tf_op jit(solution)/shard_map/ppermute | solution.py:797
  362.7 5.7 %collective-permute-start.39 = (bf16[24,2432]{1,0:T(8,128)(2,1)S(1)}, bf16[24,2432]{1,0:T(8,128)(2,1)S(1)}, u32[]{:S(2)}, u32[]{:S(2)}) collective-permute-start(bf16[24,2432]{1,0:T(8,128)(2,1)S(1)} %concatenate.96.refs_4_), channel_id=1, source_target_pairs={{0,24},{8,16},{16,8},{24,0},{1,25},{9,17},{17,9},{25,1},{2,26},{10... | collective-permute-start | bytes 350216 | tf_op jit(solution)/shard_map/ppermute | solution.py:797
  (29 other events, 306.2 us)
Sparse Core Ops, SparseCore 0:
  9.7 73.0 all-gather.2
  101.4 67.2 all-gather.4
  217.6 55.9 reduce-scatter.4
  277.2 80.0 reduce-scatter.2

commit v3 on v2

--- a/solution.py
+++ b/solution.py
@@ -1061,9 +1061,30 @@
     )
 
 
-def down_kernel(
-    weights_ref, active_ref, down_grad_ref, w_down_ref, b_down_ref, middle_ref, mix_ref,
-    cotangent_ref, down_ref, layer_ref, depth_ref, total_ref,
+def down_kernel(active_ref, down_grad_ref, down_ref):
+    down_ref[...] = contract(active_ref[...], down_grad_ref[...], 0, 0).astype(BF16)
+
+
+def down_part(active, down_grad):
+    rows, model_width = down_grad.shape
+    steps = active.shape[1] // model_width
+    return pl.pallas_call(
+        down_kernel,
+        name="down_part",
+        grid=(steps,),
+        in_specs=[
+            pl.BlockSpec((rows, model_width), lambda j: (0, j)),
+            pl.BlockSpec((rows, model_width), lambda j: (0, 0)),
+        ],
+        out_specs=pl.BlockSpec((model_width, model_width), lambda j: (j, 0)),
+        out_shape=jax.ShapeDtypeStruct((steps * model_width, model_width), BF16),
+        compiler_params=pltpu.CompilerParams(vmem_limit_bytes=VMEM_LIMIT),
+    )(active, down_grad)
+
+
+def result_kernel(
+    weights_ref, active_ref, w_down_ref, b_down_ref, middle_ref, mix_ref, cotangent_ref,
+    layer_ref, depth_ref, total_ref,
 ):
     step = pl.program_id(0)
 
@@ -1072,7 +1093,6 @@
         total_ref[...] = middle_ref[...] + b_down_ref[...]
 
     total_ref[...] += contract(active_ref[...], w_down_ref[...], 1, 0)
-    down_ref[...] = contract(active_ref[...], down_grad_ref[...], 0, 0).astype(BF16)
 
     @pl.when(step == pl.num_programs(0) - 1)
     def _():
@@ -1082,33 +1102,28 @@
         depth_ref[...] = jnp.sum(depth, axis=0)
 
 
-def down_part(depth_weights, active, down_grad, w_down, b_down, middle, mix, cotangent):
+def result_part(depth_weights, active, w_down, b_down, middle, mix, cotangent):
     rows, model_width = middle.shape
     steps = active.shape[1] // model_width
     whole = lambda value: pl.BlockSpec(value.shape, lambda j, *_: (0,) * value.ndim)
-    square = pl.BlockSpec((model_width, model_width), lambda j, *_: (j, 0))
     depth = jax.ShapeDtypeStruct((8, model_width), F32)
     return pl.pallas_call(
-        down_kernel,
-        name="down_part",
+        result_kernel,
+        name="result_part",
         grid_spec=pltpu.PrefetchScalarGridSpec(
             num_scalar_prefetch=1,
             grid=(steps,),
             in_specs=[
                 pl.BlockSpec((rows, model_width), lambda j, *_: (0, j)),
-                whole(down_grad), square, whole(b_down), whole(middle), whole(mix),
-                whole(cotangent),
+                pl.BlockSpec((model_width, model_width), lambda j, *_: (j, 0)),
+                whole(b_down), whole(middle), whole(mix), whole(cotangent),
             ],
-            out_specs=[square, whole(middle), whole(depth)],
+            out_specs=[whole(middle), whole(depth)],
             scratch_shapes=[pltpu.VMEM((rows, model_width), F32)],
         ),
-        out_shape=[
-            jax.ShapeDtypeStruct((steps * model_width, model_width), BF16),
-            jax.ShapeDtypeStruct(middle.shape, F32),
-            depth,
-        ],
+        out_shape=[jax.ShapeDtypeStruct(middle.shape, F32), depth],
         compiler_params=pltpu.CompilerParams(vmem_limit_bytes=VMEM_LIMIT),
-    )(depth_weights, active, down_grad, w_down, b_down, middle, mix, cotangent)
+    )(depth_weights, active, w_down, b_down, middle, mix, cotangent)
 
 
 def pair_kernel(
@@ -1386,22 +1401,17 @@
     grad_own = lax.all_to_all(grad_own, "shard", 0, 0)
     pair_own = (normed_two_low, grad_hidden, mixed_two, branch_grad)
     pair_twin = tuple(swap_core(value) for value in pair_own)
-    grad_down_w, layer_out, last_depth = down_part(
-        depth_weights, active, down_grad, w_down, b_down, middle, mix, cotangent
-    )
+    grad_down_w = down_part(active, down_grad)
     folded = pair_sums(core_index, pair_own, pair_twin)
     grad_down_b = jnp.sum(down_grad.astype(F32), axis=0)
-    grad_own, folded, grad_down_w, last_depth = lax.optimization_barrier(
-        (grad_own, folded, grad_down_w, last_depth)
-    )
-    depth = jnp.concatenate([depth_sums, last_depth[None]], axis=0).sum(axis=(1, 2))
+    grad_own, folded, grad_down_w = lax.optimization_barrier((grad_own, folded, grad_down_w))
     sent = send_rep(folded)
     down_sums = lax.psum_scatter(grad_down_w, "shard", scatter_dimension=0, tiled=True)
     joint_t, grad_normed = retrace(
         core_index, qt, grad_own, attended, stats, cosine, sine, kv, kt, w_turned
     )
-    joint_t, grad_normed, folded, plain_all, depth, *sent = lax.optimization_barrier(
-        (joint_t, grad_normed, folded, plain_all, depth, *sent)
+    joint_t, grad_normed, folded, plain_all, active, *sent = lax.optimization_barrier(
+        (joint_t, grad_normed, folded, plain_all, active, *sent)
     )
     grad_normed = lax.psum_scatter(
         grad_normed, "shard", scatter_dimension=0, tiled=True
@@ -1412,8 +1422,13 @@
         core_index, plain_all, joint_t, w_turned, g_one, s_one
     )
     arrived = exchange_owner(folded, owner)
-    own_sums, other_sums, first_sums, joint_sums, *arrived = lax.optimization_barrier(
-        (own_sums, other_sums, first_sums, joint_sums, *arrived)
+    layer_out, last_depth = result_part(
+        depth_weights, active, w_down, b_down, middle, mix, cotangent
+    )
+    own_sums, other_sums, first_sums, joint_sums, last_depth, *arrived = (
+        lax.optimization_barrier(
+            (own_sums, other_sums, first_sums, joint_sums, last_depth, *arrived)
+        )
     )
     pair_sum = add_low(*arrived)
     grad_gain_one, grad_shift_one = first_sums[0], first_sums[1]
@@ -1442,16 +1457,12 @@
         axis=1,
     )
     small = jnp.pad(small, ((0, 0), (0, part - small.shape[1]), (0, 128 - part)))
-    depth = split_depth(depth)
     mark = (part // 4 - 8, 3 * width)
-    marked = jnp.zeros((4, part // 4, 128), BF16).at[:, mark[0], : depth.shape[0]].set(depth)
-    small = small + marked.reshape(1, part, 128)
     small = small.reshape(owners, 2, part, 128)
-    depth_of = lambda value: join_depth(
-        value[mark[0], mark[1] : mark[1] + depth.shape[0]]
-    )
+    depth_count = 2 * depth_weights.shape[0]
+    depth_row = lambda value: value[mark[0], mark[1] : mark[1] + depth_count]
     with_depth = lambda value, sums: value.at[
-        :, mark[0], mark[1] : mark[1] + depth.shape[0]
+        :, mark[0], mark[1] : mark[1] + depth_count
     ].set(split_depth(sums))
     received = swap_core(
         jnp.concatenate([other_sums, pick(small, 1 - core, 1)], axis=2)
@@ -1459,7 +1470,7 @@
     mixed_sums = add_low(
         jnp.concatenate([own_sums, pick(small, core, 1)], axis=2), received
     )
-    depth_sum = join_depth(depth) + depth_of(received[0])
+    depth_sum = jnp.concatenate([depth_sums, last_depth[None]], axis=0).sum(axis=(1, 2))
     down_parts = pick_parts(down_sums[None])
     down_rows = part // 4
     columns = 3 * width + 128
@@ -1474,7 +1485,7 @@
     pair_pieces = every_rep(pair_sum)
     mixed_sums = add_low(sums_parts[0], *[value[:, :, :columns] for value in received])
     depth_sum = add_ordered(
-        [depth_of(value[0]) for value in (sums_parts[0], *received)], lambda k: rep ^ k
+        [join_depth(depth_row(value[0])) for value in (sums_parts[0], *received)], lambda k: rep ^ k
     )
     mixed_sums = with_depth(mixed_sums, depth_sum)
     down_sums = add_low(
@@ -1490,12 +1501,13 @@
     by_distance = jnp.stack([value[:, : 3 * width] for value in arrived])
     by_owner = [pick(by_distance, (owner - k) % owners) for k in range(owners)]
     joint_pieces = every_rep(jnp.concatenate([*by_owner, small], axis=1))
-    depth_sums = [value[mark[0], mark[1] : mark[1] + depth.shape[0]] for value in arrived]
+    depth_sums = [depth_row(value) for value in arrived]
     grad_normed, *pieces = lax.optimization_barrier((grad_normed, *joint_pieces, *depth_sums))
     joint_pieces, depth_sums = pieces[:4], pieces[4:]
     grad_depth = add_ordered(
         [join_depth(value) for value in depth_sums], lambda k: (owner - k) % owners
     )
+    grad_depth = grad_depth + swap_core(grad_depth)
     sum_in, sum_out, sum_qkv, sum_down, *small_outs = unpack(
         lax.axis_index("rep").astype(jnp.int32).reshape(1),
         pair_pieces,
@@ -1504,7 +1516,7 @@
         (hidden_width, model_width, 3 * width),
         counts,
     )
-    small_outs = [value[0] for value in small_outs]
+    small_outs = [value.reshape(-1) for value in small_outs]
     grad_normed = grad_normed.astype(F32)
     center = inputs - jnp.mean(inputs, axis=-1, keepdims=True)
     scale = lax.rsqrt(jnp.mean(center * center, axis=-1, keepdims=True) + EPSILON)

time: 392 us -> 385 us (0.982)
  starting transfers between devices: 61.6 us -> 54.3 us
  Pallas kernels: 164 us -> 168 us
    ppermute x12, starting transfers between devices: 29.4 us -> 21 us  [shift_owner(): lax.ppermute(value, 'shard', [(i, (i + step) % groups) for i in range(gro...]
    ppermute x12, waiting for transfers between devices: 21 us -> 17 us  [shift_owner(): lax.ppermute(value, 'shard', [(i, (i + step) % groups) for i in range(gro...]
    pallas_call x1 -> x2, Pallas kernels: 12 us -> 15.9 us  [the longest x1 9.36 us: result_part(): pl.pallas_call(result_kernel, name='result_part', grid_spec=pltpu.Prefetc...]
  transfers between devices with their start and end apart: 46 -> 47, of which waited for: 19 -> 21; matrix products, arithmetic and copies ran while one was open for 13% -> 13% of each run, Pallas kernels for 37% -> 40%
where the time goes in v3:
time: 385 us; the launch traced here: 378 us
  Pallas kernels  168 us (44%)
  waiting for transfers between devices  81.6 us (21%)
  starting transfers between devices  54.3 us (14%)
  local copies, waits for them, and re-layouts  31.9 us (8%)
  other arithmetic  19.7 us (5%)
  between operations  15.3 us (4%)
  matrix products  6.42 us (2%)
    pallas_call x1, Pallas kernels, retrace(): pl.pallas_call(retrace_kernel, name='retrace', cost_estimate=cost(5 * 2 *...  52.5 us
    ppermute x18, waiting for transfers between devices, cross_rep(): lax.ppermute(value, 'rep', [(i, i ^ mask) for i in range(lax.axis_size('r...  27.2 us
    pallas_call x1, Pallas kernels, attend(): pl.pallas_call(attend_kernel, name='attend', cost_estimate=cost(2 * 2 * B...  25.9 us
    all_gather x1, waiting for transfers between devices, head_split_device(): tokens = lax.all_gather(block_in, 'shard', axis=0, tiled=True)  21.9 us
    ppermute x18, starting transfers between devices, cross_rep(): lax.ppermute(value, 'rep', [(i, i ^ mask) for i in range(lax.axis_size('r...  21.5 us
    ppermute x12, starting transfers between devices, shift_owner(): lax.ppermute(value, 'shard', [(i, (i + step) % groups) for i in range(gro...  21 us
    pallas_call x1, Pallas kernels, middle_part(): pl.pallas_call(middle_kernel, name='middle', cost_estimate=cost(4 * rows...  18.6 us
    ppermute x12, waiting for transfers between devices, shift_owner(): lax.ppermute(value, 'shard', [(i, (i + step) % groups) for i in range(gro...  17 us
  transfers between devices with their start and end apart: 47, of which 21 were waited for; matrix products, arithmetic and copies ran while one was open for 13% of the time, Pallas kernels for 40%

profile of v3, /device:TPU:0, one launch (start us, length us, event | category | flops | bytes accessed | tf_op | source)
XLA Modules:
  0.0 377.7 jit_solution(13463643276122991197)
XLA Ops:
  11.9 3.1 collective-permute-start
  15.0 2.6 collective-permute-start.1
  17.6 1.3 collective-permute-start.2
  18.9 2.8 collective-permute-done
  21.8 12.3 %collective-permute-done.1 = bf16[104,576]{0,1:T(8,128)(2,1)S(1)} collective-permute-done((bf16[104,576]{0,1:T(8,128)(2,1)S(1)}, bf16[104,576]{0,1:T(8,128)(2,1)S(1)}, u32[]{:S(2)}, u32[]{:S(2)}) %collective-permute-start.1) | collective-permute-done | bytes 119840 | tf_op jit(solution)/shard_map/ppermute | solution.py:793
  35.3 2.8 multiply_sine_fusion
  39.6 1.4 convert_element_type.274
  41.0 7.5 %average.1 = (f32[4,512,768]{2,1,0:T(8,128)}, f32[512,768]{1,0:T(8,128)}, f32[4,8,768]{2,1,0:T(8,128)}) custom-call(f32[5]{0:T(128)} %weights_ref.5, bf16[4,512,768]{2,1,0:T(8,128)(2,1)} %earlier_ref.1, f32[512,768]{1,0:T(8,128)} %cotangent_ref.5), custom_call_target="tpu_custom_call" | custom-call | flops 9437184 | bytes 12582912 | tf_op jit(solution)/shard_map/average/pallas_call | solution.py:464
  49.5 1.6 copy.95
  60.8 21.9 %all-gather.3.cloned.1.call-done.x_ref = bf16[4096,768]{1,0:T(8,128)(2,1)} async-done(((bf16[512,768]{1,0:T(8,128)(2,1)}), bf16[4096,768]{1,0:T(8,128)(2,1)}) %all-gather.3.cloned.1.call-update) | async-done | bytes 6291472 | tf_op jit(solution)/shard_map/all_gather | solution.py:1321
  82.7 1.8 collective-permute-start.6
  86.1 13.5 %project.1 = (bf16[4096,768]{1,0:T(8,128)(2,1)}, bf16[192,4096]{1,0:T(8,128)(2,1)}, bf16[192,4096]{1,0:T(8,128)(2,1)}, bf16[192,4096]{1,0:T(8,128)(2,1)}, bf16[3,4096,128]{2,1,0:T(8,128)(2,1)}) custom-call(bf16[4096,768]{1,0:T(8,128)(2,1)} %all-gather.3.cloned.1.call-done.x_ref, bf16[576,768]{1,0:T(8,128)(2,1)} %bitcast.179, f32[576,1]{1,0:T(8,128)} %copy.105.bias_ref, ...), custom_call_target="tpu_custom_call" | custom-call | flops 3623878656 | bytes 37748736 | tf_op jit(solution)/shard_map/project/pallas_call | solution.py:410
  100.8 2.5 collective-permute-start.9
  104.4 25.9 %attend.1 = (bf16[8,192,256]{2,1,0:T(8,128)(2,1)}, f32[8,192,256]{2,1,0:T(8,128)}, f32[8,8,256]{2,1,0:T(8,128)}) custom-call(s32[1]{0:T(128)} %bitcast.core_ref, bf16[192,4096]{1,0:T(8,128)(2,1)} %get-tuple-element.213.qt_ref, bf16[3,4096,128]{2,1,0:T(8,128)(2,1)} %get-tuple-element.214.kv_ref, bf16[192,4096]{1,0:T(8,128)(2,1)} %get-tuple-element.215.vt_ref), custom_call_target="tpu_custom_call" | custom-call | flops 14495514624 | bytes 9437184 | tf_op jit(solution)/shard_map/attend/pallas_call | solution.py:563
  130.3 4.9 %all-to-all-start = ((bf16[8,192,256]{2,1,0:T(8,128)(2,1)}), bf16[8,192,256]{2,1,0:T(8,128)(2,1)S(1)}, u32[]{:S(2)}, u32[]{:S(2)}) async-start(bf16[8,192,256]{2,1,0:T(8,128)(2,1)} %get-tuple-element.216), calls=%async_computation | async-start | bytes 1572864 | tf_op jit(solution)/shard_map/all_to_all | solution.py:1383
  135.1 2.2 collective-permute-done.8.refs_2_
  143.7 9.3 %assemble.1 = (bf16[3072,768]{1,0:T(8,128)(2,1)}, bf16[768,768]{1,0:T(8,128)(2,1)}) custom-call(s32[2]{0:T(128)} %pad_add_fusion.place_ref, bf16[4,128,768]{2,1,0:T(8,128)(2,1)} %copy-done.5, bf16[4,128,768]{2,1,0:T(8,128)(2,1)} %collective-permute-done.7.refs_1_, bf16[4,128,768]{2,1,0:T(8,128)(2,1)} %collective-permute-done.8.refs_2_, ...), custom_call_target="tpu_custom_call" | custom-call | tf_op jit(solution)/shard_map/assemble/pallas_call | solution.py:765
  152.9 6.4 %convolution_convert_fusion.grad_ref = bf16[512,3072]{1,0:T(8,128)(2,1)} fusion(bf16[512,768]{1,0:T(8,128)(2,1)S(1)} %multiply_convert_fusion.down_grad_ref, bf16[3072,768]{1,0:T(8,128)(2,1)} %get-tuple-element.224.w_down_ref), kind=kOutput, calls=%fused_computation | convolution fusion | flops 2417491968 | bytes 8650752 | tf_op jit(solution)/shard_map/dot_general | solution.py:361
  159.4 9.7 %all-to-all-done.mixed_ref = bf16[8,192,256]{2,1,0:T(8,128)(2,1)S(1)} async-done(((bf16[8,192,256]{2,1,0:T(8,128)(2,1)}), bf16[8,192,256]{2,1,0:T(8,128)(2,1)S(1)}, u32[]{:S(2)}, u32[]{:S(2)}) %all-to-all-start) | async-done | bytes 786464 | tf_op jit(solution)/shard_map/all_to_all | solution.py:1383
  170.0 18.6 %middle.1 = (f32[512,768]{1,0:T(8,128)}, bf16[512,768]{1,0:T(8,128)(2,1)}, bf16[512,3072]{1,0:T(8,128)(2,1)}, bf16[512,3072]{1,0:T(8,128)(2,1)}, f32[512,768]{1,...) custom-call(s32[1]{0:T(128)} %bitcast.core_ref, ...), custom_call_target="tpu_custom_call" | custom-call | flops 6039797760 | bytes 17301504 | tf_op jit(solution)/shard_map/middle/pallas_call | solution.py:1026
  188.7 4.2 %all-to-all-start.1 = ((bf16[8,192,256]{2,1,0:T(8,128)(2,1)}), bf16[8,192,256]{2,1,0:T(8,128)(2,1)}, u32[]{:S(2)}, u32[]{:S(2)}) async-start(bf16[8,192,256]{2,1,0:T(8,128)(2,1)} %get-tuple-element.229), calls=%async_computation.1 | async-start | bytes 1572864 | tf_op jit(solution)/shard_map/all_to_all | solution.py:1401
  194.2 6.5 %down_part.1 = bf16[3072,768]{1,0:T(8,128)(2,1)} custom-call(bf16[512,3072]{1,0:T(8,128)(2,1)} %get-tuple-element.242.active_ref, bf16[512,768]{1,0:T(8,128)(2,1)} %copy-done.3), custom_call_target="tpu_custom_call" | custom-call | tf_op jit(solution)/shard_map/down_part/pallas_call | solution.py:1071
  200.7 1.7 copy-done.6
  202.4 9.1 %pair_sums.1 = bf16[4,96,3840]{2,1,0:T(8,128)(2,1)} custom-call(s32[1]{0:T(128)} %bitcast.core_ref, bf16[512,768]{1,0:T(8,128)(2,1)} %get-tuple-element.230.low_ref, bf16[512,3072]{1,0:T(8,128)(2,1)} %get-tuple-element.231.hidden_ref, bf16[8,192,256]{2,1,0:T(8,128)(2,1)} %copy-done.8, bf16[512,768]{1,0:T(8,128)(2,1)} %get-tuple-element.232.branch_ref, ...), custom_call_target="tpu_custom_call" | custom-call | tf_op jit(solution)/shard_map/pair_sums/pallas_call | solution.py:1184
  211.6 2.3 all-to-all-done.1.grad_ref
  214.2 2.4 collective-permute-start.20
  217.8 52.5 %retrace.1 = (bf16[576,4096]{1,0:T(8,128)(2,1)}, bf16[4096,768]{1,0:T(8,128)(2,1)}) custom-call(s32[1]{0:T(128)} %bitcast.core_ref, bf16[192,4096]{1,0:T(8,128)(2,1)} %get-tuple-element.213.qt_ref, bf16[8,192,256]{2,1,0:T(8,128)(2,1)} %all-to-all-done.1.grad_ref, f32[8,192,256]{2,1,0:T(8,128)} %get-tuple-element.235.full_ref, ...), custom_call_target="tpu_custom_call" | custom-call | flops 36238786560 | bytes 11010048 | tf_op jit(solution)/shard_map/retrace/pallas_call | solution.py:687
  273.4 1.7 fusion.12
  275.2 2.9 collective-permute-start.23
  279.9 12.3 %joint_part.1 = (bf16[4,96,576]{2,1,0:T(8,128)(2,1)}, bf16[4,96,576]{2,1,0:T(8,128)(2,1)}, f32[8,768]{1,0:T(8,128)}, f32[8,576]{1,0:T(8,128)}) custom-call(s32[1]{0:T(128)} %bitcast.core_ref, bf16[4096,768]{1,0:T(8,128)(2,1)} %get-tuple-element.248.plain_ref, bf16[576,4096]{1,0:T(8,128)(2,1)} %get-tuple-element.249.joint_ref, bf16[576,768]{1,0:T(8,128)(2,1)} %bitcast.181, ...), custom_call_target="tpu_custom_call" | custom-call | tf_op jit(solution)/shard_map/joint_part/pallas_call | solution.py:1249
  292.2 9.4 %result_part.1 = (f32[512,768]{1,0:T(8,128)}, f32[8,768]{1,0:T(8,128)}) custom-call(f32[5]{0:T(128)} %weights_ref.5, bf16[512,3072]{1,0:T(8,128)(2,1)} %get-tuple-element.242.active_ref, bf16[3072,768]{1,0:T(8,128)(2,1)} %get-tuple-element.224.w_down_ref, f32[1,768]{1,0:T(1,128)} %reshape.467.b_down_ref, f32[512,768]{1,0:T(8,128)} %get-tuple-element.243.middle_ref, ...), custom_call_target="tpu_custom_call" | custom-call | tf_op jit(solution)/shard_map/result_part/pallas_call | solution.py:1110
  312.4 1.4 collective-permute-start.25
  314.9 5.1 %collective-permute-done.26 = bf16[4,24,1472]{2,1,0:T(8,128)(2,1)S(1)} collective-permute-done((bf16[4,24,1472]{2,1,0:T(8,128)(2,1)S(1)}, bf16[4,24,1472]{2,1,0:T(8,128)(2,1)S(1)}, u32[]{:S(2)}, u32[]{:S(2)}) %collective-permute-start.26) | collective-permute-done | bytes 282656 | tf_op jit(solution)/shard_map/ppermute | solution.py:797
  320.1 2.3 collective-permute-done.25
  322.3 5.4 %collective-permute-done.27 = bf16[4,24,1472]{2,1,0:T(8,128)(2,1)S(1)} collective-permute-done((bf16[4,24,1472]{2,1,0:T(8,128)(2,1)S(1)}, bf16[4,24,1472]{2,1,0:T(8,128)(2,1)S(1)}, u32[]{:S(2)}, u32[]{:S(2)}) %collective-permute-start.27) | collective-permute-done | bytes 282656 | tf_op jit(solution)/shard_map/ppermute | solution.py:797
  329.2 2.0 collective-permute-start.30
  331.2 3.3 collective-permute-start.29
  334.5 1.9 collective-permute-start.28
  336.7 2.0 collective-permute-start.36
  340.7 2.0 collective-permute-start.33
  345.6 4.2 %collective-permute-done.35.refs_10_ = bf16[24,3072]{1,0:T(8,128)(2,1)S(1)} collective-permute-done((bf16[24,3072]{1,0:T(8,128)(2,1)S(1)}, bf16[24,3072]{1,0:T(8,128)(2,1)S(1)}, u32[]{:S(2)}, u32[]{:S(2)}) %collective-permute-start.35) | collective-permute-done | bytes 147488 | tf_op jit(solution)/shard_map/ppermute | solution.py:797
  349.9 1.6 collective-permute-done.33.refs_3_
  351.4 1.5 collective-permute-done.32.refs_2_
  353.3 1.8 collective-permute-start.39
  357.1 2.7 collective-permute-done.39.refs_7_
  361.4 1.9 fusion.9
  363.4 3.8 %unpack.1 = (f32[96,3072]{1,0:T(8,128)}, f32[96,768]{1,0:T(8,128)}, f32[96,2304]{1,0:T(8,128)}, f32[384,768]{1,0:T(8,128)}, f32[1,192]{1,0:T(1,128)}, /*index=5*...) custom-call(s32[1]{0:T(128)} %bitcast.27.rep_ref, ...), custom_call_target="tpu_custom_call" | custom-call | tf_op jit(solution)/shard_map/unpack/pallas_call | solution.py:895
  368.4 1.7 fusion.7
  (299 shorter events, 60.4 us)
Async XLA Ops:
  7.2 75.5 %all-gather.3.cloned.1.call-start = ((), (), s32[]{:S(2)}) async-start(), calls=%async_computation.4 | async-start | bytes 7077888 | tf_op jit(solution)/shard_map/all_gather | solution.py:1321
  7.9 161.1 %all-gather.5.cloned.1.call-start = ((), (), s32[]{:S(2)}) async-start(), calls=%async_computation.5 | async-start | bytes 5308416 | tf_op jit(solution)/shard_map/all_gather | solution.py:1379
  11.9 9.9 %collective-permute-start = (bf16[104,576]{0,1:T(8,128)(2,1)S(1)}, bf16[104,576]{0,1:T(8,128)(2,1)S(1)}, u32[]{:S(2)}, u32[]{:S(2)}) collective-permute-start(bf16[104,576]{0,1:T(8,128)(2,1)S(1)} %get-tuple-element.330), channel_id=1, source_target_pairs={{0,2},{1,3},{2,4},{3,5},{4,6},{5,7},{6,0},{7,1},{8,10},{9,11},{10,... | collective-permute-start | bytes 359432 | tf_op jit(solution)/shard_map/ppermute | solution.py:793
  15.0 19.1 %collective-permute-start.1 = (bf16[104,576]{0,1:T(8,128)(2,1)S(1)}, bf16[104,576]{0,1:T(8,128)(2,1)S(1)}, u32[]{:S(2)}, u32[]{:S(2)}) collective-permute-start(bf16[104,576]{0,1:T(8,128)(2,1)S(1)} %get-tuple-element.331), channel_id=1, source_target_pairs={{0,4},{1,5},{2,6},{3,7},{4,0},{5,1},{6,2},{7,3},{8,12},{9,13},{10,... | collective-permute-start | bytes 359432 | tf_op jit(solution)/shard_map/ppermute | solution.py:793
  17.6 16.5 %collective-permute-start.2 = (bf16[104,576]{0,1:T(8,128)(2,1)S(1)}, bf16[104,576]{0,1:T(8,128)(2,1)S(1)}, u32[]{:S(2)}, u32[]{:S(2)}) collective-permute-start(bf16[104,576]{0,1:T(8,128)(2,1)S(1)} %get-tuple-element.332), channel_id=1, source_target_pairs={{0,6},{1,7},{2,0},{3,1},{4,2},{5,3},{6,4},{7,5},{8,14},{9,15},{10,... | collective-permute-start | bytes 359432 | tf_op jit(solution)/shard_map/ppermute | solution.py:793
  35.3 14.2 %collective-permute-start.3 = (bf16[4,104,576]{2,1,0:T(8,128)(2,1)}, bf16[4,104,576]{2,1,0:T(8,128)(2,1)}, u32[]{:S(2)}, u32[]{:S(2)}) collective-permute-start(bf16[4,104,576]{2,1,0:T(8,128)(2,1)} %copy.94), channel_id=1, source_target_pairs={{0,1},{1,0},{2,3},{3,2},{4,5},{5,4},{6,7},{7,6},{8,9},{9,8},{10,11... | collective-permute-start | bytes 1437704 | tf_op jit(solution)/shard_map/ppermute | solution.py:787
  49.5 103.4 %copy-start.3 = (bf16[512,768]{1,0:T(8,128)(2,1)}, bf16[512,768]{1,0:T(8,128)(2,1)S(1)}, u32[]{:S(2)}) copy-start(bf16[512,768]{1,0:T(8,128)(2,1)S(1)} %multiply_convert_fusion.down_grad_ref) | copy-start | bytes 2359300
  82.7 16.9 %collective-permute-start.6 = (bf16[128,768]{1,0:T(8,128)(2,1)S(1)}, bf16[128,768]{1,0:T(8,128)(2,1)S(1)}, u32[]{:S(2)}, u32[]{:S(2)}) collective-permute-start(bf16[128,768]{1,0:T(8,128)(2,1)S(1)} %fusion.17), channel_id=1, source_target_pairs={{0,6},{1,7},{2,0},{3,1},{4,2},{5,3},{6,4},{7,5},{8,14},{9,15},{10,... | collective-permute-start | bytes 589832 | tf_op jit(solution)/shard_map/ppermute | solution.py:793
  84.5 16.1 %collective-permute-start.5 = (bf16[128,768]{1,0:T(8,128)(2,1)S(1)}, bf16[128,768]{1,0:T(8,128)(2,1)S(1)}, u32[]{:S(2)}, u32[]{:S(2)}) collective-permute-start(bf16[128,768]{1,0:T(8,128)(2,1)S(1)} %fusion.17), channel_id=1, source_target_pairs={{0,4},{1,5},{2,6},{3,7},{4,0},{5,1},{6,2},{7,3},{8,12},{9,13},{10,... | collective-permute-start | bytes 589832 | tf_op jit(solution)/shard_map/ppermute | solution.py:793
  84.5 16.1 %collective-permute-start.4 = (bf16[128,768]{1,0:T(8,128)(2,1)S(1)}, bf16[128,768]{1,0:T(8,128)(2,1)S(1)}, u32[]{:S(2)}, u32[]{:S(2)}) collective-permute-start(bf16[128,768]{1,0:T(8,128)(2,1)S(1)} %fusion.17), channel_id=1, source_target_pairs={{0,2},{1,3},{2,4},{3,5},{4,6},{5,7},{6,0},{7,1},{8,10},{9,11},{10,... | collective-permute-start | bytes 589832 | tf_op jit(solution)/shard_map/ppermute | solution.py:793
  100.8 34.3 %collective-permute-start.9 = (bf16[4,128,768]{2,1,0:T(8,128)(2,1)S(1)}, bf16[4,128,768]{2,1,0:T(8,128)(2,1)}, u32[]{:S(2)}, u32[]{:S(2)}) collective-permute-start(bf16[4,128,768]{2,1,0:T(8,128)(2,1)S(1)} %pad_maximum_fusion.refs_0_), channel_id=1, source_target_pairs={{0,24},{8,16},{16,8},{24,0},{1,25},{9,17},{17,9},{25,1},{2,26},{10... | collective-permute-start | bytes 2359304 | tf_op jit(solution)/shard_map/ppermute | solution.py:797
  103.4 34.0 %collective-permute-start.8 = (bf16[4,128,768]{2,1,0:T(8,128)(2,1)S(1)}, bf16[4,128,768]{2,1,0:T(8,128)(2,1)}, u32[]{:S(2)}, u32[]{:S(2)}) collective-permute-start(bf16[4,128,768]{2,1,0:T(8,128)(2,1)S(1)} %pad_maximum_fusion.refs_0_), channel_id=1, source_target_pairs={{0,16},{8,24},{16,0},{24,8},{1,17},{9,25},{17,1},{25,9},{2,18},{10... | collective-permute-start | bytes 2359304 | tf_op jit(solution)/shard_map/ppermute | solution.py:797
  103.8 33.6 %collective-permute-start.7 = (bf16[4,128,768]{2,1,0:T(8,128)(2,1)S(1)}, bf16[4,128,768]{2,1,0:T(8,128)(2,1)}, u32[]{:S(2)}, u32[]{:S(2)}) collective-permute-start(bf16[4,128,768]{2,1,0:T(8,128)(2,1)S(1)} %pad_maximum_fusion.refs_0_), channel_id=1, source_target_pairs={{0,8},{8,0},{16,24},{24,16},{1,9},{9,1},{17,25},{25,17},{2,10},{10... | collective-permute-start | bytes 2359304 | tf_op jit(solution)/shard_map/ppermute | solution.py:797
  130.3 38.8 %all-to-all-start = ((bf16[8,192,256]{2,1,0:T(8,128)(2,1)}), bf16[8,192,256]{2,1,0:T(8,128)(2,1)S(1)}, u32[]{:S(2)}, u32[]{:S(2)}) async-start(bf16[8,192,256]{2,1,0:T(8,128)(2,1)} %get-tuple-element.216), calls=%async_computation | async-start | bytes 1572864 | tf_op jit(solution)/shard_map/all_to_all | solution.py:1383
  137.4 4.4 %collective-permute-start.10 = (bf16[4,128,768]{2,1,0:T(8,128)(2,1)S(1)}, bf16[4,128,768]{2,1,0:T(8,128)(2,1)}, u32[]{:S(2)}, u32[]{:S(2)}) collective-permute-start(bf16[4,128,768]{2,1,0:T(8,128)(2,1)S(1)} %pad_maximum_fusion.refs_0_), channel_id=1, source_target_pairs={{0,1},{1,0},{2,3},{3,2},{4,5},{5,4},{6,7},{7,6},{8,9},{9,8},{10,11... | collective-permute-start | bytes 2359304 | tf_op jit(solution)/shard_map/ppermute | solution.py:787
  137.4 4.4 %collective-permute-start.11 = (bf16[4,128,768]{2,1,0:T(8,128)(2,1)}, bf16[4,128,768]{2,1,0:T(8,128)(2,1)}, u32[]{:S(2)}, u32[]{:S(2)}) collective-permute-start(bf16[4,128,768]{2,1,0:T(8,128)(2,1)} %collective-permute-done.7.refs_1_), channel_id=1, source_target_pairs={{0,1},{1,0},{2,3},{3,2},{4,5},{5,4},{6,7},{7,6},{8,9},{9,8},{10,11... | collective-permute-start | bytes 2359304 | tf_op jit(solution)/shard_map/ppermute | solution.py:787
  138.0 4.6 %collective-permute-start.12 = (bf16[4,128,768]{2,1,0:T(8,128)(2,1)}, bf16[4,128,768]{2,1,0:T(8,128)(2,1)}, u32[]{:S(2)}, u32[]{:S(2)}) collective-permute-start(bf16[4,128,768]{2,1,0:T(8,128)(2,1)} %collective-permute-done.8.refs_2_), channel_id=1, source_target_pairs={{0,1},{1,0},{2,3},{3,2},{4,5},{5,4},{6,7},{7,6},{8,9},{9,8},{10,11... | collective-permute-start | bytes 2359304 | tf_op jit(solution)/shard_map/ppermute | solution.py:787
  138.0 5.7 %collective-permute-start.13 = (bf16[4,128,768]{2,1,0:T(8,128)(2,1)}, bf16[4,128,768]{2,1,0:T(8,128)(2,1)}, u32[]{:S(2)}, u32[]{:S(2)}) collective-permute-start(bf16[4,128,768]{2,1,0:T(8,128)(2,1)} %collective-permute-done.9.refs_3_), channel_id=1, source_target_pairs={{0,1},{1,0},{2,3},{3,2},{4,5},{5,4},{6,7},{7,6},{8,9},{9,8},{10,11... | collective-permute-start | bytes 2359304 | tf_op jit(solution)/shard_map/ppermute | solution.py:787
  188.6 12.1 %collective-permute-start.15 = (bf16[512,3072]{1,0:T(8,128)(2,1)}, bf16[512,3072]{1,0:T(8,128)(2,1)S(1)}, u32[]{:S(2)}, u32[]{:S(2)}) collective-permute-start(bf16[512,3072]{1,0:T(8,128)(2,1)} %get-tuple-element.231.hidden_ref), channel_id=1, source_target_pairs={{0,1},{1,0},{2,3},{3,2},{4,5},{5,4},{6,7},{7,6},{8,9},{9,8},{10,11... | collective-permute-start | bytes 9437192 | tf_op jit(solution)/shard_map/ppermute | solution.py:787
  188.7 25.2 %all-to-all-start.1 = ((bf16[8,192,256]{2,1,0:T(8,128)(2,1)}), bf16[8,192,256]{2,1,0:T(8,128)(2,1)}, u32[]{:S(2)}, u32[]{:S(2)}) async-start(bf16[8,192,256]{2,1,0:T(8,128)(2,1)} %get-tuple-element.229), calls=%async_computation.1 | async-start | bytes 1572864 | tf_op jit(solution)/shard_map/all_to_all | solution.py:1401
  192.9 116.7 %reduce-scatter.5.cloned.1.call-start = ((), (), s32[]{:S(2)}) async-start(), calls=%async_computation.7 | async-start | bytes 5308416 | tf_op jit(solution)/shard_map/reduce_scatter | solution.py:1409
  193.2 7.5 %collective-permute-start.16 = (bf16[8,192,256]{2,1,0:T(8,128)(2,1)}, bf16[8,192,256]{2,1,0:T(8,128)(2,1)}, u32[]{:S(2)}, u32[]{:S(2)}) collective-permute-start(bf16[8,192,256]{2,1,0:T(8,128)(2,1)} %copy-done.8), channel_id=1, source_target_pairs={{0,1},{1,0},{2,3},{3,2},{4,5},{5,4},{6,7},{7,6},{8,9},{9,8},{10,11... | collective-permute-start | bytes 2359304 | tf_op jit(solution)/shard_map/ppermute | solution.py:787
  193.7 7.0 %collective-permute-start.14 = (bf16[512,768]{1,0:T(8,128)(2,1)}, bf16[512,768]{1,0:T(8,128)(2,1)}, u32[]{:S(2)}, u32[]{:S(2)}) collective-permute-start(bf16[512,768]{1,0:T(8,128)(2,1)} %get-tuple-element.230.low_ref), channel_id=1, source_target_pairs={{0,1},{1,0},{2,3},{3,2},{4,5},{5,4},{6,7},{7,6},{8,9},{9,8},{10,11... | collective-permute-start | bytes 2359304 | tf_op jit(solution)/shard_map/ppermute | solution.py:787
  193.7 7.0 %collective-permute-start.17 = (bf16[512,768]{1,0:T(8,128)(2,1)}, bf16[512,768]{1,0:T(8,128)(2,1)}, u32[]{:S(2)}, u32[]{:S(2)}) collective-permute-start(bf16[512,768]{1,0:T(8,128)(2,1)} %get-tuple-element.232.branch_ref), channel_id=1, source_target_pairs={{0,1},{1,0},{2,3},{3,2},{4,5},{5,4},{6,7},{7,6},{8,9},{9,8},{10,11... | collective-permute-start | bytes 2359304 | tf_op jit(solution)/shard_map/ppermute | solution.py:787
  213.9 146.8 %reduce-scatter.3.cloned.1.call-start = ((), (), s32[]{:S(2)}) async-start(), calls=%async_computation.6 | async-start | bytes 7077888 | tf_op jit(solution)/shard_map/reduce_scatter | solution.py:1416
  214.2 56.1 %collective-permute-start.20 = (bf16[4,24,3840]{2,1,0:T(8,128)(2,1)S(1)}, bf16[4,24,3840]{2,1,0:T(8,128)(2,1)S(1)}, u32[]{:S(2)}, u32[]{:S(2)}) collective-permute-start(bf16[4,24,3840]{2,1,0:T(8,128)(2,1)S(1)} %get-tuple-element.318), channel_id=1, source_target_pairs={{0,24},{8,16},{16,8},{24,0},{1,25},{9,17},{17,9},{25,1},{2,26},{10... | collective-permute-start | bytes 2211848 | tf_op jit(solution)/shard_map/ppermute | solution.py:797
  216.6 53.7 %collective-permute-start.19 = (bf16[4,24,3840]{2,1,0:T(8,128)(2,1)S(1)}, bf16[4,24,3840]{2,1,0:T(8,128)(2,1)S(1)}, u32[]{:S(2)}, u32[]{:S(2)}) collective-permute-start(bf16[4,24,3840]{2,1,0:T(8,128)(2,1)S(1)} %get-tuple-element.319), channel_id=1, source_target_pairs={{0,16},{8,24},{16,0},{24,8},{1,17},{9,25},{17,1},{25,9},{2,18},{10... | collective-permute-start | bytes 2211848 | tf_op jit(solution)/shard_map/ppermute | solution.py:797
  217.1 53.2 %collective-permute-start.18 = (bf16[4,24,3840]{2,1,0:T(8,128)(2,1)S(1)}, bf16[4,24,3840]{2,1,0:T(8,128)(2,1)S(1)}, u32[]{:S(2)}, u32[]{:S(2)}) collective-permute-start(bf16[4,24,3840]{2,1,0:T(8,128)(2,1)S(1)} %get-tuple-element.320), channel_id=1, source_target_pairs={{0,8},{8,0},{16,24},{24,16},{1,9},{9,1},{17,25},{25,17},{2,10},{10... | collective-permute-start | bytes 2211848 | tf_op jit(solution)/shard_map/ppermute | solution.py:797
  275.2 26.4 %collective-permute-start.23 = (bf16[24,3840]{1,0:T(8,128)(2,1)S(1)}, bf16[24,3840]{1,0:T(8,128)(2,1)S(1)}, u32[]{:S(2)}, u32[]{:S(2)}) collective-permute-start(bf16[24,3840]{1,0:T(8,128)(2,1)S(1)} %get-tuple-element.333), channel_id=1, source_target_pairs={{0,6},{1,7},{2,0},{3,1},{4,2},{5,3},{6,4},{7,5},{8,14},{9,15},{10,... | collective-permute-start | bytes 552968 | tf_op jit(solution)/shard_map/ppermute | solution.py:793
  278.1 24.3 %collective-permute-start.22 = (bf16[24,3840]{1,0:T(8,128)(2,1)S(1)}, bf16[24,3840]{1,0:T(8,128)(2,1)S(1)}, u32[]{:S(2)}, u32[]{:S(2)}) collective-permute-start(bf16[24,3840]{1,0:T(8,128)(2,1)S(1)} %get-tuple-element.334), channel_id=1, source_target_pairs={{0,4},{1,5},{2,6},{3,7},{4,0},{5,1},{6,2},{7,3},{8,12},{9,13},{10,... | collective-permute-start | bytes 552968 | tf_op jit(solution)/shard_map/ppermute | solution.py:793
  278.1 24.3 %collective-permute-start.21 = (bf16[24,3840]{1,0:T(8,128)(2,1)S(1)}, bf16[24,3840]{1,0:T(8,128)(2,1)S(1)}, u32[]{:S(2)}, u32[]{:S(2)}) collective-permute-start(bf16[24,3840]{1,0:T(8,128)(2,1)S(1)} %get-tuple-element.335), channel_id=1, source_target_pairs={{0,2},{1,3},{2,4},{3,5},{4,6},{5,7},{6,0},{7,1},{8,10},{9,11},{10,... | collective-permute-start | bytes 552968 | tf_op jit(solution)/shard_map/ppermute | solution.py:793
  304.1 2.2 collective-permute-start.24
  310.9 9.1 %collective-permute-start.26 = (bf16[4,24,1472]{2,1,0:T(8,128)(2,1)S(1)}, bf16[4,24,1472]{2,1,0:T(8,128)(2,1)S(1)}, u32[]{:S(2)}, u32[]{:S(2)}) collective-permute-start(bf16[4,24,1472]{2,1,0:T(8,128)(2,1)S(1)} %pad_maximum_fusion.4), channel_id=1, source_target_pairs={{0,16},{8,24},{16,0},{24,8},{1,17},{9,25},{17,1},{25,9},{2,18},{10... | collective-permute-start | bytes 847880 | tf_op jit(solution)/shard_map/ppermute | solution.py:797
  312.4 10.0 %collective-permute-start.25 = (bf16[4,24,1472]{2,1,0:T(8,128)(2,1)S(1)}, bf16[4,24,1472]{2,1,0:T(8,128)(2,1)S(1)}, u32[]{:S(2)}, u32[]{:S(2)}) collective-permute-start(bf16[4,24,1472]{2,1,0:T(8,128)(2,1)S(1)} %pad_maximum_fusion.3), channel_id=1, source_target_pairs={{0,8},{8,0},{16,24},{24,16},{1,9},{9,1},{17,25},{25,17},{2,10},{10... | collective-permute-start | bytes 847880 | tf_op jit(solution)/shard_map/ppermute | solution.py:797
  313.9 13.9 %collective-permute-start.27 = (bf16[4,24,1472]{2,1,0:T(8,128)(2,1)S(1)}, bf16[4,24,1472]{2,1,0:T(8,128)(2,1)S(1)}, u32[]{:S(2)}, u32[]{:S(2)}) collective-permute-start(bf16[4,24,1472]{2,1,0:T(8,128)(2,1)S(1)} %pad_maximum_fusion.5), channel_id=1, source_target_pairs={{0,24},{8,16},{16,8},{24,0},{1,25},{9,17},{17,9},{25,1},{2,26},{10... | collective-permute-start | bytes 847880 | tf_op jit(solution)/shard_map/ppermute | solution.py:797
  329.2 10.5 %collective-permute-start.30 = (bf16[24,704]{1,0:T(8,128)(2,1)S(1)}, bf16[24,704]{1,0:T(8,128)(2,1)S(1)}, u32[]{:S(2)}, u32[]{:S(2)}) collective-permute-start(bf16[24,704]{1,0:T(8,128)(2,1)S(1)} %get-tuple-element.353), channel_id=1, source_target_pairs={{0,6},{1,7},{2,0},{3,1},{4,2},{5,3},{6,4},{7,5},{8,14},{9,15},{10,... | collective-permute-start | bytes 101384 | tf_op jit(solution)/shard_map/ppermute | solution.py:793
  331.2 9.5 %collective-permute-start.29 = (bf16[24,704]{1,0:T(8,128)(2,1)S(1)}, bf16[24,704]{1,0:T(8,128)(2,1)S(1)}, u32[]{:S(2)}, u32[]{:S(2)}) collective-permute-start(bf16[24,704]{1,0:T(8,128)(2,1)S(1)} %get-tuple-element.354), channel_id=1, source_target_pairs={{0,4},{1,5},{2,6},{3,7},{4,0},{5,1},{6,2},{7,3},{8,12},{9,13},{10,... | collective-permute-start | bytes 101384 | tf_op jit(solution)/shard_map/ppermute | solution.py:793
  334.5 8.2 %collective-permute-start.28 = (bf16[24,704]{1,0:T(8,128)(2,1)S(1)}, bf16[24,704]{1,0:T(8,128)(2,1)S(1)}, u32[]{:S(2)}, u32[]{:S(2)}) collective-permute-start(bf16[24,704]{1,0:T(8,128)(2,1)S(1)} %get-tuple-element.355), channel_id=1, source_target_pairs={{0,2},{1,3},{2,4},{3,5},{4,6},{5,7},{6,0},{7,1},{8,10},{9,11},{10,... | collective-permute-start | bytes 101384 | tf_op jit(solution)/shard_map/ppermute | solution.py:793
  336.7 7.8 %collective-permute-start.36 = (bf16[24,3072]{1,0:T(8,128)(2,1)S(1)}, bf16[24,3072]{1,0:T(8,128)(2,1)}, u32[]{:S(2)}, u32[]{:S(2)}) collective-permute-start(bf16[24,3072]{1,0:T(8,128)(2,1)S(1)} %pad_maximum_fusion.6.refs_8_), channel_id=1, source_target_pairs={{0,24},{8,16},{16,8},{24,0},{1,25},{9,17},{17,9},{25,1},{2,26},{10... | collective-permute-start | bytes 442376 | tf_op jit(solution)/shard_map/ppermute | solution.py:797
  339.1 10.7 %collective-permute-start.35 = (bf16[24,3072]{1,0:T(8,128)(2,1)S(1)}, bf16[24,3072]{1,0:T(8,128)(2,1)S(1)}, u32[]{:S(2)}, u32[]{:S(2)}) collective-permute-start(bf16[24,3072]{1,0:T(8,128)(2,1)S(1)} %pad_maximum_fusion.6.refs_8_), channel_id=1, source_target_pairs={{0,16},{8,24},{16,0},{24,8},{1,17},{9,25},{17,1},{25,9},{2,18},{10... | collective-permute-start | bytes 442376 | tf_op jit(solution)/shard_map/ppermute | solution.py:797
  339.7 10.1 %collective-permute-start.34 = (bf16[24,3072]{1,0:T(8,128)(2,1)S(1)}, bf16[24,3072]{1,0:T(8,128)(2,1)S(1)}, u32[]{:S(2)}, u32[]{:S(2)}) collective-permute-start(bf16[24,3072]{1,0:T(8,128)(2,1)S(1)} %pad_maximum_fusion.6.refs_8_), channel_id=1, source_target_pairs={{0,8},{8,0},{16,24},{24,16},{1,9},{9,1},{17,25},{25,17},{2,10},{10... | collective-permute-start | bytes 442376 | tf_op jit(solution)/shard_map/ppermute | solution.py:797
  340.7 10.7 %collective-permute-start.33 = (bf16[24,3840]{1,0:T(8,128)(2,1)S(1)}, bf16[24,3840]{1,0:T(8,128)(2,1)S(1)}, u32[]{:S(2)}, u32[]{:S(2)}) collective-permute-start(bf16[24,3840]{1,0:T(8,128)(2,1)S(1)} %add_convert_fusion.1.refs_0_), channel_id=1, source_target_pairs={{0,24},{8,16},{16,8},{24,0},{1,25},{9,17},{17,9},{25,1},{2,26},{10... | collective-permute-start | bytes 552968 | tf_op jit(solution)/shard_map/ppermute | solution.py:797
  342.7 10.3 %collective-permute-start.32 = (bf16[24,3840]{1,0:T(8,128)(2,1)S(1)}, bf16[24,3840]{1,0:T(8,128)(2,1)S(1)}, u32[]{:S(2)}, u32[]{:S(2)}) collective-permute-start(bf16[24,3840]{1,0:T(8,128)(2,1)S(1)} %add_convert_fusion.1.refs_0_), channel_id=1, source_target_pairs={{0,16},{8,24},{16,0},{24,8},{1,17},{9,25},{17,1},{25,9},{2,18},{10... | collective-permute-start | bytes 552968 | tf_op jit(solution)/shard_map/ppermute | solution.py:797
  344.5 8.5 %collective-permute-start.31 = (bf16[24,3840]{1,0:T(8,128)(2,1)S(1)}, bf16[24,3840]{1,0:T(8,128)(2,1)S(1)}, u32[]{:S(2)}, u32[]{:S(2)}) collective-permute-start(bf16[24,3840]{1,0:T(8,128)(2,1)S(1)} %add_convert_fusion.1.refs_0_), channel_id=1, source_target_pairs={{0,8},{8,0},{16,24},{24,16},{1,9},{9,1},{17,25},{25,17},{2,10},{10... | collective-permute-start | bytes 552968 | tf_op jit(solution)/shard_map/ppermute | solution.py:797
  353.3 6.6 %collective-permute-start.39 = (bf16[24,2432]{1,0:T(8,128)(2,1)S(1)}, bf16[24,2432]{1,0:T(8,128)(2,1)S(1)}, u32[]{:S(2)}, u32[]{:S(2)}) collective-permute-start(bf16[24,2432]{1,0:T(8,128)(2,1)S(1)} %concatenate.75.refs_4_), channel_id=1, source_target_pairs={{0,24},{8,16},{16,8},{24,0},{1,25},{9,17},{17,9},{25,1},{2,26},{10... | collective-permute-start | bytes 350216 | tf_op jit(solution)/shard_map/ppermute | solution.py:797
  355.0 5.6 %collective-permute-start.38 = (bf16[24,2432]{1,0:T(8,128)(2,1)S(1)}, bf16[24,2432]{1,0:T(8,128)(2,1)S(1)}, u32[]{:S(2)}, u32[]{:S(2)}) collective-permute-start(bf16[24,2432]{1,0:T(8,128)(2,1)S(1)} %concatenate.75.refs_4_), channel_id=1, source_target_pairs={{0,16},{8,24},{16,0},{24,8},{1,17},{9,25},{17,1},{25,9},{2,18},{10... | collective-permute-start | bytes 350216 | tf_op jit(solution)/shard_map/ppermute | solution.py:797
  355.8 4.9 %collective-permute-start.37 = (bf16[24,2432]{1,0:T(8,128)(2,1)S(1)}, bf16[24,2432]{1,0:T(8,128)(2,1)S(1)}, u32[]{:S(2)}, u32[]{:S(2)}) collective-permute-start(bf16[24,2432]{1,0:T(8,128)(2,1)S(1)} %concatenate.75.refs_4_), channel_id=1, source_target_pairs={{0,8},{8,0},{16,24},{24,16},{1,9},{9,1},{17,25},{25,17},{2,10},{10... | collective-permute-start | bytes 350216 | tf_op jit(solution)/shard_map/ppermute | solution.py:797
  363.3 6.8 %collective-permute-start.40 = (f32[5]{0:T(128)S(1)}, f32[5]{0:T(128)S(1)}, u32[]{:S(2)}, u32[]{:S(2)}) collective-permute-start(f32[5]{0:T(128)S(1)} %fusion.43), channel_id=1, source_target_pairs={{0,1},{1,0},{2,3},{3,2},{4,5},{5,4},{6,7},{7,6},{8,9},{9,8},{10,11... | collective-permute-start | bytes 68 | tf_op jit(solution)/shard_map/ppermute | solution.py:787
  (33 other events, 252.0 us)
Sparse Core Ops, SparseCore 0:
  9.7 73.0 all-gather.2
  100.9 67.9 all-gather.4
  214.0 53.7 reduce-scatter.4
  271.3 81.3 reduce-scatter.2

commit v4 on v3

--- a/solution.py
+++ b/solution.py
@@ -1005,7 +1005,7 @@
 ):
     rows, model_width = x.shape
     hidden_width = w_in.shape[1]
-    chunk = CHUNK
+    chunk = 2 * CHUNK if hidden_width % (2 * CHUNK) == 0 else CHUNK
     whole = lambda value: pl.BlockSpec(value.shape, lambda j, *_: (0,) * value.ndim)
     across = pl.BlockSpec((rows, chunk), lambda j, *_: (0, j))
     line = pl.BlockSpec((1, chunk), lambda j, *_: (0, j))
@@ -1239,6 +1239,7 @@
     columns = joint_t.shape[0]
     owners = length // CHUNK // 2
     part = model_width // (2 * owners)
+    tile = 2 * CHUNK
     whole = lambda value: pl.BlockSpec(value.shape, lambda j, core: (0,) * value.ndim)
     shapes = [
         jax.ShapeDtypeStruct((owners, part, columns), BF16),
@@ -1251,10 +1252,10 @@
         name="joint_part",
         grid_spec=pltpu.PrefetchScalarGridSpec(
             num_scalar_prefetch=1,
-            grid=(length // CHUNK,),
+            grid=(length // tile,),
             in_specs=[
-                pl.BlockSpec((CHUNK, model_width), lambda j, core: (j, 0)),
-                pl.BlockSpec((columns, CHUNK), lambda j, core: (0, j)),
+                pl.BlockSpec((tile, model_width), lambda j, core: (j, 0)),
+                pl.BlockSpec((columns, tile), lambda j, core: (0, j)),
                 whole(weight_t),
                 whole(gain),
                 whole(shift),
@@ -1471,6 +1472,7 @@
         jnp.concatenate([own_sums, pick(small, core, 1)], axis=2), received
     )
     depth_sum = jnp.concatenate([depth_sums, last_depth[None]], axis=0).sum(axis=(1, 2))
+    depth_sum = depth_sum + swap_core(depth_sum)
     down_parts = pick_parts(down_sums[None])
     down_rows = part // 4
     columns = 3 * width + 128
@@ -1494,20 +1496,19 @@
     )
     down_pieces = every_rep(jnp.concatenate([down_sums[k] for k in range(owners)], axis=1))
     arrived = exchange_owner(mixed_sums, owner)
-    arrived = lax.optimization_barrier((*arrived, *pair_pieces, *down_pieces))
-    pair_pieces, down_pieces = arrived[owners : owners + 4], arrived[owners + 4 :]
-    arrived = arrived[:owners]
     small = add_low(*[value[:, 3 * width :] for value in arrived])
     by_distance = jnp.stack([value[:, : 3 * width] for value in arrived])
     by_owner = [pick(by_distance, (owner - k) % owners) for k in range(owners)]
     joint_pieces = every_rep(jnp.concatenate([*by_owner, small], axis=1))
     depth_sums = [depth_row(value) for value in arrived]
-    grad_normed, *pieces = lax.optimization_barrier((grad_normed, *joint_pieces, *depth_sums))
-    joint_pieces, depth_sums = pieces[:4], pieces[4:]
+    pieces = lax.optimization_barrier(
+        (*joint_pieces, *pair_pieces, *down_pieces, *depth_sums)
+    )
+    joint_pieces, pair_pieces = pieces[:4], pieces[4:8]
+    down_pieces, depth_sums = pieces[8:12], pieces[12:]
     grad_depth = add_ordered(
         [join_depth(value) for value in depth_sums], lambda k: (owner - k) % owners
     )
-    grad_depth = grad_depth + swap_core(grad_depth)
     sum_in, sum_out, sum_qkv, sum_down, *small_outs = unpack(
         lax.axis_index("rep").astype(jnp.int32).reshape(1),
         pair_pieces,
@@ -1517,6 +1518,10 @@
         counts,
     )
     small_outs = [value.reshape(-1) for value in small_outs]
+    finished = (sum_in, sum_out, sum_qkv, sum_down, grad_depth, *small_outs)
+    grad_normed, sum_in, sum_out, sum_qkv, sum_down, grad_depth, *small_outs = (
+        lax.optimization_barrier((grad_normed, *finished))
+    )
     grad_normed = grad_normed.astype(F32)
     center = inputs - jnp.mean(inputs, axis=-1, keepdims=True)
     scale = lax.rsqrt(jnp.mean(center * center, axis=-1, keepdims=True) + EPSILON)

time: 385 us -> 383 us (level)
    ppermute x18, waiting for transfers between devices: 27.2 us -> 20.6 us  [cross_rep(): lax.ppermute(value, 'rep', [(i, i ^ mask) for i in range(lax.axis_size('r...]
    unnamed x80 -> x84, local copies, waits for them, and re-layouts: 7.76 us -> 7.65 us
  transfers between devices with their start and end apart: 47 -> 47, of which waited for: 21 -> 20; matrix products, arithmetic and copies ran while one was open for 13% -> 14% of each run, Pallas kernels for 40% -> 39%
where the time goes in v4:
time: 383 us; the launch traced here: 376 us
  Pallas kernels  166 us (43%)
  waiting for transfers between devices  79.1 us (21%)
  starting transfers between devices  56.7 us (15%)
  local copies, waits for them, and re-layouts  33.3 us (9%)
  other arithmetic  19.6 us (5%)
  between operations  15.4 us (4%)
  matrix products  6.41 us (2%)
    pallas_call x1, Pallas kernels, retrace(): pl.pallas_call(retrace_kernel, name='retrace', cost_estimate=cost(5 * 2 *...  52.1 us
    pallas_call x1, Pallas kernels, attend(): pl.pallas_call(attend_kernel, name='attend', cost_estimate=cost(2 * 2 * B...  25.9 us
    ppermute x18, starting transfers between devices, cross_rep(): lax.ppermute(value, 'rep', [(i, i ^ mask) for i in range(lax.axis_size('r...  23.5 us
    all_gather x1, waiting for transfers between devices, head_split_device(): tokens = lax.all_gather(block_in, 'shard', axis=0, tiled=True)  21.8 us
    ppermute x12, starting transfers between devices, shift_owner(): lax.ppermute(value, 'shard', [(i, (i + step) % groups) for i in range(gro...  21 us
    ppermute x12, waiting for transfers between devices, shift_owner(): lax.ppermute(value, 'shard', [(i, (i + step) % groups) for i in range(gro...  20.6 us
    ppermute x18, waiting for transfers between devices, cross_rep(): lax.ppermute(value, 'rep', [(i, i ^ mask) for i in range(lax.axis_size('r...  20.6 us
    pallas_call x1, Pallas kernels, middle_part(): pl.pallas_call(middle_kernel, name='middle', cost_estimate=cost(4 * rows...  18.1 us
  transfers between devices with their start and end apart: 47, of which 20 were waited for; matrix products, arithmetic and copies ran while one was open for 14% of the time, Pallas kernels for 39%

profile of v4, /device:TPU:0, one launch (start us, length us, event | category | flops | bytes accessed | tf_op | source)
XLA Modules:
  0.0 376.0 jit_solution(9144890927578485397)
XLA Ops:
  11.9 3.1 collective-permute-start
  15.0 2.6 collective-permute-start.1
  18.9 2.8 collective-permute-done
  21.8 12.3 %collective-permute-done.1 = bf16[104,576]{0,1:T(8,128)(2,1)S(1)} collective-permute-done((bf16[104,576]{0,1:T(8,128)(2,1)S(1)}, bf16[104,576]{0,1:T(8,128)(2,1)S(1)}, u32[]{:S(2)}, u32[]{:S(2)}) %collective-permute-start.1) | collective-permute-done | bytes 119840 | tf_op jit(solution)/shard_map/ppermute | solution.py:793
  35.3 2.8 multiply_sine_fusion
  41.1 7.5 %average.1 = (f32[4,512,768]{2,1,0:T(8,128)}, f32[512,768]{1,0:T(8,128)}, f32[4,8,768]{2,1,0:T(8,128)}) custom-call(f32[5]{0:T(128)} %weights_ref.5, bf16[4,512,768]{2,1,0:T(8,128)(2,1)} %earlier_ref.1, f32[512,768]{1,0:T(8,128)} %cotangent_ref.5), custom_call_target="tpu_custom_call" | custom-call | flops 9437184 | bytes 12582912 | tf_op jit(solution)/shard_map/average/pallas_call | solution.py:464
  49.6 1.6 copy.95
  60.9 21.8 %all-gather.3.cloned.1.call-done.x_ref = bf16[4096,768]{1,0:T(8,128)(2,1)} async-done(((bf16[512,768]{1,0:T(8,128)(2,1)}), bf16[4096,768]{1,0:T(8,128)(2,1)}) %all-gather.3.cloned.1.call-update) | async-done | bytes 6291472 | tf_op jit(solution)/shard_map/all_gather | solution.py:1322
  82.7 1.8 collective-permute-start.6
  86.1 13.5 %project.1 = (bf16[4096,768]{1,0:T(8,128)(2,1)}, bf16[192,4096]{1,0:T(8,128)(2,1)}, bf16[192,4096]{1,0:T(8,128)(2,1)}, bf16[192,4096]{1,0:T(8,128)(2,1)}, bf16[3,4096,128]{2,1,0:T(8,128)(2,1)}) custom-call(bf16[4096,768]{1,0:T(8,128)(2,1)} %all-gather.3.cloned.1.call-done.x_ref, bf16[576,768]{1,0:T(8,128)(2,1)} %bitcast.177, f32[576,1]{1,0:T(8,128)} %copy.105.bias_ref, ...), custom_call_target="tpu_custom_call" | custom-call | flops 3623878656 | bytes 37748736 | tf_op jit(solution)/shard_map/project/pallas_call | solution.py:410
  100.8 2.5 collective-permute-start.9
  104.4 25.9 %attend.1 = (bf16[8,192,256]{2,1,0:T(8,128)(2,1)}, f32[8,192,256]{2,1,0:T(8,128)}, f32[8,8,256]{2,1,0:T(8,128)}) custom-call(s32[1]{0:T(128)} %bitcast.core_ref, bf16[192,4096]{1,0:T(8,128)(2,1)} %get-tuple-element.223.qt_ref, bf16[3,4096,128]{2,1,0:T(8,128)(2,1)} %get-tuple-element.224.kv_ref, bf16[192,4096]{1,0:T(8,128)(2,1)} %get-tuple-element.225.vt_ref), custom_call_target="tpu_custom_call" | custom-call | flops 14495514624 | bytes 9437184 | tf_op jit(solution)/shard_map/attend/pallas_call | solution.py:563
  130.3 4.9 %all-to-all-start = ((bf16[8,192,256]{2,1,0:T(8,128)(2,1)}), bf16[8,192,256]{2,1,0:T(8,128)(2,1)S(1)}, u32[]{:S(2)}, u32[]{:S(2)}) async-start(bf16[8,192,256]{2,1,0:T(8,128)(2,1)} %get-tuple-element.226), calls=%async_computation | async-start | bytes 1572864 | tf_op jit(solution)/shard_map/all_to_all | solution.py:1384
  135.1 2.2 collective-permute-done.8.refs_2_
  143.7 9.3 %assemble.1 = (bf16[3072,768]{1,0:T(8,128)(2,1)}, bf16[768,768]{1,0:T(8,128)(2,1)}) custom-call(s32[2]{0:T(128)} %pad_add_fusion.place_ref, bf16[4,128,768]{2,1,0:T(8,128)(2,1)} %copy-done.4, bf16[4,128,768]{2,1,0:T(8,128)(2,1)} %collective-permute-done.7.refs_1_, bf16[4,128,768]{2,1,0:T(8,128)(2,1)} %collective-permute-done.8.refs_2_, ...), custom_call_target="tpu_custom_call" | custom-call | tf_op jit(solution)/shard_map/assemble/pallas_call | solution.py:765
  152.9 6.4 %convolution_convert_fusion.grad_ref = bf16[512,3072]{1,0:T(8,128)(2,1)} fusion(bf16[512,768]{1,0:T(8,128)(2,1)S(1)} %multiply_convert_fusion.down_grad_ref, bf16[3072,768]{1,0:T(8,128)(2,1)} %get-tuple-element.234.w_down_ref), kind=kOutput, calls=%fused_computation | convolution fusion | flops 2417491968 | bytes 8650752 | tf_op jit(solution)/shard_map/dot_general | solution.py:361
  159.3 9.7 %all-to-all-done.mixed_ref = bf16[8,192,256]{2,1,0:T(8,128)(2,1)S(1)} async-done(((bf16[8,192,256]{2,1,0:T(8,128)(2,1)}), bf16[8,192,256]{2,1,0:T(8,128)(2,1)S(1)}, u32[]{:S(2)}, u32[]{:S(2)}) %all-to-all-start) | async-done | bytes 786464 | tf_op jit(solution)/shard_map/all_to_all | solution.py:1384
  170.0 18.1 %middle.1 = (f32[512,768]{1,0:T(8,128)}, bf16[512,768]{1,0:T(8,128)(2,1)}, bf16[512,3072]{1,0:T(8,128)(2,1)}, bf16[512,3072]{1,0:T(8,128)(2,1)}, f32[512,768]{1,...) custom-call(s32[1]{0:T(128)} %bitcast.core_ref, ...), custom_call_target="tpu_custom_call" | custom-call | flops 6039797760 | bytes 17301504 | tf_op jit(solution)/shard_map/middle/pallas_call | solution.py:1026
  188.1 4.4 %all-to-all-start.1 = ((bf16[8,192,256]{2,1,0:T(8,128)(2,1)}), bf16[8,192,256]{2,1,0:T(8,128)(2,1)}, u32[]{:S(2)}, u32[]{:S(2)}) async-start(bf16[8,192,256]{2,1,0:T(8,128)(2,1)} %get-tuple-element.239), calls=%async_computation.1 | async-start | bytes 1572864 | tf_op jit(solution)/shard_map/all_to_all | solution.py:1402
  193.6 6.5 %down_part.1 = bf16[3072,768]{1,0:T(8,128)(2,1)} custom-call(bf16[512,3072]{1,0:T(8,128)(2,1)} %get-tuple-element.252.active_ref, bf16[512,768]{1,0:T(8,128)(2,1)} %copy-done.2), custom_call_target="tpu_custom_call" | custom-call | tf_op jit(solution)/shard_map/down_part/pallas_call | solution.py:1071
  200.2 1.7 copy-done.5
  201.9 9.1 %pair_sums.1 = bf16[4,96,3840]{2,1,0:T(8,128)(2,1)} custom-call(s32[1]{0:T(128)} %bitcast.core_ref, bf16[512,768]{1,0:T(8,128)(2,1)} %get-tuple-element.240.low_ref, bf16[512,3072]{1,0:T(8,128)(2,1)} %get-tuple-element.241.hidden_ref, bf16[8,192,256]{2,1,0:T(8,128)(2,1)} %copy-done.7, bf16[512,768]{1,0:T(8,128)(2,1)} %get-tuple-element.242.branch_ref, ...), custom_call_target="tpu_custom_call" | custom-call | tf_op jit(solution)/shard_map/pair_sums/pallas_call | solution.py:1184
  211.0 2.6 all-to-all-done.1.grad_ref
  214.2 1.7 dynamic-slice_bitcast_fusion
  215.9 2.5 collective-permute-start.20
  219.5 52.1 %retrace.1 = (bf16[576,4096]{1,0:T(8,128)(2,1)}, bf16[4096,768]{1,0:T(8,128)(2,1)}) custom-call(s32[1]{0:T(128)} %bitcast.core_ref, bf16[192,4096]{1,0:T(8,128)(2,1)} %get-tuple-element.223.qt_ref, bf16[8,192,256]{2,1,0:T(8,128)(2,1)} %all-to-all-done.1.grad_ref, f32[8,192,256]{2,1,0:T(8,128)} %get-tuple-element.245.full_ref, ...), custom_call_target="tpu_custom_call" | custom-call | flops 36238786560 | bytes 11010048 | tf_op jit(solution)/shard_map/retrace/pallas_call | solution.py:687
  273.8 1.7 fusion.12
  275.6 2.3 collective-permute-start.23
  279.6 10.3 %joint_part.1 = (bf16[4,96,576]{2,1,0:T(8,128)(2,1)}, bf16[4,96,576]{2,1,0:T(8,128)(2,1)}, f32[8,768]{1,0:T(8,128)}, f32[8,576]{1,0:T(8,128)}) custom-call(s32[1]{0:T(128)} %bitcast.core_ref, bf16[4096,768]{1,0:T(8,128)(2,1)} %get-tuple-element.258.plain_ref, bf16[576,4096]{1,0:T(8,128)(2,1)} %get-tuple-element.259.joint_ref, bf16[576,768]{1,0:T(8,128)(2,1)} %bitcast.179, ...), custom_call_target="tpu_custom_call" | custom-call | tf_op jit(solution)/shard_map/joint_part/pallas_call | solution.py:1250
  290.0 9.4 %result_part.1 = (f32[512,768]{1,0:T(8,128)}, f32[8,768]{1,0:T(8,128)}) custom-call(f32[5]{0:T(128)} %weights_ref.5, bf16[512,3072]{1,0:T(8,128)(2,1)} %get-tuple-element.252.active_ref, bf16[3072,768]{1,0:T(8,128)(2,1)} %get-tuple-element.234.w_down_ref, f32[1,768]{1,0:T(1,128)} %reshape.467.b_down_ref, f32[512,768]{1,0:T(8,128)} %get-tuple-element.253.middle_ref, ...), custom_call_target="tpu_custom_call" | custom-call | tf_op jit(solution)/shard_map/result_part/pallas_call | solution.py:1110
  299.4 2.1 collective-permute-done.22
  311.0 1.6 collective-permute-start.27
  312.7 1.5 collective-permute-start.26
  315.0 5.3 %collective-permute-done.27 = bf16[4,24,1472]{2,1,0:T(8,128)(2,1)S(1)} collective-permute-done((bf16[4,24,1472]{2,1,0:T(8,128)(2,1)S(1)}, bf16[4,24,1472]{2,1,0:T(8,128)(2,1)S(1)}, u32[]{:S(2)}, u32[]{:S(2)}) %collective-permute-start.27) | collective-permute-done | bytes 282656 | tf_op jit(solution)/shard_map/ppermute | solution.py:797
  320.4 2.3 collective-permute-done.26
  322.6 5.4 %collective-permute-done.28 = bf16[4,24,1472]{2,1,0:T(8,128)(2,1)S(1)} collective-permute-done((bf16[4,24,1472]{2,1,0:T(8,128)(2,1)S(1)}, bf16[4,24,1472]{2,1,0:T(8,128)(2,1)S(1)}, u32[]{:S(2)}, u32[]{:S(2)}) %collective-permute-start.28) | collective-permute-done | bytes 282656 | tf_op jit(solution)/shard_map/ppermute | solution.py:797
  330.9 2.3 collective-permute-start.40
  334.4 4.8 %collective-permute-start.30 = (bf16[24,704]{1,0:T(8,128)(2,1)S(1)}, bf16[24,704]{1,0:T(8,128)(2,1)S(1)}, u32[]{:S(2)}, u32[]{:S(2)}) collective-permute-start(bf16[24,704]{1,0:T(8,128)(2,1)S(1)} %get-tuple-element.375), channel_id=1, source_target_pairs={{0,4},{1,5},{2,6},{3,7},{4,0},{5,1},{6,2},{7,3},{8,12},{9,13},{10,... | collective-permute-start | bytes 101384 | tf_op jit(solution)/shard_map/ppermute | solution.py:793
  339.2 2.0 collective-permute-start.29
  341.3 1.9 collective-permute-done.30
  343.1 2.4 collective-permute-start.37
  346.2 2.4 collective-permute-start.34
  351.5 2.2 collective-permute-done.34.refs_7_
  353.8 1.8 collective-permute-start.32
  355.6 2.8 collective-permute-done.33.refs_6_
  359.4 3.9 %unpack.1 = (f32[96,3072]{1,0:T(8,128)}, f32[96,768]{1,0:T(8,128)}, f32[96,2304]{1,0:T(8,128)}, f32[384,768]{1,0:T(8,128)}, f32[1,192]{1,0:T(1,128)}, /*index=5*...) custom-call(s32[1]{0:T(128)} %bitcast.27.rep_ref, ...), custom_call_target="tpu_custom_call" | custom-call | tf_op jit(solution)/shard_map/unpack/pallas_call | solution.py:895
  365.4 1.8 fusion.9
  367.3 1.7 fusion.7
  (302 shorter events, 59.3 us)
Async XLA Ops:
  7.2 75.5 %all-gather.3.cloned.1.call-start = ((), (), s32[]{:S(2)}) async-start(), calls=%async_computation.4 | async-start | bytes 7077888 | tf_op jit(solution)/shard_map/all_gather | solution.py:1322
  7.9 161.1 %all-gather.5.cloned.1.call-start = ((), (), s32[]{:S(2)}) async-start(), calls=%async_computation.5 | async-start | bytes 5308416 | tf_op jit(solution)/shard_map/all_gather | solution.py:1380
  11.9 9.9 %collective-permute-start = (bf16[104,576]{0,1:T(8,128)(2,1)S(1)}, bf16[104,576]{0,1:T(8,128)(2,1)S(1)}, u32[]{:S(2)}, u32[]{:S(2)}) collective-permute-start(bf16[104,576]{0,1:T(8,128)(2,1)S(1)} %get-tuple-element.350), channel_id=1, source_target_pairs={{0,2},{1,3},{2,4},{3,5},{4,6},{5,7},{6,0},{7,1},{8,10},{9,11},{10,... | collective-permute-start | bytes 359432 | tf_op jit(solution)/shard_map/ppermute | solution.py:793
  15.0 19.1 %collective-permute-start.1 = (bf16[104,576]{0,1:T(8,128)(2,1)S(1)}, bf16[104,576]{0,1:T(8,128)(2,1)S(1)}, u32[]{:S(2)}, u32[]{:S(2)}) collective-permute-start(bf16[104,576]{0,1:T(8,128)(2,1)S(1)} %get-tuple-element.351), channel_id=1, source_target_pairs={{0,4},{1,5},{2,6},{3,7},{4,0},{5,1},{6,2},{7,3},{8,12},{9,13},{10,... | collective-permute-start | bytes 359432 | tf_op jit(solution)/shard_map/ppermute | solution.py:793
  17.6 16.5 %collective-permute-start.2 = (bf16[104,576]{0,1:T(8,128)(2,1)S(1)}, bf16[104,576]{0,1:T(8,128)(2,1)S(1)}, u32[]{:S(2)}, u32[]{:S(2)}) collective-permute-start(bf16[104,576]{0,1:T(8,128)(2,1)S(1)} %get-tuple-element.352), channel_id=1, source_target_pairs={{0,6},{1,7},{2,0},{3,1},{4,2},{5,3},{6,4},{7,5},{8,14},{9,15},{10,... | collective-permute-start | bytes 359432 | tf_op jit(solution)/shard_map/ppermute | solution.py:793
  35.3 14.3 %collective-permute-start.3 = (bf16[4,104,576]{2,1,0:T(8,128)(2,1)}, bf16[4,104,576]{2,1,0:T(8,128)(2,1)}, u32[]{:S(2)}, u32[]{:S(2)}) collective-permute-start(bf16[4,104,576]{2,1,0:T(8,128)(2,1)} %copy.94), channel_id=1, source_target_pairs={{0,1},{1,0},{2,3},{3,2},{4,5},{5,4},{6,7},{7,6},{8,9},{9,8},{10,11... | collective-permute-start | bytes 1437704 | tf_op jit(solution)/shard_map/ppermute | solution.py:787
  49.6 103.3 %copy-start.2 = (bf16[512,768]{1,0:T(8,128)(2,1)}, bf16[512,768]{1,0:T(8,128)(2,1)S(1)}, u32[]{:S(2)}) copy-start(bf16[512,768]{1,0:T(8,128)(2,1)S(1)} %multiply_convert_fusion.down_grad_ref) | copy-start | bytes 2359300
  82.7 16.9 %collective-permute-start.6 = (bf16[128,768]{1,0:T(8,128)(2,1)S(1)}, bf16[128,768]{1,0:T(8,128)(2,1)S(1)}, u32[]{:S(2)}, u32[]{:S(2)}) collective-permute-start(bf16[128,768]{1,0:T(8,128)(2,1)S(1)} %fusion.17), channel_id=1, source_target_pairs={{0,6},{1,7},{2,0},{3,1},{4,2},{5,3},{6,4},{7,5},{8,14},{9,15},{10,... | collective-permute-start | bytes 589832 | tf_op jit(solution)/shard_map/ppermute | solution.py:793
  84.5 16.1 %collective-permute-start.5 = (bf16[128,768]{1,0:T(8,128)(2,1)S(1)}, bf16[128,768]{1,0:T(8,128)(2,1)S(1)}, u32[]{:S(2)}, u32[]{:S(2)}) collective-permute-start(bf16[128,768]{1,0:T(8,128)(2,1)S(1)} %fusion.17), channel_id=1, source_target_pairs={{0,4},{1,5},{2,6},{3,7},{4,0},{5,1},{6,2},{7,3},{8,12},{9,13},{10,... | collective-permute-start | bytes 589832 | tf_op jit(solution)/shard_map/ppermute | solution.py:793
  84.5 16.1 %collective-permute-start.4 = (bf16[128,768]{1,0:T(8,128)(2,1)S(1)}, bf16[128,768]{1,0:T(8,128)(2,1)S(1)}, u32[]{:S(2)}, u32[]{:S(2)}) collective-permute-start(bf16[128,768]{1,0:T(8,128)(2,1)S(1)} %fusion.17), channel_id=1, source_target_pairs={{0,2},{1,3},{2,4},{3,5},{4,6},{5,7},{6,0},{7,1},{8,10},{9,11},{10,... | collective-permute-start | bytes 589832 | tf_op jit(solution)/shard_map/ppermute | solution.py:793
  100.8 34.3 %collective-permute-start.9 = (bf16[4,128,768]{2,1,0:T(8,128)(2,1)S(1)}, bf16[4,128,768]{2,1,0:T(8,128)(2,1)}, u32[]{:S(2)}, u32[]{:S(2)}) collective-permute-start(bf16[4,128,768]{2,1,0:T(8,128)(2,1)S(1)} %pad_maximum_fusion.refs_0_), channel_id=1, source_target_pairs={{0,24},{8,16},{16,8},{24,0},{1,25},{9,17},{17,9},{25,1},{2,26},{10... | collective-permute-start | bytes 2359304 | tf_op jit(solution)/shard_map/ppermute | solution.py:797
  103.4 34.0 %collective-permute-start.8 = (bf16[4,128,768]{2,1,0:T(8,128)(2,1)S(1)}, bf16[4,128,768]{2,1,0:T(8,128)(2,1)}, u32[]{:S(2)}, u32[]{:S(2)}) collective-permute-start(bf16[4,128,768]{2,1,0:T(8,128)(2,1)S(1)} %pad_maximum_fusion.refs_0_), channel_id=1, source_target_pairs={{0,16},{8,24},{16,0},{24,8},{1,17},{9,25},{17,1},{25,9},{2,18},{10... | collective-permute-start | bytes 2359304 | tf_op jit(solution)/shard_map/ppermute | solution.py:797
  103.8 33.6 %collective-permute-start.7 = (bf16[4,128,768]{2,1,0:T(8,128)(2,1)S(1)}, bf16[4,128,768]{2,1,0:T(8,128)(2,1)}, u32[]{:S(2)}, u32[]{:S(2)}) collective-permute-start(bf16[4,128,768]{2,1,0:T(8,128)(2,1)S(1)} %pad_maximum_fusion.refs_0_), channel_id=1, source_target_pairs={{0,8},{8,0},{16,24},{24,16},{1,9},{9,1},{17,25},{25,17},{2,10},{10... | collective-permute-start | bytes 2359304 | tf_op jit(solution)/shard_map/ppermute | solution.py:797
  130.3 38.8 %all-to-all-start = ((bf16[8,192,256]{2,1,0:T(8,128)(2,1)}), bf16[8,192,256]{2,1,0:T(8,128)(2,1)S(1)}, u32[]{:S(2)}, u32[]{:S(2)}) async-start(bf16[8,192,256]{2,1,0:T(8,128)(2,1)} %get-tuple-element.226), calls=%async_computation | async-start | bytes 1572864 | tf_op jit(solution)/shard_map/all_to_all | solution.py:1384
  137.4 4.4 %collective-permute-start.10 = (bf16[4,128,768]{2,1,0:T(8,128)(2,1)S(1)}, bf16[4,128,768]{2,1,0:T(8,128)(2,1)}, u32[]{:S(2)}, u32[]{:S(2)}) collective-permute-start(bf16[4,128,768]{2,1,0:T(8,128)(2,1)S(1)} %pad_maximum_fusion.refs_0_), channel_id=1, source_target_pairs={{0,1},{1,0},{2,3},{3,2},{4,5},{5,4},{6,7},{7,6},{8,9},{9,8},{10,11... | collective-permute-start | bytes 2359304 | tf_op jit(solution)/shard_map/ppermute | solution.py:787
  137.4 4.4 %collective-permute-start.11 = (bf16[4,128,768]{2,1,0:T(8,128)(2,1)}, bf16[4,128,768]{2,1,0:T(8,128)(2,1)}, u32[]{:S(2)}, u32[]{:S(2)}) collective-permute-start(bf16[4,128,768]{2,1,0:T(8,128)(2,1)} %collective-permute-done.7.refs_1_), channel_id=1, source_target_pairs={{0,1},{1,0},{2,3},{3,2},{4,5},{5,4},{6,7},{7,6},{8,9},{9,8},{10,11... | collective-permute-start | bytes 2359304 | tf_op jit(solution)/shard_map/ppermute | solution.py:787
  138.0 4.6 %collective-permute-start.12 = (bf16[4,128,768]{2,1,0:T(8,128)(2,1)}, bf16[4,128,768]{2,1,0:T(8,128)(2,1)}, u32[]{:S(2)}, u32[]{:S(2)}) collective-permute-start(bf16[4,128,768]{2,1,0:T(8,128)(2,1)} %collective-permute-done.8.refs_2_), channel_id=1, source_target_pairs={{0,1},{1,0},{2,3},{3,2},{4,5},{5,4},{6,7},{7,6},{8,9},{9,8},{10,11... | collective-permute-start | bytes 2359304 | tf_op jit(solution)/shard_map/ppermute | solution.py:787
  138.0 5.7 %collective-permute-start.13 = (bf16[4,128,768]{2,1,0:T(8,128)(2,1)}, bf16[4,128,768]{2,1,0:T(8,128)(2,1)}, u32[]{:S(2)}, u32[]{:S(2)}) collective-permute-start(bf16[4,128,768]{2,1,0:T(8,128)(2,1)} %collective-permute-done.9.refs_3_), channel_id=1, source_target_pairs={{0,1},{1,0},{2,3},{3,2},{4,5},{5,4},{6,7},{7,6},{8,9},{9,8},{10,11... | collective-permute-start | bytes 2359304 | tf_op jit(solution)/shard_map/ppermute | solution.py:787
  188.0 12.1 %collective-permute-start.15 = (bf16[512,3072]{1,0:T(8,128)(2,1)}, bf16[512,3072]{1,0:T(8,128)(2,1)S(1)}, u32[]{:S(2)}, u32[]{:S(2)}) collective-permute-start(bf16[512,3072]{1,0:T(8,128)(2,1)} %get-tuple-element.241.hidden_ref), channel_id=1, source_target_pairs={{0,1},{1,0},{2,3},{3,2},{4,5},{5,4},{6,7},{7,6},{8,9},{9,8},{10,11... | collective-permute-start | bytes 9437192 | tf_op jit(solution)/shard_map/ppermute | solution.py:787
  188.1 25.4 %all-to-all-start.1 = ((bf16[8,192,256]{2,1,0:T(8,128)(2,1)}), bf16[8,192,256]{2,1,0:T(8,128)(2,1)}, u32[]{:S(2)}, u32[]{:S(2)}) async-start(bf16[8,192,256]{2,1,0:T(8,128)(2,1)} %get-tuple-element.239), calls=%async_computation.1 | async-start | bytes 1572864 | tf_op jit(solution)/shard_map/all_to_all | solution.py:1402
  192.6 117.2 %reduce-scatter.5.cloned.1.call-start = ((), (), s32[]{:S(2)}) async-start(), calls=%async_computation.7 | async-start | bytes 5308416 | tf_op jit(solution)/shard_map/reduce_scatter | solution.py:1410
  192.6 7.6 %collective-permute-start.16 = (bf16[8,192,256]{2,1,0:T(8,128)(2,1)}, bf16[8,192,256]{2,1,0:T(8,128)(2,1)}, u32[]{:S(2)}, u32[]{:S(2)}) collective-permute-start(bf16[8,192,256]{2,1,0:T(8,128)(2,1)} %copy-done.7), channel_id=1, source_target_pairs={{0,1},{1,0},{2,3},{3,2},{4,5},{5,4},{6,7},{7,6},{8,9},{9,8},{10,11... | collective-permute-start | bytes 2359304 | tf_op jit(solution)/shard_map/ppermute | solution.py:787
  193.1 7.1 %collective-permute-start.14 = (bf16[512,768]{1,0:T(8,128)(2,1)}, bf16[512,768]{1,0:T(8,128)(2,1)}, u32[]{:S(2)}, u32[]{:S(2)}) collective-permute-start(bf16[512,768]{1,0:T(8,128)(2,1)} %get-tuple-element.240.low_ref), channel_id=1, source_target_pairs={{0,1},{1,0},{2,3},{3,2},{4,5},{5,4},{6,7},{7,6},{8,9},{9,8},{10,11... | collective-permute-start | bytes 2359304 | tf_op jit(solution)/shard_map/ppermute | solution.py:787
  193.2 7.0 %collective-permute-start.17 = (bf16[512,768]{1,0:T(8,128)(2,1)}, bf16[512,768]{1,0:T(8,128)(2,1)}, u32[]{:S(2)}, u32[]{:S(2)}) collective-permute-start(bf16[512,768]{1,0:T(8,128)(2,1)} %get-tuple-element.242.branch_ref), channel_id=1, source_target_pairs={{0,1},{1,0},{2,3},{3,2},{4,5},{5,4},{6,7},{7,6},{8,9},{9,8},{10,11... | collective-permute-start | bytes 2359304 | tf_op jit(solution)/shard_map/ppermute | solution.py:787
  213.6 151.9 %reduce-scatter.3.cloned.1.call-start = ((), (), s32[]{:S(2)}) async-start(), calls=%async_computation.6 | async-start | bytes 7077888 | tf_op jit(solution)/shard_map/reduce_scatter | solution.py:1417
  215.9 55.6 %collective-permute-start.20 = (bf16[4,24,3840]{2,1,0:T(8,128)(2,1)S(1)}, bf16[4,24,3840]{2,1,0:T(8,128)(2,1)S(1)}, u32[]{:S(2)}, u32[]{:S(2)}) collective-permute-start(bf16[4,24,3840]{2,1,0:T(8,128)(2,1)S(1)} %get-tuple-element.338), channel_id=1, source_target_pairs={{0,24},{8,16},{16,8},{24,0},{1,25},{9,17},{17,9},{25,1},{2,26},{10... | collective-permute-start | bytes 2211848 | tf_op jit(solution)/shard_map/ppermute | solution.py:797
  218.3 53.2 %collective-permute-start.19 = (bf16[4,24,3840]{2,1,0:T(8,128)(2,1)S(1)}, bf16[4,24,3840]{2,1,0:T(8,128)(2,1)S(1)}, u32[]{:S(2)}, u32[]{:S(2)}) collective-permute-start(bf16[4,24,3840]{2,1,0:T(8,128)(2,1)S(1)} %get-tuple-element.339), channel_id=1, source_target_pairs={{0,16},{8,24},{16,0},{24,8},{1,17},{9,25},{17,1},{25,9},{2,18},{10... | collective-permute-start | bytes 2211848 | tf_op jit(solution)/shard_map/ppermute | solution.py:797
  218.9 52.7 %collective-permute-start.18 = (bf16[4,24,3840]{2,1,0:T(8,128)(2,1)S(1)}, bf16[4,24,3840]{2,1,0:T(8,128)(2,1)S(1)}, u32[]{:S(2)}, u32[]{:S(2)}) collective-permute-start(bf16[4,24,3840]{2,1,0:T(8,128)(2,1)S(1)} %get-tuple-element.340), channel_id=1, source_target_pairs={{0,8},{8,0},{16,24},{24,16},{1,9},{9,1},{17,25},{25,17},{2,10},{10... | collective-permute-start | bytes 2211848 | tf_op jit(solution)/shard_map/ppermute | solution.py:797
  275.6 23.8 %collective-permute-start.23 = (bf16[24,3840]{1,0:T(8,128)(2,1)S(1)}, bf16[24,3840]{1,0:T(8,128)(2,1)S(1)}, u32[]{:S(2)}, u32[]{:S(2)}) collective-permute-start(bf16[24,3840]{1,0:T(8,128)(2,1)S(1)} %get-tuple-element.353), channel_id=1, source_target_pairs={{0,6},{1,7},{2,0},{3,1},{4,2},{5,3},{6,4},{7,5},{8,14},{9,15},{10,... | collective-permute-start | bytes 552968 | tf_op jit(solution)/shard_map/ppermute | solution.py:793
  277.9 23.6 %collective-permute-start.22 = (bf16[24,3840]{1,0:T(8,128)(2,1)S(1)}, bf16[24,3840]{1,0:T(8,128)(2,1)S(1)}, u32[]{:S(2)}, u32[]{:S(2)}) collective-permute-start(bf16[24,3840]{1,0:T(8,128)(2,1)S(1)} %get-tuple-element.354), channel_id=1, source_target_pairs={{0,4},{1,5},{2,6},{3,7},{4,0},{5,1},{6,2},{7,3},{8,12},{9,13},{10,... | collective-permute-start | bytes 552968 | tf_op jit(solution)/shard_map/ppermute | solution.py:793
  277.9 23.6 %collective-permute-start.21 = (bf16[24,3840]{1,0:T(8,128)(2,1)S(1)}, bf16[24,3840]{1,0:T(8,128)(2,1)S(1)}, u32[]{:S(2)}, u32[]{:S(2)}) collective-permute-start(bf16[24,3840]{1,0:T(8,128)(2,1)S(1)} %get-tuple-element.355), channel_id=1, source_target_pairs={{0,2},{1,3},{2,4},{3,5},{4,6},{5,7},{6,0},{7,1},{8,10},{9,11},{10,... | collective-permute-start | bytes 552968 | tf_op jit(solution)/shard_map/ppermute | solution.py:793
  303.6 1.5 collective-permute-start.25
  304.2 2.2 collective-permute-start.24
  311.0 9.4 %collective-permute-start.27 = (bf16[4,24,1472]{2,1,0:T(8,128)(2,1)S(1)}, bf16[4,24,1472]{2,1,0:T(8,128)(2,1)S(1)}, u32[]{:S(2)}, u32[]{:S(2)}) collective-permute-start(bf16[4,24,1472]{2,1,0:T(8,128)(2,1)S(1)} %pad_maximum_fusion.4), channel_id=1, source_target_pairs={{0,16},{8,24},{16,0},{24,8},{1,17},{9,25},{17,1},{25,9},{2,18},{10... | collective-permute-start | bytes 847880 | tf_op jit(solution)/shard_map/ppermute | solution.py:797
  312.7 9.9 %collective-permute-start.26 = (bf16[4,24,1472]{2,1,0:T(8,128)(2,1)S(1)}, bf16[4,24,1472]{2,1,0:T(8,128)(2,1)S(1)}, u32[]{:S(2)}, u32[]{:S(2)}) collective-permute-start(bf16[4,24,1472]{2,1,0:T(8,128)(2,1)S(1)} %pad_maximum_fusion.3), channel_id=1, source_target_pairs={{0,8},{8,0},{16,24},{24,16},{1,9},{9,1},{17,25},{25,17},{2,10},{10... | collective-permute-start | bytes 847880 | tf_op jit(solution)/shard_map/ppermute | solution.py:797
  314.3 13.7 %collective-permute-start.28 = (bf16[4,24,1472]{2,1,0:T(8,128)(2,1)S(1)}, bf16[4,24,1472]{2,1,0:T(8,128)(2,1)S(1)}, u32[]{:S(2)}, u32[]{:S(2)}) collective-permute-start(bf16[4,24,1472]{2,1,0:T(8,128)(2,1)S(1)} %pad_maximum_fusion.5), channel_id=1, source_target_pairs={{0,24},{8,16},{16,8},{24,0},{1,25},{9,17},{17,9},{25,1},{2,26},{10... | collective-permute-start | bytes 847880 | tf_op jit(solution)/shard_map/ppermute | solution.py:797
  329.5 9.7 %collective-permute-start.31 = (bf16[24,704]{1,0:T(8,128)(2,1)S(1)}, bf16[24,704]{1,0:T(8,128)(2,1)S(1)}, u32[]{:S(2)}, u32[]{:S(2)}) collective-permute-start(bf16[24,704]{1,0:T(8,128)(2,1)S(1)} %get-tuple-element.374), channel_id=1, source_target_pairs={{0,6},{1,7},{2,0},{3,1},{4,2},{5,3},{6,4},{7,5},{8,14},{9,15},{10,... | collective-permute-start | bytes 101384 | tf_op jit(solution)/shard_map/ppermute | solution.py:793
  330.9 17.9 %collective-permute-start.40 = (bf16[24,3072]{1,0:T(8,128)(2,1)S(1)}, bf16[24,3072]{1,0:T(8,128)(2,1)S(1)}, u32[]{:S(2)}, u32[]{:S(2)}) collective-permute-start(bf16[24,3072]{1,0:T(8,128)(2,1)S(1)} %pad_maximum_fusion.6.refs_8_), channel_id=1, source_target_pairs={{0,24},{8,16},{16,8},{24,0},{1,25},{9,17},{17,9},{25,1},{2,26},{10... | collective-permute-start | bytes 442376 | tf_op jit(solution)/shard_map/ppermute | solution.py:797
  333.2 16.1 %collective-permute-start.39 = (bf16[24,3072]{1,0:T(8,128)(2,1)S(1)}, bf16[24,3072]{1,0:T(8,128)(2,1)S(1)}, u32[]{:S(2)}, u32[]{:S(2)}) collective-permute-start(bf16[24,3072]{1,0:T(8,128)(2,1)S(1)} %pad_maximum_fusion.6.refs_8_), channel_id=1, source_target_pairs={{0,16},{8,24},{16,0},{24,8},{1,17},{9,25},{17,1},{25,9},{2,18},{10... | collective-permute-start | bytes 442376 | tf_op jit(solution)/shard_map/ppermute | solution.py:797
  333.8 16.2 %collective-permute-start.38 = (bf16[24,3072]{1,0:T(8,128)(2,1)S(1)}, bf16[24,3072]{1,0:T(8,128)(2,1)S(1)}, u32[]{:S(2)}, u32[]{:S(2)}) collective-permute-start(bf16[24,3072]{1,0:T(8,128)(2,1)S(1)} %pad_maximum_fusion.6.refs_8_), channel_id=1, source_target_pairs={{0,8},{8,0},{16,24},{24,16},{1,9},{9,1},{17,25},{25,17},{2,10},{10... | collective-permute-start | bytes 442376 | tf_op jit(solution)/shard_map/ppermute | solution.py:797
  334.4 8.7 %collective-permute-start.30 = (bf16[24,704]{1,0:T(8,128)(2,1)S(1)}, bf16[24,704]{1,0:T(8,128)(2,1)S(1)}, u32[]{:S(2)}, u32[]{:S(2)}) collective-permute-start(bf16[24,704]{1,0:T(8,128)(2,1)S(1)} %get-tuple-element.375), channel_id=1, source_target_pairs={{0,4},{1,5},{2,6},{3,7},{4,0},{5,1},{6,2},{7,3},{8,12},{9,13},{10,... | collective-permute-start | bytes 101384 | tf_op jit(solution)/shard_map/ppermute | solution.py:793
  339.2 6.7 %collective-permute-start.29 = (bf16[24,704]{1,0:T(8,128)(2,1)S(1)}, bf16[24,704]{1,0:T(8,128)(2,1)S(1)}, u32[]{:S(2)}, u32[]{:S(2)}) collective-permute-start(bf16[24,704]{1,0:T(8,128)(2,1)S(1)} %get-tuple-element.376), channel_id=1, source_target_pairs={{0,2},{1,3},{2,4},{3,5},{4,6},{5,7},{6,0},{7,1},{8,10},{9,11},{10,... | collective-permute-start | bytes 101384 | tf_op jit(solution)/shard_map/ppermute | solution.py:793
  343.1 15.5 %collective-permute-start.37 = (bf16[24,3840]{1,0:T(8,128)(2,1)S(1)}, bf16[24,3840]{1,0:T(8,128)(2,1)S(1)}, u32[]{:S(2)}, u32[]{:S(2)}) collective-permute-start(bf16[24,3840]{1,0:T(8,128)(2,1)S(1)} %add_convert_fusion.1.refs_0_), channel_id=1, source_target_pairs={{0,24},{8,16},{16,8},{24,0},{1,25},{9,17},{17,9},{25,1},{2,26},{10... | collective-permute-start | bytes 552968 | tf_op jit(solution)/shard_map/ppermute | solution.py:797
  346.2 7.5 %collective-permute-start.34 = (bf16[24,2432]{1,0:T(8,128)(2,1)S(1)}, bf16[24,2432]{1,0:T(8,128)(2,1)S(1)}, u32[]{:S(2)}, u32[]{:S(2)}) collective-permute-start(bf16[24,2432]{1,0:T(8,128)(2,1)S(1)} %concatenate.74.refs_4_), channel_id=1, source_target_pairs={{0,24},{8,16},{16,8},{24,0},{1,25},{9,17},{17,9},{25,1},{2,26},{10... | collective-permute-start | bytes 350216 | tf_op jit(solution)/shard_map/ppermute | solution.py:797
  348.8 9.8 %collective-permute-start.36 = (bf16[24,3840]{1,0:T(8,128)(2,1)S(1)}, bf16[24,3840]{1,0:T(8,128)(2,1)S(1)}, u32[]{:S(2)}, u32[]{:S(2)}) collective-permute-start(bf16[24,3840]{1,0:T(8,128)(2,1)S(1)} %add_convert_fusion.1.refs_0_), channel_id=1, source_target_pairs={{0,16},{8,24},{16,0},{24,8},{1,17},{9,25},{17,1},{25,9},{2,18},{10... | collective-permute-start | bytes 552968 | tf_op jit(solution)/shard_map/ppermute | solution.py:797
  349.4 9.2 %collective-permute-start.35 = (bf16[24,3840]{1,0:T(8,128)(2,1)S(1)}, bf16[24,3840]{1,0:T(8,128)(2,1)S(1)}, u32[]{:S(2)}, u32[]{:S(2)}) collective-permute-start(bf16[24,3840]{1,0:T(8,128)(2,1)S(1)} %add_convert_fusion.1.refs_0_), channel_id=1, source_target_pairs={{0,8},{8,0},{16,24},{24,16},{1,9},{9,1},{17,25},{25,17},{2,10},{10... | collective-permute-start | bytes 552968 | tf_op jit(solution)/shard_map/ppermute | solution.py:797
  350.0 8.4 %collective-permute-start.33 = (bf16[24,2432]{1,0:T(8,128)(2,1)S(1)}, bf16[24,2432]{1,0:T(8,128)(2,1)S(1)}, u32[]{:S(2)}, u32[]{:S(2)}) collective-permute-start(bf16[24,2432]{1,0:T(8,128)(2,1)S(1)} %concatenate.74.refs_4_), channel_id=1, source_target_pairs={{0,16},{8,24},{16,0},{24,8},{1,17},{9,25},{17,1},{25,9},{2,18},{10... | collective-permute-start | bytes 350216 | tf_op jit(solution)/shard_map/ppermute | solution.py:797
  353.8 4.8 %collective-permute-start.32 = (bf16[24,2432]{1,0:T(8,128)(2,1)S(1)}, bf16[24,2432]{1,0:T(8,128)(2,1)S(1)}, u32[]{:S(2)}, u32[]{:S(2)}) collective-permute-start(bf16[24,2432]{1,0:T(8,128)(2,1)S(1)} %concatenate.74.refs_4_), channel_id=1, source_target_pairs={{0,8},{8,0},{16,24},{24,16},{1,9},{9,1},{17,25},{25,17},{2,10},{10... | collective-permute-start | bytes 350216 | tf_op jit(solution)/shard_map/ppermute | solution.py:797
  (35 other events, 267.6 us)
Sparse Core Ops, SparseCore 0:
  9.7 73.0 all-gather.2
  100.9 67.9 all-gather.4
  213.7 53.7 reduce-scatter.4
  272.6 80.3 reduce-scatter.2

commit v5 on v4

--- a/solution.py
+++ b/solution.py
@@ -393,7 +393,7 @@
         start = 2 * width + base
         value = joint[start : start + HEAD_DIM]
         vt_ref[base : base + HEAD_DIM, :] = value.astype(BF16)
-        kv_ref[head] = jnp.transpose(jnp.concatenate([key, value], axis=0)).astype(BF16)
+        kv_ref[head] = jnp.transpose(jnp.concatenate([key, value], axis=0).astype(BF16))
 
 
 def project(tokens, weight_t, bias, gain, shift, cosine, sine, first, count, held):
@@ -1139,7 +1139,7 @@
     @pl.when(step == 0)
     def _():
         for side, ref in ((0, low_ref), (1, low_twin_ref)):
-            turned_ref[...] = jnp.transpose(ref[...].astype(F32)).astype(BF16)
+            turned_ref[...] = jnp.transpose(ref[...])
             for z in range(owners):
                 start = pl.multiple_of((2 * z + core) * part, part)
                 rows_ref[side, z * part : (z + 1) * part, :] = turned_ref[pl.ds(start, part), :]

time: 383 us -> 383 us (level)
  no operation moved by 1% of the time
where the time goes in v5:
time: 383 us; the launch traced here: 376 us
  Pallas kernels  166 us (43%)
  waiting for transfers between devices  79.2 us (21%)
  starting transfers between devices  56.7 us (15%)
  local copies, waits for them, and re-layouts  33.3 us (9%)
  other arithmetic  19.6 us (5%)
  between operations  15.4 us (4%)
  matrix products  6.41 us (2%)
    pallas_call x1, Pallas kernels, retrace(): pl.pallas_call(retrace_kernel, name='retrace', cost_estimate=cost(5 * 2 *...  52.1 us
    pallas_call x1, Pallas kernels, attend(): pl.pallas_call(attend_kernel, name='attend', cost_estimate=cost(2 * 2 * B...  25.9 us
    ppermute x18, starting transfers between devices, cross_rep(): lax.ppermute(value, 'rep', [(i, i ^ mask) for i in range(lax.axis_size('r...  23.5 us
    all_gather x1, waiting for transfers between devices, head_split_device(): tokens = lax.all_gather(block_in, 'shard', axis=0, tiled=True)  21.8 us
    ppermute x12, starting transfers between devices, shift_owner(): lax.ppermute(value, 'shard', [(i, (i + step) % groups) for i in range(gro...  21 us
    ppermute x18, waiting for transfers between devices, cross_rep(): lax.ppermute(value, 'rep', [(i, i ^ mask) for i in range(lax.axis_size('r...  20.6 us
    ppermute x12, waiting for transfers between devices, shift_owner(): lax.ppermute(value, 'shard', [(i, (i + step) % groups) for i in range(gro...  20.6 us
    pallas_call x1, Pallas kernels, middle_part(): pl.pallas_call(middle_kernel, name='middle', cost_estimate=cost(4 * rows...  18.1 us
  transfers between devices with their start and end apart: 47, of which 20 were waited for; matrix products, arithmetic and copies ran while one was open for 14% of the time, Pallas kernels for 39%

profile of v5, /device:TPU:0, one launch (start us, length us, event | category | flops | bytes accessed | tf_op | source)
XLA Modules:
  0.0 376.0 jit_solution(14722377187236217272)
XLA Ops:
  11.9 3.1 collective-permute-start
  15.0 2.6 collective-permute-start.1
  18.9 2.8 collective-permute-done
  21.8 12.3 %collective-permute-done.1 = bf16[104,576]{0,1:T(8,128)(2,1)S(1)} collective-permute-done((bf16[104,576]{0,1:T(8,128)(2,1)S(1)}, bf16[104,576]{0,1:T(8,128)(2,1)S(1)}, u32[]{:S(2)}, u32[]{:S(2)}) %collective-permute-start.1) | collective-permute-done | bytes 119840 | tf_op jit(solution)/shard_map/ppermute | solution.py:793
  35.3 2.8 multiply_sine_fusion
  41.1 7.5 %average.1 = (f32[4,512,768]{2,1,0:T(8,128)}, f32[512,768]{1,0:T(8,128)}, f32[4,8,768]{2,1,0:T(8,128)}) custom-call(f32[5]{0:T(128)} %weights_ref.5, bf16[4,512,768]{2,1,0:T(8,128)(2,1)} %earlier_ref.1, f32[512,768]{1,0:T(8,128)} %cotangent_ref.5), custom_call_target="tpu_custom_call" | custom-call | flops 9437184 | bytes 12582912 | tf_op jit(solution)/shard_map/average/pallas_call | solution.py:464
  49.6 1.6 copy.95
  60.9 21.8 %all-gather.3.cloned.1.call-done.x_ref = bf16[4096,768]{1,0:T(8,128)(2,1)} async-done(((bf16[512,768]{1,0:T(8,128)(2,1)}), bf16[4096,768]{1,0:T(8,128)(2,1)}) %all-gather.3.cloned.1.call-update) | async-done | bytes 6291472 | tf_op jit(solution)/shard_map/all_gather | solution.py:1322
  82.7 1.8 collective-permute-start.6
  86.1 13.5 %project.1 = (bf16[4096,768]{1,0:T(8,128)(2,1)}, bf16[192,4096]{1,0:T(8,128)(2,1)}, bf16[192,4096]{1,0:T(8,128)(2,1)}, bf16[192,4096]{1,0:T(8,128)(2,1)}, bf16[3,4096,128]{2,1,0:T(8,128)(2,1)}) custom-call(bf16[4096,768]{1,0:T(8,128)(2,1)} %all-gather.3.cloned.1.call-done.x_ref, bf16[576,768]{1,0:T(8,128)(2,1)} %bitcast.177, f32[576,1]{1,0:T(8,128)} %copy.105.bias_ref, ...), custom_call_target="tpu_custom_call" | custom-call | flops 3623878656 | bytes 37748736 | tf_op jit(solution)/shard_map/project/pallas_call | solution.py:410
  100.8 2.5 collective-permute-start.9
  104.4 25.9 %attend.1 = (bf16[8,192,256]{2,1,0:T(8,128)(2,1)}, f32[8,192,256]{2,1,0:T(8,128)}, f32[8,8,256]{2,1,0:T(8,128)}) custom-call(s32[1]{0:T(128)} %bitcast.core_ref, bf16[192,4096]{1,0:T(8,128)(2,1)} %get-tuple-element.223.qt_ref, bf16[3,4096,128]{2,1,0:T(8,128)(2,1)} %get-tuple-element.224.kv_ref, bf16[192,4096]{1,0:T(8,128)(2,1)} %get-tuple-element.225.vt_ref), custom_call_target="tpu_custom_call" | custom-call | flops 14495514624 | bytes 9437184 | tf_op jit(solution)/shard_map/attend/pallas_call | solution.py:563
  130.3 4.9 %all-to-all-start = ((bf16[8,192,256]{2,1,0:T(8,128)(2,1)}), bf16[8,192,256]{2,1,0:T(8,128)(2,1)S(1)}, u32[]{:S(2)}, u32[]{:S(2)}) async-start(bf16[8,192,256]{2,1,0:T(8,128)(2,1)} %get-tuple-element.226), calls=%async_computation | async-start | bytes 1572864 | tf_op jit(solution)/shard_map/all_to_all | solution.py:1384
  135.1 2.2 collective-permute-done.8.refs_2_
  143.7 9.2 %assemble.1 = (bf16[3072,768]{1,0:T(8,128)(2,1)}, bf16[768,768]{1,0:T(8,128)(2,1)}) custom-call(s32[2]{0:T(128)} %pad_add_fusion.place_ref, bf16[4,128,768]{2,1,0:T(8,128)(2,1)} %copy-done.4, bf16[4,128,768]{2,1,0:T(8,128)(2,1)} %collective-permute-done.7.refs_1_, bf16[4,128,768]{2,1,0:T(8,128)(2,1)} %collective-permute-done.8.refs_2_, ...), custom_call_target="tpu_custom_call" | custom-call | tf_op jit(solution)/shard_map/assemble/pallas_call | solution.py:765
  152.9 6.4 %convolution_convert_fusion.grad_ref = bf16[512,3072]{1,0:T(8,128)(2,1)} fusion(bf16[512,768]{1,0:T(8,128)(2,1)S(1)} %multiply_convert_fusion.down_grad_ref, bf16[3072,768]{1,0:T(8,128)(2,1)} %get-tuple-element.234.w_down_ref), kind=kOutput, calls=%fused_computation | convolution fusion | flops 2417491968 | bytes 8650752 | tf_op jit(solution)/shard_map/dot_general | solution.py:361
  159.3 9.8 %all-to-all-done.mixed_ref = bf16[8,192,256]{2,1,0:T(8,128)(2,1)S(1)} async-done(((bf16[8,192,256]{2,1,0:T(8,128)(2,1)}), bf16[8,192,256]{2,1,0:T(8,128)(2,1)S(1)}, u32[]{:S(2)}, u32[]{:S(2)}) %all-to-all-start) | async-done | bytes 786464 | tf_op jit(solution)/shard_map/all_to_all | solution.py:1384
  170.0 18.1 %middle.1 = (f32[512,768]{1,0:T(8,128)}, bf16[512,768]{1,0:T(8,128)(2,1)}, bf16[512,3072]{1,0:T(8,128)(2,1)}, bf16[512,3072]{1,0:T(8,128)(2,1)}, f32[512,768]{1,...) custom-call(s32[1]{0:T(128)} %bitcast.core_ref, ...), custom_call_target="tpu_custom_call" | custom-call | flops 6039797760 | bytes 17301504 | tf_op jit(solution)/shard_map/middle/pallas_call | solution.py:1026
  188.1 4.4 %all-to-all-start.1 = ((bf16[8,192,256]{2,1,0:T(8,128)(2,1)}), bf16[8,192,256]{2,1,0:T(8,128)(2,1)}, u32[]{:S(2)}, u32[]{:S(2)}) async-start(bf16[8,192,256]{2,1,0:T(8,128)(2,1)} %get-tuple-element.239), calls=%async_computation.1 | async-start | bytes 1572864 | tf_op jit(solution)/shard_map/all_to_all | solution.py:1402
  193.6 6.5 %down_part.1 = bf16[3072,768]{1,0:T(8,128)(2,1)} custom-call(bf16[512,3072]{1,0:T(8,128)(2,1)} %get-tuple-element.252.active_ref, bf16[512,768]{1,0:T(8,128)(2,1)} %copy-done.2), custom_call_target="tpu_custom_call" | custom-call | tf_op jit(solution)/shard_map/down_part/pallas_call | solution.py:1071
  200.2 1.7 copy-done.5
  201.9 9.1 %pair_sums.1 = bf16[4,96,3840]{2,1,0:T(8,128)(2,1)} custom-call(s32[1]{0:T(128)} %bitcast.core_ref, bf16[512,768]{1,0:T(8,128)(2,1)} %get-tuple-element.240.low_ref, bf16[512,3072]{1,0:T(8,128)(2,1)} %get-tuple-element.241.hidden_ref, bf16[8,192,256]{2,1,0:T(8,128)(2,1)} %copy-done.7, bf16[512,768]{1,0:T(8,128)(2,1)} %get-tuple-element.242.branch_ref, ...), custom_call_target="tpu_custom_call" | custom-call | tf_op jit(solution)/shard_map/pair_sums/pallas_call | solution.py:1184
  211.0 2.6 all-to-all-done.1.grad_ref
  214.2 1.7 dynamic-slice_bitcast_fusion
  215.9 2.4 collective-permute-start.20
  219.5 52.1 %retrace.1 = (bf16[576,4096]{1,0:T(8,128)(2,1)}, bf16[4096,768]{1,0:T(8,128)(2,1)}) custom-call(s32[1]{0:T(128)} %bitcast.core_ref, bf16[192,4096]{1,0:T(8,128)(2,1)} %get-tuple-element.223.qt_ref, bf16[8,192,256]{2,1,0:T(8,128)(2,1)} %all-to-all-done.1.grad_ref, f32[8,192,256]{2,1,0:T(8,128)} %get-tuple-element.245.full_ref, ...), custom_call_target="tpu_custom_call" | custom-call | flops 36238786560 | bytes 11010048 | tf_op jit(solution)/shard_map/retrace/pallas_call | solution.py:687
  273.8 1.7 fusion.12
  275.6 2.2 collective-permute-start.23
  279.6 10.3 %joint_part.1 = (bf16[4,96,576]{2,1,0:T(8,128)(2,1)}, bf16[4,96,576]{2,1,0:T(8,128)(2,1)}, f32[8,768]{1,0:T(8,128)}, f32[8,576]{1,0:T(8,128)}) custom-call(s32[1]{0:T(128)} %bitcast.core_ref, bf16[4096,768]{1,0:T(8,128)(2,1)} %get-tuple-element.258.plain_ref, bf16[576,4096]{1,0:T(8,128)(2,1)} %get-tuple-element.259.joint_ref, bf16[576,768]{1,0:T(8,128)(2,1)} %bitcast.179, ...), custom_call_target="tpu_custom_call" | custom-call | tf_op jit(solution)/shard_map/joint_part/pallas_call | solution.py:1250
  290.0 9.5 %result_part.1 = (f32[512,768]{1,0:T(8,128)}, f32[8,768]{1,0:T(8,128)}) custom-call(f32[5]{0:T(128)} %weights_ref.5, bf16[512,3072]{1,0:T(8,128)(2,1)} %get-tuple-element.252.active_ref, bf16[3072,768]{1,0:T(8,128)(2,1)} %get-tuple-element.234.w_down_ref, f32[1,768]{1,0:T(1,128)} %reshape.467.b_down_ref, f32[512,768]{1,0:T(8,128)} %get-tuple-element.253.middle_ref, ...), custom_call_target="tpu_custom_call" | custom-call | tf_op jit(solution)/shard_map/result_part/pallas_call | solution.py:1110
  299.4 2.0 collective-permute-done.22
  311.0 1.6 collective-permute-start.27
  312.7 1.5 collective-permute-start.26
  315.0 5.3 %collective-permute-done.27 = bf16[4,24,1472]{2,1,0:T(8,128)(2,1)S(1)} collective-permute-done((bf16[4,24,1472]{2,1,0:T(8,128)(2,1)S(1)}, bf16[4,24,1472]{2,1,0:T(8,128)(2,1)S(1)}, u32[]{:S(2)}, u32[]{:S(2)}) %collective-permute-start.27) | collective-permute-done | bytes 282656 | tf_op jit(solution)/shard_map/ppermute | solution.py:797
  320.3 2.3 collective-permute-done.26
  322.6 5.4 %collective-permute-done.28 = bf16[4,24,1472]{2,1,0:T(8,128)(2,1)S(1)} collective-permute-done((bf16[4,24,1472]{2,1,0:T(8,128)(2,1)S(1)}, bf16[4,24,1472]{2,1,0:T(8,128)(2,1)S(1)}, u32[]{:S(2)}, u32[]{:S(2)}) %collective-permute-start.28) | collective-permute-done | bytes 282656 | tf_op jit(solution)/shard_map/ppermute | solution.py:797
  330.9 2.3 collective-permute-start.40
  334.4 4.8 %collective-permute-start.30 = (bf16[24,704]{1,0:T(8,128)(2,1)S(1)}, bf16[24,704]{1,0:T(8,128)(2,1)S(1)}, u32[]{:S(2)}, u32[]{:S(2)}) collective-permute-start(bf16[24,704]{1,0:T(8,128)(2,1)S(1)} %get-tuple-element.375), channel_id=1, source_target_pairs={{0,4},{1,5},{2,6},{3,7},{4,0},{5,1},{6,2},{7,3},{8,12},{9,13},{10,... | collective-permute-start | bytes 101384 | tf_op jit(solution)/shard_map/ppermute | solution.py:793
  339.2 2.0 collective-permute-start.29
  341.2 1.9 collective-permute-done.30
  343.1 2.4 collective-permute-start.37
  346.2 2.4 collective-permute-start.34
  351.5 2.3 collective-permute-done.34.refs_7_
  353.7 1.8 collective-permute-start.32
  355.6 2.8 collective-permute-done.33.refs_6_
  359.4 3.9 %unpack.1 = (f32[96,3072]{1,0:T(8,128)}, f32[96,768]{1,0:T(8,128)}, f32[96,2304]{1,0:T(8,128)}, f32[384,768]{1,0:T(8,128)}, f32[1,192]{1,0:T(1,128)}, /*index=5*...) custom-call(s32[1]{0:T(128)} %bitcast.27.rep_ref, ...), custom_call_target="tpu_custom_call" | custom-call | tf_op jit(solution)/shard_map/unpack/pallas_call | solution.py:895
  365.4 1.8 fusion.9
  367.3 1.7 fusion.7
  (302 shorter events, 59.3 us)
Async XLA Ops:
  7.2 75.5 %all-gather.3.cloned.1.call-start = ((), (), s32[]{:S(2)}) async-start(), calls=%async_computation.4 | async-start | bytes 7077888 | tf_op jit(solution)/shard_map/all_gather | solution.py:1322
  7.9 161.1 %all-gather.5.cloned.1.call-start = ((), (), s32[]{:S(2)}) async-start(), calls=%async_computation.5 | async-start | bytes 5308416 | tf_op jit(solution)/shard_map/all_gather | solution.py:1380
  11.9 9.9 %collective-permute-start = (bf16[104,576]{0,1:T(8,128)(2,1)S(1)}, bf16[104,576]{0,1:T(8,128)(2,1)S(1)}, u32[]{:S(2)}, u32[]{:S(2)}) collective-permute-start(bf16[104,576]{0,1:T(8,128)(2,1)S(1)} %get-tuple-element.350), channel_id=1, source_target_pairs={{0,2},{1,3},{2,4},{3,5},{4,6},{5,7},{6,0},{7,1},{8,10},{9,11},{10,... | collective-permute-start | bytes 359432 | tf_op jit(solution)/shard_map/ppermute | solution.py:793
  15.0 19.1 %collective-permute-start.1 = (bf16[104,576]{0,1:T(8,128)(2,1)S(1)}, bf16[104,576]{0,1:T(8,128)(2,1)S(1)}, u32[]{:S(2)}, u32[]{:S(2)}) collective-permute-start(bf16[104,576]{0,1:T(8,128)(2,1)S(1)} %get-tuple-element.351), channel_id=1, source_target_pairs={{0,4},{1,5},{2,6},{3,7},{4,0},{5,1},{6,2},{7,3},{8,12},{9,13},{10,... | collective-permute-start | bytes 359432 | tf_op jit(solution)/shard_map/ppermute | solution.py:793
  17.6 16.5 %collective-permute-start.2 = (bf16[104,576]{0,1:T(8,128)(2,1)S(1)}, bf16[104,576]{0,1:T(8,128)(2,1)S(1)}, u32[]{:S(2)}, u32[]{:S(2)}) collective-permute-start(bf16[104,576]{0,1:T(8,128)(2,1)S(1)} %get-tuple-element.352), channel_id=1, source_target_pairs={{0,6},{1,7},{2,0},{3,1},{4,2},{5,3},{6,4},{7,5},{8,14},{9,15},{10,... | collective-permute-start | bytes 359432 | tf_op jit(solution)/shard_map/ppermute | solution.py:793
  35.3 14.3 %collective-permute-start.3 = (bf16[4,104,576]{2,1,0:T(8,128)(2,1)}, bf16[4,104,576]{2,1,0:T(8,128)(2,1)}, u32[]{:S(2)}, u32[]{:S(2)}) collective-permute-start(bf16[4,104,576]{2,1,0:T(8,128)(2,1)} %copy.94), channel_id=1, source_target_pairs={{0,1},{1,0},{2,3},{3,2},{4,5},{5,4},{6,7},{7,6},{8,9},{9,8},{10,11... | collective-permute-start | bytes 1437704 | tf_op jit(solution)/shard_map/ppermute | solution.py:787
  49.6 103.3 %copy-start.2 = (bf16[512,768]{1,0:T(8,128)(2,1)}, bf16[512,768]{1,0:T(8,128)(2,1)S(1)}, u32[]{:S(2)}) copy-start(bf16[512,768]{1,0:T(8,128)(2,1)S(1)} %multiply_convert_fusion.down_grad_ref) | copy-start | bytes 2359300
  82.7 16.9 %collective-permute-start.6 = (bf16[128,768]{1,0:T(8,128)(2,1)S(1)}, bf16[128,768]{1,0:T(8,128)(2,1)S(1)}, u32[]{:S(2)}, u32[]{:S(2)}) collective-permute-start(bf16[128,768]{1,0:T(8,128)(2,1)S(1)} %fusion.17), channel_id=1, source_target_pairs={{0,6},{1,7},{2,0},{3,1},{4,2},{5,3},{6,4},{7,5},{8,14},{9,15},{10,... | collective-permute-start | bytes 589832 | tf_op jit(solution)/shard_map/ppermute | solution.py:793
  84.5 16.1 %collective-permute-start.5 = (bf16[128,768]{1,0:T(8,128)(2,1)S(1)}, bf16[128,768]{1,0:T(8,128)(2,1)S(1)}, u32[]{:S(2)}, u32[]{:S(2)}) collective-permute-start(bf16[128,768]{1,0:T(8,128)(2,1)S(1)} %fusion.17), channel_id=1, source_target_pairs={{0,4},{1,5},{2,6},{3,7},{4,0},{5,1},{6,2},{7,3},{8,12},{9,13},{10,... | collective-permute-start | bytes 589832 | tf_op jit(solution)/shard_map/ppermute | solution.py:793
  84.5 16.1 %collective-permute-start.4 = (bf16[128,768]{1,0:T(8,128)(2,1)S(1)}, bf16[128,768]{1,0:T(8,128)(2,1)S(1)}, u32[]{:S(2)}, u32[]{:S(2)}) collective-permute-start(bf16[128,768]{1,0:T(8,128)(2,1)S(1)} %fusion.17), channel_id=1, source_target_pairs={{0,2},{1,3},{2,4},{3,5},{4,6},{5,7},{6,0},{7,1},{8,10},{9,11},{10,... | collective-permute-start | bytes 589832 | tf_op jit(solution)/shard_map/ppermute | solution.py:793
  100.8 34.3 %collective-permute-start.9 = (bf16[4,128,768]{2,1,0:T(8,128)(2,1)S(1)}, bf16[4,128,768]{2,1,0:T(8,128)(2,1)}, u32[]{:S(2)}, u32[]{:S(2)}) collective-permute-start(bf16[4,128,768]{2,1,0:T(8,128)(2,1)S(1)} %pad_maximum_fusion.refs_0_), channel_id=1, source_target_pairs={{0,24},{8,16},{16,8},{24,0},{1,25},{9,17},{17,9},{25,1},{2,26},{10... | collective-permute-start | bytes 2359304 | tf_op jit(solution)/shard_map/ppermute | solution.py:797
  103.4 34.0 %collective-permute-start.8 = (bf16[4,128,768]{2,1,0:T(8,128)(2,1)S(1)}, bf16[4,128,768]{2,1,0:T(8,128)(2,1)}, u32[]{:S(2)}, u32[]{:S(2)}) collective-permute-start(bf16[4,128,768]{2,1,0:T(8,128)(2,1)S(1)} %pad_maximum_fusion.refs_0_), channel_id=1, source_target_pairs={{0,16},{8,24},{16,0},{24,8},{1,17},{9,25},{17,1},{25,9},{2,18},{10... | collective-permute-start | bytes 2359304 | tf_op jit(solution)/shard_map/ppermute | solution.py:797
  103.8 33.6 %collective-permute-start.7 = (bf16[4,128,768]{2,1,0:T(8,128)(2,1)S(1)}, bf16[4,128,768]{2,1,0:T(8,128)(2,1)}, u32[]{:S(2)}, u32[]{:S(2)}) collective-permute-start(bf16[4,128,768]{2,1,0:T(8,128)(2,1)S(1)} %pad_maximum_fusion.refs_0_), channel_id=1, source_target_pairs={{0,8},{8,0},{16,24},{24,16},{1,9},{9,1},{17,25},{25,17},{2,10},{10... | collective-permute-start | bytes 2359304 | tf_op jit(solution)/shard_map/ppermute | solution.py:797
  130.3 38.8 %all-to-all-start = ((bf16[8,192,256]{2,1,0:T(8,128)(2,1)}), bf16[8,192,256]{2,1,0:T(8,128)(2,1)S(1)}, u32[]{:S(2)}, u32[]{:S(2)}) async-start(bf16[8,192,256]{2,1,0:T(8,128)(2,1)} %get-tuple-element.226), calls=%async_computation | async-start | bytes 1572864 | tf_op jit(solution)/shard_map/all_to_all | solution.py:1384
  137.4 4.4 %collective-permute-start.10 = (bf16[4,128,768]{2,1,0:T(8,128)(2,1)S(1)}, bf16[4,128,768]{2,1,0:T(8,128)(2,1)}, u32[]{:S(2)}, u32[]{:S(2)}) collective-permute-start(bf16[4,128,768]{2,1,0:T(8,128)(2,1)S(1)} %pad_maximum_fusion.refs_0_), channel_id=1, source_target_pairs={{0,1},{1,0},{2,3},{3,2},{4,5},{5,4},{6,7},{7,6},{8,9},{9,8},{10,11... | collective-permute-start | bytes 2359304 | tf_op jit(solution)/shard_map/ppermute | solution.py:787
  137.4 4.4 %collective-permute-start.11 = (bf16[4,128,768]{2,1,0:T(8,128)(2,1)}, bf16[4,128,768]{2,1,0:T(8,128)(2,1)}, u32[]{:S(2)}, u32[]{:S(2)}) collective-permute-start(bf16[4,128,768]{2,1,0:T(8,128)(2,1)} %collective-permute-done.7.refs_1_), channel_id=1, source_target_pairs={{0,1},{1,0},{2,3},{3,2},{4,5},{5,4},{6,7},{7,6},{8,9},{9,8},{10,11... | collective-permute-start | bytes 2359304 | tf_op jit(solution)/shard_map/ppermute | solution.py:787
  138.0 4.6 %collective-permute-start.12 = (bf16[4,128,768]{2,1,0:T(8,128)(2,1)}, bf16[4,128,768]{2,1,0:T(8,128)(2,1)}, u32[]{:S(2)}, u32[]{:S(2)}) collective-permute-start(bf16[4,128,768]{2,1,0:T(8,128)(2,1)} %collective-permute-done.8.refs_2_), channel_id=1, source_target_pairs={{0,1},{1,0},{2,3},{3,2},{4,5},{5,4},{6,7},{7,6},{8,9},{9,8},{10,11... | collective-permute-start | bytes 2359304 | tf_op jit(solution)/shard_map/ppermute | solution.py:787
  138.0 5.7 %collective-permute-start.13 = (bf16[4,128,768]{2,1,0:T(8,128)(2,1)}, bf16[4,128,768]{2,1,0:T(8,128)(2,1)}, u32[]{:S(2)}, u32[]{:S(2)}) collective-permute-start(bf16[4,128,768]{2,1,0:T(8,128)(2,1)} %collective-permute-done.9.refs_3_), channel_id=1, source_target_pairs={{0,1},{1,0},{2,3},{3,2},{4,5},{5,4},{6,7},{7,6},{8,9},{9,8},{10,11... | collective-permute-start | bytes 2359304 | tf_op jit(solution)/shard_map/ppermute | solution.py:787
  188.0 12.1 %collective-permute-start.15 = (bf16[512,3072]{1,0:T(8,128)(2,1)}, bf16[512,3072]{1,0:T(8,128)(2,1)S(1)}, u32[]{:S(2)}, u32[]{:S(2)}) collective-permute-start(bf16[512,3072]{1,0:T(8,128)(2,1)} %get-tuple-element.241.hidden_ref), channel_id=1, source_target_pairs={{0,1},{1,0},{2,3},{3,2},{4,5},{5,4},{6,7},{7,6},{8,9},{9,8},{10,11... | collective-permute-start | bytes 9437192 | tf_op jit(solution)/shard_map/ppermute | solution.py:787
  188.1 25.4 %all-to-all-start.1 = ((bf16[8,192,256]{2,1,0:T(8,128)(2,1)}), bf16[8,192,256]{2,1,0:T(8,128)(2,1)}, u32[]{:S(2)}, u32[]{:S(2)}) async-start(bf16[8,192,256]{2,1,0:T(8,128)(2,1)} %get-tuple-element.239), calls=%async_computation.1 | async-start | bytes 1572864 | tf_op jit(solution)/shard_map/all_to_all | solution.py:1402
  192.6 117.1 %reduce-scatter.5.cloned.1.call-start = ((), (), s32[]{:S(2)}) async-start(), calls=%async_computation.7 | async-start | bytes 5308416 | tf_op jit(solution)/shard_map/reduce_scatter | solution.py:1410
  192.6 7.5 %collective-permute-start.16 = (bf16[8,192,256]{2,1,0:T(8,128)(2,1)}, bf16[8,192,256]{2,1,0:T(8,128)(2,1)}, u32[]{:S(2)}, u32[]{:S(2)}) collective-permute-start(bf16[8,192,256]{2,1,0:T(8,128)(2,1)} %copy-done.7), channel_id=1, source_target_pairs={{0,1},{1,0},{2,3},{3,2},{4,5},{5,4},{6,7},{7,6},{8,9},{9,8},{10,11... | collective-permute-start | bytes 2359304 | tf_op jit(solution)/shard_map/ppermute | solution.py:787
  193.1 7.1 %collective-permute-start.14 = (bf16[512,768]{1,0:T(8,128)(2,1)}, bf16[512,768]{1,0:T(8,128)(2,1)}, u32[]{:S(2)}, u32[]{:S(2)}) collective-permute-start(bf16[512,768]{1,0:T(8,128)(2,1)} %get-tuple-element.240.low_ref), channel_id=1, source_target_pairs={{0,1},{1,0},{2,3},{3,2},{4,5},{5,4},{6,7},{7,6},{8,9},{9,8},{10,11... | collective-permute-start | bytes 2359304 | tf_op jit(solution)/shard_map/ppermute | solution.py:787
  193.2 7.0 %collective-permute-start.17 = (bf16[512,768]{1,0:T(8,128)(2,1)}, bf16[512,768]{1,0:T(8,128)(2,1)}, u32[]{:S(2)}, u32[]{:S(2)}) collective-permute-start(bf16[512,768]{1,0:T(8,128)(2,1)} %get-tuple-element.242.branch_ref), channel_id=1, source_target_pairs={{0,1},{1,0},{2,3},{3,2},{4,5},{5,4},{6,7},{7,6},{8,9},{9,8},{10,11... | collective-permute-start | bytes 2359304 | tf_op jit(solution)/shard_map/ppermute | solution.py:787
  213.6 151.9 %reduce-scatter.3.cloned.1.call-start = ((), (), s32[]{:S(2)}) async-start(), calls=%async_computation.6 | async-start | bytes 7077888 | tf_op jit(solution)/shard_map/reduce_scatter | solution.py:1417
  215.9 55.6 %collective-permute-start.20 = (bf16[4,24,3840]{2,1,0:T(8,128)(2,1)S(1)}, bf16[4,24,3840]{2,1,0:T(8,128)(2,1)S(1)}, u32[]{:S(2)}, u32[]{:S(2)}) collective-permute-start(bf16[4,24,3840]{2,1,0:T(8,128)(2,1)S(1)} %get-tuple-element.338), channel_id=1, source_target_pairs={{0,24},{8,16},{16,8},{24,0},{1,25},{9,17},{17,9},{25,1},{2,26},{10... | collective-permute-start | bytes 2211848 | tf_op jit(solution)/shard_map/ppermute | solution.py:797
  218.3 53.2 %collective-permute-start.19 = (bf16[4,24,3840]{2,1,0:T(8,128)(2,1)S(1)}, bf16[4,24,3840]{2,1,0:T(8,128)(2,1)S(1)}, u32[]{:S(2)}, u32[]{:S(2)}) collective-permute-start(bf16[4,24,3840]{2,1,0:T(8,128)(2,1)S(1)} %get-tuple-element.339), channel_id=1, source_target_pairs={{0,16},{8,24},{16,0},{24,8},{1,17},{9,25},{17,1},{25,9},{2,18},{10... | collective-permute-start | bytes 2211848 | tf_op jit(solution)/shard_map/ppermute | solution.py:797
  218.9 52.7 %collective-permute-start.18 = (bf16[4,24,3840]{2,1,0:T(8,128)(2,1)S(1)}, bf16[4,24,3840]{2,1,0:T(8,128)(2,1)S(1)}, u32[]{:S(2)}, u32[]{:S(2)}) collective-permute-start(bf16[4,24,3840]{2,1,0:T(8,128)(2,1)S(1)} %get-tuple-element.340), channel_id=1, source_target_pairs={{0,8},{8,0},{16,24},{24,16},{1,9},{9,1},{17,25},{25,17},{2,10},{10... | collective-permute-start | bytes 2211848 | tf_op jit(solution)/shard_map/ppermute | solution.py:797
  275.6 23.8 %collective-permute-start.23 = (bf16[24,3840]{1,0:T(8,128)(2,1)S(1)}, bf16[24,3840]{1,0:T(8,128)(2,1)S(1)}, u32[]{:S(2)}, u32[]{:S(2)}) collective-permute-start(bf16[24,3840]{1,0:T(8,128)(2,1)S(1)} %get-tuple-element.353), channel_id=1, source_target_pairs={{0,6},{1,7},{2,0},{3,1},{4,2},{5,3},{6,4},{7,5},{8,14},{9,15},{10,... | collective-permute-start | bytes 552968 | tf_op jit(solution)/shard_map/ppermute | solution.py:793
  277.8 23.6 %collective-permute-start.22 = (bf16[24,3840]{1,0:T(8,128)(2,1)S(1)}, bf16[24,3840]{1,0:T(8,128)(2,1)S(1)}, u32[]{:S(2)}, u32[]{:S(2)}) collective-permute-start(bf16[24,3840]{1,0:T(8,128)(2,1)S(1)} %get-tuple-element.354), channel_id=1, source_target_pairs={{0,4},{1,5},{2,6},{3,7},{4,0},{5,1},{6,2},{7,3},{8,12},{9,13},{10,... | collective-permute-start | bytes 552968 | tf_op jit(solution)/shard_map/ppermute | solution.py:793
  277.8 23.6 %collective-permute-start.21 = (bf16[24,3840]{1,0:T(8,128)(2,1)S(1)}, bf16[24,3840]{1,0:T(8,128)(2,1)S(1)}, u32[]{:S(2)}, u32[]{:S(2)}) collective-permute-start(bf16[24,3840]{1,0:T(8,128)(2,1)S(1)} %get-tuple-element.355), channel_id=1, source_target_pairs={{0,2},{1,3},{2,4},{3,5},{4,6},{5,7},{6,0},{7,1},{8,10},{9,11},{10,... | collective-permute-start | bytes 552968 | tf_op jit(solution)/shard_map/ppermute | solution.py:793
  303.5 1.5 collective-permute-start.25
  304.1 2.2 collective-permute-start.24
  311.0 9.4 %collective-permute-start.27 = (bf16[4,24,1472]{2,1,0:T(8,128)(2,1)S(1)}, bf16[4,24,1472]{2,1,0:T(8,128)(2,1)S(1)}, u32[]{:S(2)}, u32[]{:S(2)}) collective-permute-start(bf16[4,24,1472]{2,1,0:T(8,128)(2,1)S(1)} %pad_maximum_fusion.4), channel_id=1, source_target_pairs={{0,16},{8,24},{16,0},{24,8},{1,17},{9,25},{17,1},{25,9},{2,18},{10... | collective-permute-start | bytes 847880 | tf_op jit(solution)/shard_map/ppermute | solution.py:797
  312.7 9.9 %collective-permute-start.26 = (bf16[4,24,1472]{2,1,0:T(8,128)(2,1)S(1)}, bf16[4,24,1472]{2,1,0:T(8,128)(2,1)S(1)}, u32[]{:S(2)}, u32[]{:S(2)}) collective-permute-start(bf16[4,24,1472]{2,1,0:T(8,128)(2,1)S(1)} %pad_maximum_fusion.3), channel_id=1, source_target_pairs={{0,8},{8,0},{16,24},{24,16},{1,9},{9,1},{17,25},{25,17},{2,10},{10... | collective-permute-start | bytes 847880 | tf_op jit(solution)/shard_map/ppermute | solution.py:797
  314.3 13.7 %collective-permute-start.28 = (bf16[4,24,1472]{2,1,0:T(8,128)(2,1)S(1)}, bf16[4,24,1472]{2,1,0:T(8,128)(2,1)S(1)}, u32[]{:S(2)}, u32[]{:S(2)}) collective-permute-start(bf16[4,24,1472]{2,1,0:T(8,128)(2,1)S(1)} %pad_maximum_fusion.5), channel_id=1, source_target_pairs={{0,24},{8,16},{16,8},{24,0},{1,25},{9,17},{17,9},{25,1},{2,26},{10... | collective-permute-start | bytes 847880 | tf_op jit(solution)/shard_map/ppermute | solution.py:797
  329.5 9.7 %collective-permute-start.31 = (bf16[24,704]{1,0:T(8,128)(2,1)S(1)}, bf16[24,704]{1,0:T(8,128)(2,1)S(1)}, u32[]{:S(2)}, u32[]{:S(2)}) collective-permute-start(bf16[24,704]{1,0:T(8,128)(2,1)S(1)} %get-tuple-element.374), channel_id=1, source_target_pairs={{0,6},{1,7},{2,0},{3,1},{4,2},{5,3},{6,4},{7,5},{8,14},{9,15},{10,... | collective-permute-start | bytes 101384 | tf_op jit(solution)/shard_map/ppermute | solution.py:793
  330.9 17.9 %collective-permute-start.40 = (bf16[24,3072]{1,0:T(8,128)(2,1)S(1)}, bf16[24,3072]{1,0:T(8,128)(2,1)S(1)}, u32[]{:S(2)}, u32[]{:S(2)}) collective-permute-start(bf16[24,3072]{1,0:T(8,128)(2,1)S(1)} %pad_maximum_fusion.6.refs_8_), channel_id=1, source_target_pairs={{0,24},{8,16},{16,8},{24,0},{1,25},{9,17},{17,9},{25,1},{2,26},{10... | collective-permute-start | bytes 442376 | tf_op jit(solution)/shard_map/ppermute | solution.py:797
  333.2 16.1 %collective-permute-start.39 = (bf16[24,3072]{1,0:T(8,128)(2,1)S(1)}, bf16[24,3072]{1,0:T(8,128)(2,1)S(1)}, u32[]{:S(2)}, u32[]{:S(2)}) collective-permute-start(bf16[24,3072]{1,0:T(8,128)(2,1)S(1)} %pad_maximum_fusion.6.refs_8_), channel_id=1, source_target_pairs={{0,16},{8,24},{16,0},{24,8},{1,17},{9,25},{17,1},{25,9},{2,18},{10... | collective-permute-start | bytes 442376 | tf_op jit(solution)/shard_map/ppermute | solution.py:797
  333.8 16.3 %collective-permute-start.38 = (bf16[24,3072]{1,0:T(8,128)(2,1)S(1)}, bf16[24,3072]{1,0:T(8,128)(2,1)S(1)}, u32[]{:S(2)}, u32[]{:S(2)}) collective-permute-start(bf16[24,3072]{1,0:T(8,128)(2,1)S(1)} %pad_maximum_fusion.6.refs_8_), channel_id=1, source_target_pairs={{0,8},{8,0},{16,24},{24,16},{1,9},{9,1},{17,25},{25,17},{2,10},{10... | collective-permute-start | bytes 442376 | tf_op jit(solution)/shard_map/ppermute | solution.py:797
  334.4 8.7 %collective-permute-start.30 = (bf16[24,704]{1,0:T(8,128)(2,1)S(1)}, bf16[24,704]{1,0:T(8,128)(2,1)S(1)}, u32[]{:S(2)}, u32[]{:S(2)}) collective-permute-start(bf16[24,704]{1,0:T(8,128)(2,1)S(1)} %get-tuple-element.375), channel_id=1, source_target_pairs={{0,4},{1,5},{2,6},{3,7},{4,0},{5,1},{6,2},{7,3},{8,12},{9,13},{10,... | collective-permute-start | bytes 101384 | tf_op jit(solution)/shard_map/ppermute | solution.py:793
  339.2 6.7 %collective-permute-start.29 = (bf16[24,704]{1,0:T(8,128)(2,1)S(1)}, bf16[24,704]{1,0:T(8,128)(2,1)S(1)}, u32[]{:S(2)}, u32[]{:S(2)}) collective-permute-start(bf16[24,704]{1,0:T(8,128)(2,1)S(1)} %get-tuple-element.376), channel_id=1, source_target_pairs={{0,2},{1,3},{2,4},{3,5},{4,6},{5,7},{6,0},{7,1},{8,10},{9,11},{10,... | collective-permute-start | bytes 101384 | tf_op jit(solution)/shard_map/ppermute | solution.py:793
  343.1 15.5 %collective-permute-start.37 = (bf16[24,3840]{1,0:T(8,128)(2,1)S(1)}, bf16[24,3840]{1,0:T(8,128)(2,1)S(1)}, u32[]{:S(2)}, u32[]{:S(2)}) collective-permute-start(bf16[24,3840]{1,0:T(8,128)(2,1)S(1)} %add_convert_fusion.1.refs_0_), channel_id=1, source_target_pairs={{0,24},{8,16},{16,8},{24,0},{1,25},{9,17},{17,9},{25,1},{2,26},{10... | collective-permute-start | bytes 552968 | tf_op jit(solution)/shard_map/ppermute | solution.py:797
  346.2 7.5 %collective-permute-start.34 = (bf16[24,2432]{1,0:T(8,128)(2,1)S(1)}, bf16[24,2432]{1,0:T(8,128)(2,1)S(1)}, u32[]{:S(2)}, u32[]{:S(2)}) collective-permute-start(bf16[24,2432]{1,0:T(8,128)(2,1)S(1)} %concatenate.74.refs_4_), channel_id=1, source_target_pairs={{0,24},{8,16},{16,8},{24,0},{1,25},{9,17},{17,9},{25,1},{2,26},{10... | collective-permute-start | bytes 350216 | tf_op jit(solution)/shard_map/ppermute | solution.py:797
  348.8 9.8 %collective-permute-start.36 = (bf16[24,3840]{1,0:T(8,128)(2,1)S(1)}, bf16[24,3840]{1,0:T(8,128)(2,1)S(1)}, u32[]{:S(2)}, u32[]{:S(2)}) collective-permute-start(bf16[24,3840]{1,0:T(8,128)(2,1)S(1)} %add_convert_fusion.1.refs_0_), channel_id=1, source_target_pairs={{0,16},{8,24},{16,0},{24,8},{1,17},{9,25},{17,1},{25,9},{2,18},{10... | collective-permute-start | bytes 552968 | tf_op jit(solution)/shard_map/ppermute | solution.py:797
  349.3 9.2 %collective-permute-start.35 = (bf16[24,3840]{1,0:T(8,128)(2,1)S(1)}, bf16[24,3840]{1,0:T(8,128)(2,1)S(1)}, u32[]{:S(2)}, u32[]{:S(2)}) collective-permute-start(bf16[24,3840]{1,0:T(8,128)(2,1)S(1)} %add_convert_fusion.1.refs_0_), channel_id=1, source_target_pairs={{0,8},{8,0},{16,24},{24,16},{1,9},{9,1},{17,25},{25,17},{2,10},{10... | collective-permute-start | bytes 552968 | tf_op jit(solution)/shard_map/ppermute | solution.py:797
  350.0 8.4 %collective-permute-start.33 = (bf16[24,2432]{1,0:T(8,128)(2,1)S(1)}, bf16[24,2432]{1,0:T(8,128)(2,1)S(1)}, u32[]{:S(2)}, u32[]{:S(2)}) collective-permute-start(bf16[24,2432]{1,0:T(8,128)(2,1)S(1)} %concatenate.74.refs_4_), channel_id=1, source_target_pairs={{0,16},{8,24},{16,0},{24,8},{1,17},{9,25},{17,1},{25,9},{2,18},{10... | collective-permute-start | bytes 350216 | tf_op jit(solution)/shard_map/ppermute | solution.py:797
  353.7 4.8 %collective-permute-start.32 = (bf16[24,2432]{1,0:T(8,128)(2,1)S(1)}, bf16[24,2432]{1,0:T(8,128)(2,1)S(1)}, u32[]{:S(2)}, u32[]{:S(2)}) collective-permute-start(bf16[24,2432]{1,0:T(8,128)(2,1)S(1)} %concatenate.74.refs_4_), channel_id=1, source_target_pairs={{0,8},{8,0},{16,24},{24,16},{1,9},{9,1},{17,25},{25,17},{2,10},{10... | collective-permute-start | bytes 350216 | tf_op jit(solution)/shard_map/ppermute | solution.py:797
  (35 other events, 267.6 us)
Sparse Core Ops, SparseCore 0:
  9.7 73.0 all-gather.2
  100.9 67.9 all-gather.4
  213.7 53.7 reduce-scatter.4
  272.6 80.3 reduce-scatter.2
